TPU v7x, 32 devices: a whole 2x2x4 slice. The times are simulated.
32 devices in a mesh: shard: 4 (over z), ctx: 2 (over x), tp: 4 (over y, core).
Axes of the slice: x: 2, y: 2, z: 4, core: 2. Of those that a mesh axis runs over, the one named last changes fastest.
Arguments:
- activations: bfloat16 [4, 1040, 768], P('shard', 'ctx'), may hold values from -6 to 6
- slot_counts: int32 [4, 2], P('shard'), may hold values from 1 to 520, as said below
- qkv_weight: bfloat16 [3, 768, 768], P(None, 'shard', 'tp'), may hold values from -0.21875 to 0.21875
- proj_weight: bfloat16 [768, 768], P('tp', 'shard'), may hold values from -3 to 3
- up_weight: bfloat16 [768, 3072], P('shard', 'tp'), may hold values from -0.21875 to 0.21875
- down_weight: bfloat16 [3072, 768], P('tp', 'shard'), may hold values from -0.109375 to 0.109375
- norm_gains: bfloat16 [2, 768], P(None, 'shard'), may hold values from 0.5 to 1.5
- row_biases: bfloat16 [4, 768], P(None, 'shard'), may hold values from -3 to 3
- head_biases: bfloat16 [2, 768], P(None, 'tp'), may hold values from -0.59765625 to 0.59765625
- hidden_bias: bfloat16 [3072], P('tp'), may hold values from -3 to 3
- cotangent: bfloat16 [4, 1040, 768], P('shard', 'ctx'), may hold values from -6 to 6
Outputs:
- layer_out: bfloat16 [4, 1040, 768], P('shard', ('ctx', 'tp'))
- input_grad: bfloat16 [4, 1040, 768], P('shard', ('ctx', 'tp'))
- qkv_weight_grad: float32 [3, 768, 768], P(None, 'shard', 'tp')
- proj_weight_grad: float32 [768, 768], P('tp', 'shard')
- up_weight_grad: float32 [768, 3072], P('shard', 'tp')
- down_weight_grad: float32 [3072, 768], P('tp', 'shard')
- norm_gains_grad: float32 [2, 768], P(None, 'shard')
- row_biases_grad: float32 [4, 768], P(None, 'shard')
- head_biases_grad: float32 [2, 768], P(None, 'tp')
- hidden_bias_grad: float32 [3072], P('tp')
Inputs may be any that keep to these rules, and one draw needn't show every extreme that they name: Row b splits image b's 1025 tokens over the indices of ctx: slot_counts[b, r] of them lie in the first slots of index r's 520; each row sums to 1025; in each row one index holds exactly 520 and the others share the rest as evenly as possible.
All inputs are finite; a program needn't handle non-finite values.
Results may differ from a plain program's by a relative error of at most 0.012.
Values may be sent and summed in bfloat16 or wider, within the bound.
No kernel may reach another device: no remote copies, remote signals or barrier semaphores. Data moves between devices by JAX's collectives and lax.ppermute only.
A program may use at most 64 MiB of HBM per device.

v0:
```python
import math

import jax
import jax.numpy as jnp
from jax import lax
from jax.sharding import PartitionSpec as P

HD = 64


EPS = 1e-06
NEG = -1e30


def layer_norm(values, gain, shift):
    centred = values - jnp.mean(values, axis=-1, keepdims=True)
    spread = jnp.mean(centred * centred, axis=-1, keepdims=True)
    return centred * lax.rsqrt(spread + EPS) * gain + shift


def exact_gelu(hidden):
    return jax.nn.gelu(hidden, approximate=False)


def head_scores(queries, keys, keep):
    scale = 1.0 / math.sqrt(HD)
    scores = jnp.einsum("qhd,khd->hqk", queries, keys, preferred_element_type=jnp.float32) * scale
    return jnp.where(keep[None, None, :], scores, NEG)


def attend(item):
    queries, keys, values, keep = item
    slot_total = queries.shape[0]
    query_heads = queries.reshape(slot_total, -1, HD)
    key_heads = keys.reshape(keys.shape[0], -1, HD)
    value_heads = values.reshape(values.shape[0], -1, HD)
    scores = head_scores(query_heads, key_heads, keep)
    peak = jnp.max(scores, axis=-1, keepdims=True)
    log_total = peak + jnp.log(jnp.sum(jnp.exp(scores - peak), axis=-1, keepdims=True))
    attn_weights = jnp.exp(scores - log_total).astype(jnp.bfloat16)
    mixed = jnp.einsum(
        "hqk,khd->qhd", attn_weights, value_heads, preferred_element_type=jnp.float32
    )
    return (mixed.reshape(slot_total, -1).astype(jnp.bfloat16), log_total)


def attend_back(item):
    queries, keys, values, keep, log_total, grad_mixed = item
    scale = 1.0 / math.sqrt(HD)
    slot_total = queries.shape[0]
    key_total = keys.shape[0]
    query_heads = queries.reshape(slot_total, -1, HD)
    key_heads = keys.reshape(key_total, -1, HD)
    value_heads = values.reshape(key_total, -1, HD)
    grad_heads = grad_mixed.reshape(slot_total, -1, HD)
    scores = head_scores(query_heads, key_heads, keep)
    attn_weights = jnp.exp(scores - log_total)
    weights_low = attn_weights.astype(jnp.bfloat16)
    grad_weights = jnp.einsum(
        "qhd,khd->hqk", grad_heads, value_heads, preferred_element_type=jnp.float32
    )
    grad_values = jnp.einsum(
        "hqk,qhd->khd", weights_low, grad_heads, preferred_element_type=jnp.float32
    )
    inner = jnp.sum(grad_weights * attn_weights, axis=-1, keepdims=True)
    grad_scores = (attn_weights * (grad_weights - inner)).astype(jnp.bfloat16)
    grad_queries = (
        jnp.einsum("hqk,khd->qhd", grad_scores, key_heads, preferred_element_type=jnp.float32)
        * scale
    )
    grad_keys = (
        jnp.einsum("hqk,qhd->khd", grad_scores, query_heads, preferred_element_type=jnp.float32)
        * scale
    )
    return (
        grad_queries.reshape(slot_total, -1),
        grad_keys.reshape(key_total, -1),
        grad_values.reshape(key_total, -1),
    )


def per_device(
    activations,
    slot_counts,
    qkv_weight,
    proj_weight,
    up_weight,
    down_weight,
    norm_gains,
    row_biases,
    head_biases,
    hidden_bias,
    cotangent,
):
    images, slots, width = activations.shape
    n_ctx = lax.axis_size("ctx")
    n_tp = lax.axis_size("tp")
    row_count = images * slots
    quarter = row_count // n_tp
    row_start = lax.axis_index("tp") * quarter

    def own_rows(values):
        return lax.dynamic_slice_in_dim(values, row_start, quarter, 0)

    gathered = (
        lax.all_gather(qkv_weight, "shard", axis=1, tiled=True),
        lax.all_gather(proj_weight, "shard", axis=1, tiled=True),
        lax.all_gather(up_weight, "shard", axis=0, tiled=True),
        lax.all_gather(down_weight, "shard", axis=1, tiled=True),
        lax.all_gather(norm_gains, "shard", axis=1, tiled=True),
        lax.all_gather(row_biases, "shard", axis=1, tiled=True),
    )
    qkv_full, proj_full, up_full, down_full, gains_full, shifts_full = gathered
    gains = gains_full.astype(jnp.float32)
    shifts = shifts_full.astype(jnp.float32)
    ctx_rank = lax.axis_index("ctx")
    rank_ids = jnp.arange(n_ctx, dtype=jnp.int32)
    own_count = jnp.sum(jnp.where(rank_ids[None, :] == ctx_rank, slot_counts, 0), axis=1)
    slot_ids = jnp.arange(slots, dtype=jnp.int32)
    row_valid = (slot_ids[None, :] < own_count[:, None]).reshape(row_count, 1)
    share_valid = own_rows(row_valid)
    key_valid = jnp.repeat(slot_counts, slots, axis=1) > jnp.tile(slot_ids, n_ctx)[None, :]
    act_in = activations.reshape(row_count, width).astype(jnp.float32)
    normed, norm_one_back = jax.vjp(layer_norm, act_in, gains[0], shifts[0])
    normed_low = normed.astype(jnp.bfloat16)
    projected = jnp.einsum("rd,kde->kre", normed_low, qkv_full, preferred_element_type=jnp.float32)
    biases = head_biases.astype(jnp.float32)
    queries = (projected[0] + biases[0]).astype(jnp.bfloat16).reshape(images, slots, -1)
    keys = projected[1].astype(jnp.bfloat16).reshape(images, slots, -1)
    values = (projected[2] + biases[1]).astype(jnp.bfloat16).reshape(images, slots, -1)
    keys_all, values_all = (
        lax.all_gather(keys, "ctx", axis=1, tiled=True),
        lax.all_gather(values, "ctx", axis=1, tiled=True),
    )
    mixed, log_totals = lax.map(attend, (queries, keys_all, values_all, key_valid))
    mixed_flat = mixed.reshape(row_count, -1)
    attn_part = jnp.dot(mixed_flat, proj_full, preferred_element_type=jnp.float32)
    attn_sum = lax.psum(attn_part, "tp")
    middle_full = act_in + attn_sum + shifts[2]
    normed_two, norm_two_back = jax.vjp(layer_norm, middle_full, gains[1], shifts[1])
    normed_two_low = normed_two.astype(jnp.bfloat16)
    middle = own_rows(middle_full)
    hidden = jnp.dot(
        normed_two_low, up_full, preferred_element_type=jnp.float32
    ) + hidden_bias.astype(jnp.float32)
    gelu_out, gelu_back = jax.vjp(exact_gelu, hidden)
    gelu_low = gelu_out.astype(jnp.bfloat16)
    mlp_part = jnp.dot(gelu_low, down_full, preferred_element_type=jnp.float32)
    mlp_sum = own_rows(lax.psum(mlp_part.astype(jnp.bfloat16), "tp").astype(jnp.float32))
    layer_out = (
        jnp.where(share_valid, middle + mlp_sum + shifts[3], 0.0)
        .astype(jnp.bfloat16)
        .reshape(images, quarter, width)
    )
    qkv_use, proj_use, up_use, down_use = (qkv_full, proj_full, up_full, down_full)
    grad_out = jnp.where(row_valid, cotangent.reshape(row_count, width).astype(jnp.float32), 0.0)
    grad_branch = grad_out.astype(jnp.bfloat16)
    down_grad = jnp.einsum("rf,rd->fd", gelu_low, grad_branch, preferred_element_type=jnp.float32)
    grad_gelu = jnp.einsum("rd,fd->rf", grad_branch, down_use, preferred_element_type=jnp.float32)
    (grad_hidden,) = gelu_back(grad_gelu)
    grad_hidden_low = grad_hidden.astype(jnp.bfloat16)
    up_grad = jnp.einsum(
        "rd,rf->df", normed_two_low, grad_hidden_low, preferred_element_type=jnp.float32
    )
    hidden_grad = jnp.sum(grad_hidden_low.astype(jnp.float32), axis=0)
    grad_normed_part = jnp.einsum(
        "rf,df->rd", grad_hidden_low, up_use, preferred_element_type=jnp.float32
    )
    grad_normed_two = lax.psum(grad_normed_part, "tp")
    grad_middle_norm, gain_two_grad, shift_two_grad = norm_two_back(grad_normed_two)
    grad_middle_full = grad_out + grad_middle_norm
    grad_attn = grad_middle_full.astype(jnp.bfloat16)
    grad_middle = own_rows(grad_middle_full)
    proj_grad = jnp.einsum("re,rd->ed", mixed_flat, grad_attn, preferred_element_type=jnp.float32)
    grad_mixed = (
        jnp.einsum("rd,ed->re", grad_attn, proj_use, preferred_element_type=jnp.float32)
        .astype(jnp.bfloat16)
        .reshape(images, slots, -1)
    )
    grad_queries, grad_keys_part, grad_values_part = lax.map(
        attend_back, (queries, keys_all, values_all, key_valid, log_totals, grad_mixed)
    )
    grad_keys, grad_values = (
        lax.psum_scatter(grad_keys_part, "ctx", scatter_dimension=1, tiled=True),
        lax.psum_scatter(grad_values_part, "ctx", scatter_dimension=1, tiled=True),
    )
    stacked = jnp.stack(
        [
            grad_queries.reshape(row_count, -1),
            grad_keys.reshape(row_count, -1),
            grad_values.reshape(row_count, -1),
        ]
    ).astype(jnp.bfloat16)
    qkv_grad = jnp.einsum("rd,kre->kde", normed_low, stacked, preferred_element_type=jnp.float32)
    stacked_wide = stacked.astype(jnp.float32)
    head_grad = jnp.stack([jnp.sum(stacked_wide[0], axis=0), jnp.sum(stacked_wide[2], axis=0)])
    grad_normed_one_part = jnp.einsum(
        "kre,kde->rd", stacked, qkv_use, preferred_element_type=jnp.float32
    )
    grad_normed_one = lax.psum(grad_normed_one_part, "tp")
    grad_input_norm_full, gain_one_grad, shift_one_grad = norm_one_back(grad_normed_one)
    grad_input_norm = own_rows(grad_input_norm_full)
    gains_grad = jnp.stack([gain_one_grad, gain_two_grad])
    norm_shift_grads = jnp.stack([shift_one_grad, shift_two_grad])
    input_grad = (
        (grad_middle + grad_input_norm).astype(jnp.bfloat16).reshape(images, quarter, width)
    )
    shifts_grad = jnp.concatenate(
        [
            norm_shift_grads,
            jnp.stack(
                [
                    jnp.sum(grad_attn.astype(jnp.float32), axis=0),
                    jnp.sum(grad_branch.astype(jnp.float32), axis=0),
                ]
            ),
        ],
        axis=0,
    )
    summed = lax.psum((qkv_grad, proj_grad, up_grad, down_grad, gains_grad, shifts_grad), "ctx")
    owned = (
        lax.psum_scatter(summed[0], "shard", scatter_dimension=1, tiled=True),
        lax.psum_scatter(summed[1], "shard", scatter_dimension=1, tiled=True),
        lax.psum_scatter(summed[2], "shard", scatter_dimension=0, tiled=True),
        lax.psum_scatter(summed[3], "shard", scatter_dimension=1, tiled=True),
        lax.psum_scatter(summed[4], "shard", scatter_dimension=1, tiled=True),
        lax.psum_scatter(summed[5], "shard", scatter_dimension=1, tiled=True),
    )
    bias_totals = lax.psum((head_grad, hidden_grad), ("shard", "ctx"))
    return (
        layer_out,
        input_grad,
        owned[0],
        owned[1],
        owned[2],
        owned[3],
        owned[4],
        owned[5],
        bias_totals[0],
        bias_totals[1],
    )


def solution(mesh):
    placed = (
        P("shard", "ctx", None),
        P("shard", None),
        P(None, "shard", "tp"),
        P("tp", "shard"),
        P("shard", "tp"),
        P("tp", "shard"),
        P(None, "shard"),
        P(None, "shard"),
        P(None, "tp"),
        P("tp"),
        P("shard", "ctx", None),
    )
    return jax.shard_map(
        per_device,
        mesh=mesh,
        in_specs=placed,
        out_specs=(
            P("shard", ("ctx", "tp"), None),
            P("shard", ("ctx", "tp"), None),
            P(None, "shard", "tp"),
            P("tp", "shard"),
            P("shard", "tp"),
            P("tp", "shard"),
            P(None, "shard"),
            P(None, "shard"),
            P(None, "tp"),
            P("tp"),
        ),
        check_vma=False,
    )
```

profile of v0, /device:TPU:0, one launch (start us, length us, event | category | flops | bytes accessed | tf_op | source)
XLA Modules:
  0.0 542.7 jit_solution(16820646463041530862)
XLA Ops:
  10.4 12.8 %all-gather = bf16[4,192,2]{1,2,0:T(2,128)(2,1)S(1)} all-gather(bf16[1,192,2]{1,2,0:T(2,128)(2,1)} %bitcast.183), channel_id=1, replica_groups=mesh['shard'=4,'ctx'=2,'tp'=4] {'shard'}, dimensions={0}, use_global_device_ids=true | all-gather | bytes 3840 | tf_op jit(solution)/shard_map/all_gather | solution.py:110
  26.3 11.9 %all-gather.1 = bf16[4,192,4]{1,2,0:T(4,128)(2,1)S(1)} all-gather(bf16[1,192,4]{1,2,0:T(4,128)(2,1)S(1)} %bitcast.182), channel_id=1, replica_groups=mesh['shard'=4,'ctx'=2,'tp'=4] {'shard'}, dimensions={0}, use_global_device_ids=true | all-gather | bytes 7680 | tf_op jit(solution)/shard_map/all_gather | solution.py:111
  38.4 15.8 %all_gather.29 = bf16[192,768]{0,1:T(8,128)(2,1)} all-gather(bf16[192,192]{0,1:T(8,128)(2,1)S(1)} %copy.48), channel_id=1, replica_groups=mesh['shard'=4,'ctx'=2,'tp'=4] {'shard'}, dimensions={1}, use_global_device_ids=true | all-gather | bytes 368640 | tf_op jit(solution)/shard_map/all_gather | solution.py:107
  54.5 22.9 %all_gather.26 = bf16[3,768,192]{2,0,1:T(4,128)(2,1)S(1)} all-gather(bf16[3,192,192]{2,0,1:T(4,128)(2,1)S(1)} %copy.42), channel_id=1, replica_groups=mesh['shard'=4,'ctx'=2,'tp'=4] {'shard'}, dimensions={1}, use_global_device_ids=true | all-gather | bytes 1105920 | tf_op jit(solution)/shard_map/all_gather | solution.py:106
  81.4 11.9 %all_gather.28 = bf16[1,1040,192]{2,0,1:T(2,128)(2,1)S(1)} all-gather(bf16[1,520,192]{2,0,1:T(2,128)(2,1)S(1)} %copy.46), channel_id=1, replica_groups=mesh['shard'=4,'ctx'=2,'tp'=4] {'ctx'}, dimensions={1}, use_global_device_ids=true | all-gather | bytes 599040 | tf_op jit(solution)/shard_map/all_gather | solution.py:132
  97.7 9.9 %all_gather.27 = bf16[1,1040,192]{2,0,1:T(2,128)(2,1)S(1)} all-gather(bf16[1,520,192]{2,0,1:T(2,128)(2,1)S(1)} %copy.44), channel_id=1, replica_groups=mesh['shard'=4,'ctx'=2,'tp'=4] {'ctx'}, dimensions={1}, use_global_device_ids=true | all-gather | bytes 599040 | tf_op jit(solution)/shard_map/all_gather | solution.py:133
  120.6 39.9 %all-reduce.9.cloned.1.call-done = f32[520,768]{1,0:T(8,128)} async-done(((f32[520,768]{1,0:T(8,128)}), f32[520,768]{1,0:T(8,128)}) %all-reduce.9.cloned.1.call-update) | async-done | bytes 1597456 | tf_op jit(solution)/shard_map/psum | solution.py:138
  162.6 6.9 %multiply_convert_fusion.1 = (bf16[520,768]{1,0:T(8,128)(2,1)}, f32[520,768]{1,0:T(8,128)}, f32[520,768]{1,0:T(8,128)}) fusion(f32[768]{0:T(1024)S(1)} %convert_element_type.113, bf16[768,768]{1,0:T(8,128)(2,1)} %all-gather.5.cloned.1.call-done, f32[520,768]{1,0:T(8,128)S(1)} %get-tuple-element.132, f32[768]{0:T(1024)S(1)} %get-tuple-element.110, ...), kind=kOutput, calls=%fused_computation.36 | convolution fusion | flops 641771520 | bytes 6784064 | tf_op jit(solution)/shard_map/dot_general | solution.py:143
  169.6 10.6 %all-gather.7.cloned.1.call-done = bf16[768,768]{0,1:T(8,128)(2,1)} async-done(((bf16[768,192]{0,1:T(8,128)(2,1)}), bf16[768,768]{0,1:T(8,128)(2,1)}) %all-gather.7.cloned.1.call-update) | async-done | bytes 1179664 | tf_op jit(solution)/shard_map/all_gather | solution.py:109
  186.9 42.7 %all-reduce.13.cloned.1.call-done = f32[520,768]{1,0:T(8,128)} async-done(((f32[520,768]{1,0:T(8,128)}), f32[520,768]{1,0:T(8,128)}) %all-reduce.13.cloned.1.call-update) | async-done | bytes 1597456 | tf_op jit(solution)/shard_map/psum | solution.py:169
  238.8 4.8 multiply_reduce_fusion
  249.7 6.0 %multiply_convert_fusion = bf16[3,520,1040]{2,1,0:T(8,128)(2,1)S(1)} fusion(f32[3,520,1040]{2,1,0:T(8,128)} %get-tuple-element.140, f32[3,520,1040]{2,1,0:T(8,128)} %copy-done, f32[3,520]{1,0:T(4,128)S(1)} %get-tuple-element.139, f32[3,520]{1,0:T(4,128)S(1)} %log_add_fusion), kind=kLoop, calls=%fused_computation | loop fusion | flops 6489600 | bytes 16236480 | tf_op jit(solution)/shard_map/while/body/eval_jaxpr/convert_element_type | solution.py:66
  265.8 4.5 reduce-scatter.27.cloned.1.call-done
  272.6 20.4 %reduce-scatter.25.cloned.1.call-done = f32[520,192]{1,0:T(8,128)} async-done(((f32[1040,192]{1,0:T(8,128)}), f32[520,192]{1,0:T(8,128)}) %reduce-scatter.25.cloned.1.call-update) | async-done | bytes 399376
  305.5 4.2 copy.55
  309.7 4.7 reshape.243
  326.2 16.6 %all-reduce.15.cloned.1.call-done = f32[520,768]{1,0:T(8,128)} async-done(((f32[520,768]{1,0:T(8,128)}), f32[520,768]{1,0:T(8,128)}) %all-reduce.15.cloned.1.call-update) | async-done | bytes 1597456 | tf_op jit(solution)/shard_map/psum | solution.py:200
  348.8 20.7 %reduce-scatter.29.cloned.1.call-done = f32[192,576]{1,0:T(8,128)} async-done(((f32[768,576]{1,0:T(8,128)}), f32[192,576]{1,0:T(8,128)}) %reduce-scatter.29.cloned.1.call-update) | async-done | bytes 442384
  372.0 46.6 %reduce-scatter.21.cloned.1.call-done = f32[192,768]{1,0:T(8,128)} async-done(((f32[768,768]{1,0:T(8,128)}), f32[192,768]{1,0:T(8,128)}) %reduce-scatter.21.cloned.1.call-update) | async-done | bytes 589840 | tf_op jit(solution)/shard_map/reduce_scatter | solution.py:224
  418.6 49.6 %reduce-scatter.23.cloned.1.call-done = f32[768,192]{0,1:T(8,128)} async-done(((f32[768,768]{0,1:T(8,128)}), f32[768,192]{0,1:T(8,128)}) %reduce-scatter.23.cloned.1.call-update) | async-done | bytes 589840 | tf_op jit(solution)/shard_map/reduce_scatter | solution.py:225
  471.0 21.1 %all-reduce = (f32[2,192]{1,0:T(2,128)}, f32[768]{0:T(1024)}) all-reduce(f32[2,192]{1,0:T(2,128)S(1)} %pad_maximum_fusion.3, f32[768]{0:T(1024)S(1)} %get-tuple-element.141), channel_id=1, replica_groups=mesh['shard'=4,'ctx'=2,'tp'=4] {'shard','ctx'}, use_global_device_ids=true, to_apply=%region_38.39 | all-reduce | flops 1152 | bytes 9216 | tf_op jit(solution)/shard_map/psum | solution.py:229
  495.8 17.1 %reduce-scatter.35.cloned.1.call-done = f32[192,4]{1,0:T(8,128)} async-done(((f32[768,4]{1,0:T(8,128)}), f32[192,4]{1,0:T(8,128)}) %reduce-scatter.35.cloned.1.call-update) | async-done | bytes 3088
  513.8 5.7 %all-reduce.1 = (f32[2,192]{1,0:T(2,128)}, f32[4,192]{1,0:T(4,128)}) all-reduce(f32[2,192]{1,0:T(2,128)S(1)} %copy.60, f32[4,192]{1,0:T(4,128)S(1)} %copy.62), channel_id=1, replica_groups=mesh['shard'=4,'ctx'=2,'tp'=4] {'ctx'}, use_global_device_ids=true, to_apply=%region_28.29 | all-reduce | flops 1152 | bytes 9216 | tf_op jit(solution)/shard_map/psum | solution.py:220
  519.5 10.2 %all-reduce.17.cloned.1.call-done = (f32[3,192,192]{1,2,0:T(8,128)}, f32[192,192]{1,0:T(8,128)}, f32[192,768]{1,0:T(8,128)}, f32[768,192]{0,1:T(8,128)}) async-done(((f32[3,192,192]{1,2,0:T(8,128)}, f32[192,192]{1,0:T(8,128)}, f32[192,768]{1,0:T(8,128)}, f32[768,192]{0,1:T(8,128)}), (f32[3,192,192]{1,2,0:T(8,128)}, f32[192,192]{1,0:T(8,128)}, f32[192,768]{1,0:T(8,128)}, ...) | async-done | bytes 1769488 | tf_op jit(solution)/shard_map/psum | solution.py:220
  (182 shorter events, 108.7 us)
Async XLA Ops:
  8.0 18.3 %copy-start.20 = (bf16[4,192]{1,0:T(4,128)(2,1)S(1)}, bf16[4,192]{1,0:T(4,128)(2,1)}, u32[]{:S(2)}) copy-start(bf16[4,192]{1,0:T(4,128)(2,1)} %param.18) | copy-start | bytes 4612
  8.0 30.3 %copy-start.19 = (bf16[192,192]{1,0:T(8,128)(2,1)S(1)}, bf16[192,192]{1,0:T(8,128)(2,1)}, u32[]{:S(2)}) copy-start(bf16[192,192]{1,0:T(8,128)(2,1)} %param.14) | copy-start | bytes 221188
  8.0 46.2 %copy-start.18 = (bf16[3,192,192]{2,1,0:T(8,128)(2,1)S(1)}, bf16[3,192,192]{2,1,0:T(8,128)(2,1)}, u32[]{:S(2)}) copy-start(bf16[3,192,192]{2,1,0:T(8,128)(2,1)} %param.13) | copy-start | bytes 663556
  8.0 152.5 %all-reduce.9.cloned.1.call-start = ((), (), s32[]{:S(2)}) async-start(), calls=%async_computation.8 | async-start | bytes 3194880 | tf_op jit(solution)/shard_map/psum | solution.py:138
  95.9 14.4 %copy-start.5 = (bf16[1,1040,192]{1,2,0:T(8,128)(2,1)}, bf16[1,1040,192]{1,2,0:T(8,128)(2,1)S(1)}, u32[]{:S(2)}) copy-start(bf16[1,1040,192]{1,2,0:T(8,128)(2,1)S(1)} %copy.47) | copy-start | bytes 1198084
  117.9 44.7 %all-gather.5.cloned.1.call-start = ((), (), s32[]{:S(2)}) async-start(), calls=%async_computation.9 | async-start | bytes 1474560 | tf_op jit(solution)/shard_map/all_gather | solution.py:108
  118.5 61.7 %all-gather.7.cloned.1.call-start = ((), (), s32[]{:S(2)}) async-start(), calls=%async_computation.10 | async-start | bytes 1474560 | tf_op jit(solution)/shard_map/all_gather | solution.py:109
  119.1 110.5 %all-reduce.13.cloned.1.call-start = ((), (), s32[]{:S(2)}) async-start(), calls=%async_computation.12 | async-start | bytes 3194880 | tf_op jit(solution)/shard_map/psum | solution.py:169
  186.9 83.4 %reduce-scatter.27.cloned.1.call-start = ((), (), s32[]{:S(2)}) async-start(), calls=%async_computation.17 | async-start | bytes 1597440
  229.6 6.7 %slice-start = ((s8[7188480]{0:T(1024)(128)(4,1)}), s8[4194304]{0:T(1024)(128)(4,1)S(1)}, s32[]{:S(2)}) async-start(s8[7188480]{0:T(1024)(128)(4,1)} %bitcast.146), calls=%async_computation.23 | async-start | bytes 8388608
  249.7 43.4 %reduce-scatter.25.cloned.1.call-start = ((), (), s32[]{:S(2)}) async-start(), calls=%async_computation.16 | async-start | bytes 1597440
  262.1 80.6 %all-reduce.15.cloned.1.call-start = ((), (), s32[]{:S(2)}) async-start(), calls=%async_computation.13 | async-start | bytes 3194880 | tf_op jit(solution)/shard_map/psum | solution.py:200
  272.6 30.5 %copy-start.10 = (bf16[1,520,192]{1,2,0:T(8,128)(2,1)}, bf16[1,520,192]{1,2,0:T(8,128)(2,1)S(1)}, u32[]{:S(2)}) copy-start(bf16[1,520,192]{1,2,0:T(8,128)(2,1)S(1)} %copy.54) | copy-start | bytes 599044
  299.2 47.8 %reduce-scatter.31.cloned.1.call-start = ((), (), s32[]{:S(2)}) async-start(), calls=%async_computation.19 | async-start | bytes 983040
  303.0 66.4 %reduce-scatter.29.cloned.1.call-start = ((), (), s32[]{:S(2)}) async-start(), calls=%async_computation.18 | async-start | bytes 2457600
  314.5 104.1 %reduce-scatter.21.cloned.1.call-start = ((), (), s32[]{:S(2)}) async-start(), calls=%async_computation.14 | async-start | bytes 2949120 | tf_op jit(solution)/shard_map/reduce_scatter | solution.py:224
  318.6 149.6 %reduce-scatter.23.cloned.1.call-start = ((), (), s32[]{:S(2)}) async-start(), calls=%async_computation.15 | async-start | bytes 2949120 | tf_op jit(solution)/shard_map/reduce_scatter | solution.py:225
  322.8 146.1 %all-reduce.11.cloned.1.call-start = ((), (), s32[]{:S(2)}) async-start(), calls=%async_computation.11 | async-start | bytes 1597440 | tf_op jit(solution)/shard_map/psum | solution.py:149
  326.1 168.7 %reduce-scatter.33.cloned.1.call-start = ((), (), s32[]{:S(2)}) async-start(), calls=%async_computation.20 | async-start | bytes 491520
  346.0 166.9 %reduce-scatter.35.cloned.1.call-start = ((), (), s32[]{:S(2)}) async-start(), calls=%async_computation.21 | async-start | bytes 491520
  347.0 182.7 %all-reduce.17.cloned.1.call-start = ((), (), s32[]{:S(2)}) async-start(), calls=%async_computation.22 | async-start | bytes 3932160 | tf_op jit(solution)/shard_map/psum | solution.py:220
  372.0 98.7 %copy-start.11 = (bf16[1,520,192]{1,2,0:T(8,128)(2,1)S(1)}, bf16[1,520,192]{1,2,0:T(8,128)(2,1)}, u32[]{:S(2)}) copy-start(bf16[1,520,192]{1,2,0:T(8,128)(2,1)} %copy-done.10) | copy-start | bytes 599044
  372.0 98.7 %copy-start.13 = (bf16[1,520,192]{1,2,0:T(8,128)(2,1)S(1)}, bf16[1,520,192]{1,2,0:T(8,128)(2,1)}, u32[]{:S(2)}) copy-start(bf16[1,520,192]{1,2,0:T(8,128)(2,1)} %copy.52) | copy-start | bytes 599044
  470.7 21.5 %copy-start.4 = (f32[520,768]{1,0:T(8,128)S(1)}, f32[520,768]{1,0:T(8,128)}, u32[]{:S(2)}) copy-start(f32[520,768]{1,0:T(8,128)} %all-reduce.15.cloned.1.call-done) | copy-start | bytes 4792324
  (18 other events, 43.1 us)
Sparse Core Ops, SparseCore 0:
  118.0 42.4 all-reduce.8
  187.0 42.5 all-reduce.12
  249.8 20.4 reduce-scatter.26
  272.5 20.4 reduce-scatter.24
  299.4 43.3 all-reduce.14
  345.0 34.5 all-reduce.10
  468.3 61.3 all-reduce.16
Sparse Core Ops, SparseCore 1:
  120.0 29.3 all-gather.4
  150.7 29.4 all-gather.6
  303.1 23.0 reduce-scatter.30
  328.5 40.9 reduce-scatter.28
  371.8 46.7 reduce-scatter.20
  420.9 47.2 reduce-scatter.22
  471.0 20.1 reduce-scatter.32
  493.9 18.9 reduce-scatter.34
where the time goes:
time: 544 us; the launch traced here: 543 us
  waiting for transfers between devices  280 us (51%)
  blocking collectives  112 us (21%)
  local copies, waits for them, and re-layouts  53.1 us (10%)
  matrix products  51.7 us (10%)
  other arithmetic  28.1 us (5%)
  between operations  16.2 us (3%)
    unnamed x21, waiting for transfers between devices  63.9 us
    reduce_scatter x1, waiting for transfers between devices, per_device(): lax.psum_scatter(summed[3], 'shard', scatter_dimension=1, tiled=True)  49.6 us
    reduce_scatter x1, waiting for transfers between devices, per_device(): lax.psum_scatter(summed[2], 'shard', scatter_dimension=0, tiled=True)  46.6 us
    unnamed x77, local copies, waits for them, and re-layouts  43 us
    psum x1, waiting for transfers between devices, per_device(): grad_normed_two = lax.psum(grad_normed_part, 'tp')  42.7 us
    psum x1, waiting for transfers between devices, per_device(): attn_sum = lax.psum(attn_part, 'tp')  39.9 us
    all_gather x1, blocking collectives, per_device(): lax.all_gather(qkv_weight, 'shard', axis=1, tiled=True)  22.9 us
    psum x1, blocking collectives, per_device(): bias_totals = lax.psum((head_grad, hidden_grad), ('shard', 'ctx'))  21.1 us
  transfers between devices with their start and end apart: 15, of which 11 were waited for; matrix products, arithmetic and copies ran while one was open for 13% of the time, Pallas kernels for 0%

commit v1 on v0

v1 whole, which is shorter than its diff:
```python
import math

import jax
import jax.numpy as jnp
from jax import lax
from jax.sharding import PartitionSpec as P

HD = 64
EPS = 1e-06
NEG = -1e30
F32 = jnp.float32
LOW = jnp.bfloat16


def norm_stats(values):
    centred = values - jnp.mean(values, axis=-1, keepdims=True)
    rate = lax.rsqrt(jnp.mean(centred * centred, axis=-1, keepdims=True) + EPS)
    return centred * rate, rate


def norm_back(grad, scaled, rate, gain):
    e = grad * gain
    inner = jnp.mean(e * scaled, axis=-1, keepdims=True)
    return rate * (e - jnp.mean(e, axis=-1, keepdims=True) - scaled * inner)


def dot(left, right, left_dim=1, right_dim=0):
    return lax.dot_general(
        left, right, (((left_dim,), (right_dim,)), ((), ())), preferred_element_type=F32
    )


def per_device(
    activations,
    slot_counts,
    qkv_weight,
    proj_weight,
    up_weight,
    down_weight,
    norm_gains,
    row_biases,
    head_biases,
    hidden_bias,
    cotangent,
):
    images, slots, width = activations.shape
    n_shard = lax.axis_size("shard")
    n_ctx = lax.axis_size("ctx")
    n_tp = lax.axis_size("tp")
    assert images == 1 and n_ctx == 2 and n_tp == 4
    part = width // n_shard
    heads_width = qkv_weight.shape[2]
    hidden_width = up_weight.shape[1]
    quarter = slots // n_tp
    shard = lax.axis_index("shard")
    ctx = lax.axis_index("ctx")
    tp = lax.axis_index("tp")

    def over_ctx(x):
        return lax.ppermute(x, "ctx", [(i, i ^ 1) for i in range(n_ctx)])

    def over_tp(x, bit):
        return lax.ppermute(x, "tp", [(i, i ^ bit) for i in range(n_tp)])

    def shift(x, k):
        return lax.ppermute(x, "shard", [(i, (i + k) % n_shard) for i in range(n_shard)])

    def pick(x, i):
        return lax.dynamic_index_in_dim(x, i, 0, keepdims=False)

    def half(x, axis, which):
        size = x.shape[axis] // 2
        return lax.dynamic_slice_in_dim(x, which * size, size, axis)

    def whole_shards(x, axis):
        mine = half(x, axis, ctx)
        held = [mine] + [shift(mine, k) for k in range(1, n_shard)]
        mine_all = jnp.stack(held[1:])
        other_all = over_ctx(mine_all)
        lower = jnp.where(ctx == 0, mine_all, other_all)
        upper = jnp.where(ctx == 0, other_all, mine_all)
        fetched = jnp.concatenate([lower, upper], axis=axis + 1)
        local = jnp.concatenate([x[None], fetched], axis=0)
        order = (shard - jnp.arange(n_shard)) % n_shard
        return jnp.take(local, order, axis=0)

    def spread_tp(x):
        far = over_tp(x, 2)
        near = over_tp(jnp.stack([x, far]), 1)
        return [x, near[0], far, near[1]]

    def sum_tp(blocks):
        near = over_tp(jnp.stack([blocks[1], blocks[3]]).astype(LOW), 1).astype(F32)
        own = blocks[0].astype(F32) + near[0]
        other = (blocks[2].astype(F32) + near[1]).astype(LOW)
        return own + over_tp(other, 2).astype(F32)

    def rows_of(x):
        cut = x.reshape(n_tp, quarter, width)
        return [pick(cut, tp ^ j) for j in range(n_tp)]

    def sum_owned(blocks, axis):
        sent = over_ctx(half(blocks, axis + 1, 1 - ctx).astype(LOW))
        mine = half(blocks, axis + 1, ctx).astype(F32) + sent.astype(F32)
        total = pick(mine, shard)
        low = mine.astype(LOW)
        for k in range(1, n_shard):
            total = total + shift(pick(low, (shard + k) % n_shard), k).astype(F32)
        other = over_ctx(total.astype(LOW)).astype(F32)
        lower = jnp.where(ctx == 0, total, other)
        upper = jnp.where(ctx == 0, other, total)
        return jnp.concatenate([lower, upper], axis=axis)

    act = activations[0]
    act_other = over_ctx(act)
    vectors = jnp.concatenate([norm_gains, row_biases], axis=0)
    vec_rows = -(-vectors.size // (heads_width * 16)) * 16
    vec_pack = jnp.pad(vectors.reshape(-1), (0, vec_rows * heads_width - vectors.size))
    first_pack = jnp.concatenate(
        [qkv_weight.reshape(3 * part, heads_width), vec_pack.reshape(vec_rows, heads_width)]
    )
    first = lax.all_gather(first_pack, "shard")
    qkv_full = (
        first[:, : 3 * part].reshape(n_shard, 3, part, heads_width).swapaxes(0, 1)
    ).reshape(3, width, heads_width)
    vec_full = first[:, 3 * part :].reshape(n_shard, -1)[:, : vectors.size]
    vec_full = (
        vec_full.reshape(n_shard, 6, part).swapaxes(0, 1).reshape(6, width).astype(F32)
    )
    gains, shifts = vec_full[:2], vec_full[2:]

    proj_own = whole_shards(proj_weight, 0).swapaxes(0, 1).reshape(heads_width, width)
    up_full = whole_shards(up_weight, 1).reshape(width, hidden_width)
    down_full = whole_shards(down_weight, 0).swapaxes(0, 1).reshape(hidden_width, width)
    proj_full = jnp.concatenate(spread_tp(proj_own), axis=0)

    slot_ids = jnp.arange(slots, dtype=jnp.int32)
    own_count = jnp.where(ctx == 0, slot_counts[0, 0], slot_counts[0, 1])
    other_count = jnp.where(ctx == 0, slot_counts[0, 1], slot_counts[0, 0])
    row_valid = (slot_ids < own_count)[:, None]
    key_valid = jnp.concatenate([slot_ids < own_count, slot_ids < other_count])

    act_in = act.astype(F32)
    both = jnp.concatenate([act_in, act_other.astype(F32)])
    scaled_one, rate_one = norm_stats(both)
    normed_low = (scaled_one * gains[0] + shifts[0]).astype(LOW)
    biases = head_biases.astype(F32)
    queries = (dot(normed_low[:slots], qkv_full[0]) + biases[0]).astype(LOW)
    keys = dot(normed_low, qkv_full[1]).astype(LOW)
    values = (dot(normed_low, qkv_full[2]) + biases[1]).astype(LOW)
    scale = 1.0 / math.sqrt(HD)
    query_heads = queries.reshape(slots, -1, HD)
    key_heads = keys.reshape(2 * slots, -1, HD)
    value_heads = values.reshape(2 * slots, -1, HD)
    scores = jnp.einsum("qhd,khd->hqk", query_heads, key_heads, preferred_element_type=F32)
    scores = jnp.where(key_valid[None, None, :], scores * scale, NEG)
    probs_low = jax.nn.softmax(scores, axis=-1).astype(LOW)
    mixed = jnp.einsum("hqk,khd->qhd", probs_low, value_heads, preferred_element_type=F32)
    mixed = mixed.reshape(slots, heads_width).astype(LOW)

    mixed_full = jnp.concatenate(spread_tp(mixed), axis=1)
    middle = act_in + dot(mixed_full, proj_full) + shifts[2]
    scaled_two, rate_two = norm_stats(middle)
    normed_two = (scaled_two * gains[1] + shifts[1]).astype(LOW)
    hidden = dot(normed_two, up_full) + hidden_bias.astype(F32)
    gelu_out, gelu_back = jax.vjp(lambda v: jax.nn.gelu(v, approximate=False), hidden)
    gelu_low = gelu_out.astype(LOW)
    grad_branch = jnp.where(row_valid, cotangent[0], jnp.zeros((), LOW))
    grad_out = grad_branch.astype(F32)
    (grad_hidden,) = gelu_back(dot(grad_branch, down_full, 1, 1))
    grad_hidden = grad_hidden.astype(LOW)
    grad_two = dot(grad_hidden, up_full, 1, 1)
    back_two = norm_back(grad_two, scaled_two, rate_two, gains[1])
    back_low = back_two.astype(LOW)
    back_mixed = dot(back_low, proj_full, 1, 1).reshape(slots, n_tp, heads_width)
    grad_mixed = sum_tp([back_mixed[:, j] for j in range(n_tp)])
    grad_mixed = (grad_mixed + dot(grad_branch, proj_own, 1, 1)).astype(LOW)

    mlp_sum = sum_tp(rows_of(dot(gelu_low, down_full).astype(LOW)))
    own_valid = rows_of(jnp.broadcast_to(row_valid, (slots, width)))[0]
    layer_out = jnp.where(own_valid, rows_of(middle)[0] + mlp_sum + shifts[3], 0.0).astype(LOW)
    back_rows = sum_tp(rows_of(back_low))
    grad_middle = rows_of(grad_out)[0] + back_rows
    attn_blocks = jnp.stack(spread_tp(grad_middle.astype(LOW)))
    grad_attn = jnp.take(attn_blocks, tp ^ jnp.arange(n_tp), axis=0).reshape(slots, width)

    down_blocks = dot(gelu_low, grad_branch, 0, 0).reshape(hidden_width, n_shard, part)
    down_grad = sum_owned(down_blocks.swapaxes(0, 1), 0)
    up_blocks = dot(normed_two, grad_hidden, 0, 0).reshape(n_shard, part, hidden_width)
    up_grad = sum_owned(up_blocks, 1)
    proj_blocks = dot(mixed, grad_attn, 0, 0).reshape(heads_width, n_shard, part)
    proj_grad = sum_owned(proj_blocks.swapaxes(0, 1), 0)

    grad_heads = grad_mixed.reshape(slots, -1, HD)
    mixed_heads = mixed.reshape(slots, -1, HD)
    inner = jnp.sum(grad_heads.astype(F32) * mixed_heads.astype(F32), axis=-1)
    grad_probs = jnp.einsum("qhd,khd->hqk", grad_heads, value_heads, preferred_element_type=F32)
    grad_scores = (probs_low.astype(F32) * (grad_probs - inner.T[:, :, None])).astype(LOW)
    grad_values = jnp.einsum("hqk,qhd->khd", probs_low, grad_heads, preferred_element_type=F32)
    grad_keys = jnp.einsum("hqk,qhd->khd", grad_scores, query_heads, preferred_element_type=F32)
    grad_queries = jnp.einsum("hqk,khd->qhd", grad_scores, key_heads, preferred_element_type=F32)
    grad_queries = (grad_queries * scale).reshape(slots, heads_width).astype(LOW)
    grad_keys = (grad_keys * scale).reshape(2 * slots, heads_width).astype(LOW)
    grad_values = grad_values.reshape(2 * slots, heads_width).astype(LOW)

    grad_other = dot(grad_keys, qkv_full[1], 1, 1) + dot(grad_values, qkv_full[2], 1, 1)
    grad_own = grad_other[:slots] + dot(grad_queries, qkv_full[0], 1, 1)
    grad_one = jnp.concatenate([grad_own, grad_other[slots:]])
    own_rows = rows_of(grad_one[:slots].astype(LOW))
    other_rows = rows_of(grad_one[slots:].astype(LOW))
    near = over_tp(jnp.stack([own_rows[1], own_rows[3], other_rows[1], other_rows[3]]), 1)
    summed = jnp.stack([own_rows[0], own_rows[2], other_rows[0], other_rows[2]]).astype(F32)
    summed = summed + near.astype(F32)
    summed_low = summed.astype(LOW)
    from_tp = over_tp(summed_low[1], 2)
    from_ctx = over_ctx(summed_low[2])
    pairs = [(i, i ^ (n_tp + 2)) for i in range(n_ctx * n_tp)]
    from_far = lax.ppermute(summed_low[3], ("ctx", "tp"), pairs)
    grad_rows = summed[0] + from_tp.astype(F32) + from_ctx.astype(F32) + from_far.astype(F32)

    qkv_grads = [
        dot(normed_low[:slots], grad_queries, 0, 0),
        dot(normed_low, grad_keys, 0, 0),
        dot(normed_low, grad_values, 0, 0),
    ]
    qkv_blocks = jnp.stack(qkv_grads).reshape(3, n_shard, part, heads_width).swapaxes(0, 1)
    qkv_grad = sum_owned(qkv_blocks, 1)

    own_scaled, own_rate = norm_stats(rows_of(act_in)[0])
    input_grad = (grad_middle + norm_back(grad_rows, own_scaled, own_rate, gains[0])).astype(LOW)

    first_tp = jnp.where(tp == 0, 1.0, 0.0)
    branch_sum = jnp.sum(grad_out, axis=0) * first_tp
    head_sums = jnp.concatenate(
        [
            jnp.sum(grad_queries.astype(F32), axis=0),
            jnp.sum(grad_values.astype(F32), axis=0),
            jnp.zeros((width - 2 * heads_width,), F32),
        ]
    )
    sums = jnp.stack(
        [
            jnp.sum(grad_one * scaled_one, axis=0),
            jnp.sum(grad_two * scaled_two, axis=0),
            jnp.sum(grad_one, axis=0),
            jnp.sum(grad_two, axis=0),
            branch_sum + jnp.sum(back_two, axis=0),
            branch_sum,
        ]
    )
    for bit in (1, 2):
        sums = sums + over_tp(sums, bit)
    own_sums = jnp.stack([jnp.sum(grad_hidden.astype(F32), axis=0), head_sums])
    sums = jnp.concatenate([sums, own_sums])
    sums = sums + over_ctx(sums)
    bit = 1
    while bit < n_shard:
        sums = sums + lax.ppermute(sums, "shard", [(i, i ^ bit) for i in range(n_shard)])
        bit *= 2
    vector_grads = lax.dynamic_slice_in_dim(sums[:6], shard * part, part, 1)
    return (
        layer_out[None],
        input_grad[None],
        qkv_grad,
        proj_grad,
        up_grad,
        down_grad,
        vector_grads[:2],
        vector_grads[2:],
        sums[7, : 2 * heads_width].reshape(2, heads_width),
        sums[6],
    )


def solution(mesh):
    placed = (
        P("shard", "ctx", None),
        P("shard", None),
        P(None, "shard", "tp"),
        P("tp", "shard"),
        P("shard", "tp"),
        P("tp", "shard"),
        P(None, "shard"),
        P(None, "shard"),
        P(None, "tp"),
        P("tp"),
        P("shard", "ctx", None),
    )
    return jax.shard_map(
        per_device,
        mesh=mesh,
        in_specs=placed,
        out_specs=(
            P("shard", ("ctx", "tp"), None),
            P("shard", ("ctx", "tp"), None),
            P(None, "shard", "tp"),
            P("tp", "shard"),
            P("shard", "tp"),
            P("tp", "shard"),
            P(None, "shard"),
            P(None, "shard"),
            P(None, "tp"),
            P("tp"),
        ),
        check_vma=False,
    )
```

time: 544 us -> 349 us (0.64)
  waiting for transfers between devices: 280 us -> 74.9 us
  blocking collectives: 112 us -> 21.9 us
  starting transfers between devices: 1.04 us -> 61.7 us
  other arithmetic: 28.1 us -> 64.9 us
  local copies, waits for them, and re-layouts: 53.1 us -> 71.8 us
  between operations: 16.2 us -> 4.82 us
  matrix products: 51.7 us -> 43.9 us
    psum x5 -> x0, waiting for transfers between devices: 109 us -> none  [the longest x1 42.7 us: per_device(): grad_normed_two = lax.psum(grad_normed_part, 'tp')]
    reduce_scatter x2 -> x0, waiting for transfers between devices: 96.2 us -> none  [the longest x1 49.6 us: per_device(): lax.psum_scatter(summed[3], 'shard', scatter_dimension=1, tiled=True)]
    ppermute x0 -> x54, waiting for transfers between devices: none -> 74.9 us  [the longest x14 40.2 us: over_ctx(): return lax.ppermute(x, 'ctx', [(i, i ^ 1) for i in range(n_ctx)])]
    unnamed x21 -> x0, waiting for transfers between devices: 63.9 us -> none
    all_gather x6 -> x1, blocking collectives: 85.3 us -> 21.9 us  [per_device(): first = lax.all_gather(first_pack, 'shard')]
    ppermute x0 -> x54, starting transfers between devices: none -> 61.7 us  [the longest x21 30.6 us: shift(): lax.ppermute(x, 'shard', [(i, (i + k) % n_shard) for i in range(n_shard)])]
    psum x2 -> x0, blocking collectives: 26.9 us -> none  [the longest x1 21.1 us: per_device(): bias_totals = lax.psum((head_grad, hidden_grad), ('shard', 'ctx'))]
    unnamed x77 -> x163, local copies, waits for them, and re-layouts: 43 us -> 16.2 us
  transfers between devices with their start and end apart: 15 -> 54, of which waited for: 11 -> 21; matrix products, arithmetic and copies ran while one was open for 13% -> 41% of each run, Pallas kernels for 0% -> 0%
where the time goes in v1:
time: 349 us; the launch traced here: 344 us
  waiting for transfers between devices  74.9 us (21%)
  local copies, waits for them, and re-layouts  71.8 us (21%)
  other arithmetic  64.9 us (19%)
  starting transfers between devices  61.7 us (18%)
  matrix products  43.9 us (13%)
  blocking collectives  21.9 us (6%)
  between operations  4.82 us (1%)
    ppermute x14, waiting for transfers between devices, over_ctx(): return lax.ppermute(x, 'ctx', [(i, i ^ 1) for i in range(n_ctx)])  40.2 us
    dot_general x19, matrix products, dot(): lax.dot_general(left, right, (((left_dim,), (right_dim,)), ((), ())), pre...  31.9 us
    ppermute x21, starting transfers between devices, shift(): lax.ppermute(x, 'shard', [(i, (i + k) % n_shard) for i in range(n_shard)])  30.6 us
    all_gather x1, blocking collectives, per_device(): first = lax.all_gather(first_pack, 'shard')  21.9 us
    ppermute x14, starting transfers between devices, over_ctx(): return lax.ppermute(x, 'ctx', [(i, i ^ 1) for i in range(n_ctx)])  17.3 us
    ppermute x21, waiting for transfers between devices, shift(): lax.ppermute(x, 'shard', [(i, (i + k) % n_shard) for i in range(n_shard)])  17 us
    unnamed x163, local copies, waits for them, and re-layouts  16.2 us
    ppermute x16, starting transfers between devices, over_tp(): return lax.ppermute(x, 'tp', [(i, i ^ bit) for i in range(n_tp)])  12.4 us
  transfers between devices with their start and end apart: 54, of which 21 were waited for; matrix products, arithmetic and copies ran while one was open for 41% of the time, Pallas kernels for 0%

profile of v1, /device:TPU:0, one launch (start us, length us, event | category | flops | bytes accessed | tf_op | source)
XLA Modules:
  0.0 343.9 jit_solution(8871572190696863287)
XLA Ops:
  2.1 3.0 collective-permute-start.3
  5.1 2.6 collective-permute-start.4
  22.0 21.9 %all-gather.1 = bf16[4,592,192]{1,2,0:T(8,128)(2,1)S(1)} all-gather(bf16[1,592,192]{1,2,0:T(8,128)(2,1)S(1)} %copy.53), channel_id=2, replica_groups=mesh['shard'=4,'ctx'=2,'tp'=4] {'shard'}, dimensions={0}, use_global_device_ids=true | all-gather | bytes 1136640 | tf_op jit(solution)/shard_map/all_gather | solution.py:122
  92.1 16.9 %collective-permute-done.12 = bf16[3,192,384]{2,1,0:T(8,128)(2,1)} collective-permute-done((bf16[3,192,384]{2,1,0:T(8,128)(2,1)}, bf16[3,192,384]{2,1,0:T(8,128)(2,1)}, u32[]{:S(2)}, u32[]{:S(2)}) %collective-permute-start.12) | collective-permute-done | bytes 442400 | tf_op jit(solution)/shard_map/ppermute | solution.py:60
  124.5 6.3 %fusion.108 = (f32[3,520]{1,0:T(4,128)S(1)}, f32[3,520,1040]{2,1,0:T(8,128)}) fusion(pred[1040]{0:T(1024)(128)(4,1)S(1)} %copy-done.74, bf16[520,3,64]{0,2,1:T(8,128)(2,1)S(1)} %bitcast.378, bf16[1040,3,64]{0,2,1:T(8,128)(2,1)} %bitcast.353), kind=kOutput, calls=%fused_computation.302 | convolution fusion | flops 214157824 | bytes 7095920 | tf_op jit(solution)/shard_map/sub | solution.py:157
  130.9 3.9 %divide_convert_fusion = bf16[3,520,1040]{2,1,0:T(8,128)(2,1)S(1)} fusion(f32[3,520,1040]{2,1,0:T(8,128)} %get-tuple-element.112, f32[3,520]{1,0:T(4,128)S(1)} %get-tuple-element.111), kind=kLoop, calls=%fused_computation.6 | loop fusion | flops 3244800 | bytes 9740640 | tf_op jit(solution)/shard_map/convert_element_type | solution.py:157
  139.6 3.5 %collective-permute-done.1 = bf16[520,192]{0,1:T(8,128)(2,1)S(1)} collective-permute-done((bf16[520,192]{0,1:T(8,128)(2,1)S(1)}, bf16[520,192]{0,1:T(8,128)(2,1)S(1)}, u32[]{:S(2)}, u32[]{:S(2)}) %collective-permute-start.1) | collective-permute-done | bytes 199712 | tf_op jit(solution)/shard_map/ppermute | solution.py:63
  148.0 3.8 %copy.65 = bf16[768,1040]{1,0:T(8,128)(2,1)} copy(bf16[768,1040]{0,1:T(8,128)(2,1)} %bitcast.325) | data formatting | bytes 3194880 | tf_op jit(solution)/shard_map/dot_general | solution.py:28
  158.3 5.3 %multiply_convert_fusion.1 = (bf16[520,768]{1,0:T(8,128)(2,1)}, f32[520,768]{1,0:T(8,128)S(1)}, f32[520,768]{1,0:T(8,128)S(1)}) fusion(f32[768]{0:T(1024)S(1)} %copy-done.66, bf16[768,768]{1,0:T(8,128)(2,1)S(1)} %copy-done.38, f32[520,768]{1,0:T(8,128)S(1)} %get-tuple-element.114, f32[768]{0:T(1024)S(1)} %copy-done.67, f32[768]{0:T(1024)S(1)} %mul.217, ...), kind=kOutput, calls=%fused_computation.36 | convolution fusion | flops 641771520 | bytes 6784064 | tf_op jit(solution)/shard_map/dot_general | solution.py:28
  167.1 2.9 fusion.84
  170.1 2.8 reshape.379
  172.9 3.3 fusion.87
  211.5 4.2 %collective-permute-done.39 = bf16[4,192,384]{2,1,0:T(8,128)(2,1)} collective-permute-done((bf16[4,192,384]{2,1,0:T(8,128)(2,1)}, bf16[4,192,384]{2,1,0:T(8,128)(2,1)}, u32[]{:S(2)}, u32[]{:S(2)}) %collective-permute-start.39) | collective-permute-done | bytes 589856 | tf_op jit(solution)/shard_map/ppermute | solution.py:60
  238.4 3.3 pad_maximum_fusion.1
  252.9 2.8 collective-permute-done.52
  268.4 3.3 collective-permute-done.40
  273.1 4.4 %collective-permute-done.41 = bf16[192,384]{1,0:T(8,128)(2,1)S(1)} collective-permute-done((bf16[192,384]{1,0:T(8,128)(2,1)S(1)}, bf16[192,384]{1,0:T(8,128)(2,1)S(1)}, u32[]{:S(2)}, u32[]{:S(2)}) %collective-permute-start.41) | collective-permute-done | bytes 147488 | tf_op jit(solution)/shard_map/ppermute | solution.py:66
  280.7 10.2 %collective-permute-done.48 = bf16[384,192]{0,1:T(8,128)(2,1)S(1)} collective-permute-done((bf16[384,192]{0,1:T(8,128)(2,1)S(1)}, bf16[384,192]{0,1:T(8,128)(2,1)S(1)}, u32[]{:S(2)}, u32[]{:S(2)}) %collective-permute-start.48) | collective-permute-done | bytes 147488 | tf_op jit(solution)/shard_map/ppermute | solution.py:60
  296.8 3.7 %collective-permute-done.24 = bf16[130,768]{1,0:T(8,128)(2,1)S(1)} collective-permute-done((bf16[130,768]{1,0:T(8,128)(2,1)S(1)}, bf16[130,768]{1,0:T(8,128)(2,1)S(1)}, u32[]{:S(2)}, u32[]{:S(2)}) %collective-permute-start.24) | collective-permute-done | bytes 199712 | tf_op jit(solution)/shard_map/ppermute | solution.py:63
  308.5 2.8 collective-permute-done.32
  313.5 3.7 %collective-permute-start.30 = (bf16[3,96,192]{2,1,0:T(8,128)(2,1)}, bf16[3,96,192]{2,1,0:T(8,128)(2,1)}, u32[]{:S(2)}, u32[]{:S(2)}) collective-permute-start(bf16[3,96,192]{2,1,0:T(8,128)(2,1)} %get-tuple-element.86), channel_id=1, source_target_pairs={{0,24},{8,0},{16,8},{24,16},{1,25},{9,1},{17,9},{25,17},{2,26},{10... | collective-permute-start | bytes 331784 | tf_op jit(solution)/shard_map/ppermute | solution.py:66
  322.2 5.3 %collective-permute-done.29 = bf16[3,96,192]{2,1,0:T(8,128)(2,1)S(1)} collective-permute-done((bf16[3,96,192]{2,1,0:T(8,128)(2,1)}, bf16[3,96,192]{2,1,0:T(8,128)(2,1)S(1)}, u32[]{:S(2)}, u32[]{:S(2)}) %collective-permute-start.29) | collective-permute-done | bytes 110624 | tf_op jit(solution)/shard_map/ppermute | solution.py:66
  330.1 3.5 %collective-permute-start.35 = (bf16[96,192]{1,0:T(8,128)(2,1)S(1)}, bf16[96,192]{1,0:T(8,128)(2,1)S(1)}, u32[]{:S(2)}, u32[]{:S(2)}) collective-permute-start(bf16[96,192]{1,0:T(8,128)(2,1)S(1)} %get-tuple-element.102), channel_id=1, source_target_pairs={{0,8},{8,16},{16,24},{24,0},{1,9},{9,17},{17,25},{25,1},{2,10},{10... | collective-permute-start | bytes 110600 | tf_op jit(solution)/shard_map/ppermute | solution.py:66
  336.1 2.7 collective-permute-done.36
  (449 shorter events, 213.1 us)
Async XLA Ops:
  2.1 62.9 %collective-permute-start.3 = (bf16[96,192]{1,0:T(8,128)(2,1)}, bf16[96,192]{1,0:T(8,128)(2,1)}, u32[]{:S(2)}, u32[]{:S(2)}) collective-permute-start(bf16[96,192]{1,0:T(8,128)(2,1)} %constant_dynamic-slice_fusion.15), channel_id=1, source_target_pairs={{0,8},{8,16},{16,24},{24,0},{1,9},{9,17},{17,25},{25,1},{2,10},{10... | collective-permute-start | bytes 110600 | tf_op jit(solution)/shard_map/ppermute | solution.py:66
  5.1 60.8 %collective-permute-start.4 = (bf16[96,192]{1,0:T(8,128)(2,1)}, bf16[96,192]{1,0:T(8,128)(2,1)}, u32[]{:S(2)}, u32[]{:S(2)}) collective-permute-start(bf16[96,192]{1,0:T(8,128)(2,1)} %constant_dynamic-slice_fusion.15), channel_id=1, source_target_pairs={{0,16},{8,24},{16,0},{24,8},{1,17},{9,25},{17,1},{25,9},{2,18},{10... | collective-permute-start | bytes 110600 | tf_op jit(solution)/shard_map/ppermute | solution.py:66
  7.7 59.3 %collective-permute-start.5 = (bf16[96,192]{1,0:T(8,128)(2,1)}, bf16[96,192]{1,0:T(8,128)(2,1)}, u32[]{:S(2)}, u32[]{:S(2)}) collective-permute-start(bf16[96,192]{1,0:T(8,128)(2,1)} %constant_dynamic-slice_fusion.15), channel_id=1, source_target_pairs={{0,24},{8,0},{16,8},{24,16},{1,25},{9,1},{17,9},{25,17},{2,26},{10... | collective-permute-start | bytes 110600 | tf_op jit(solution)/shard_map/ppermute | solution.py:66
  10.6 65.0 %collective-permute-start.9 = (bf16[192,384]{1,0:T(8,128)(2,1)}, bf16[192,384]{1,0:T(8,128)(2,1)}, u32[]{:S(2)}, u32[]{:S(2)}) collective-permute-start(bf16[192,384]{1,0:T(8,128)(2,1)} %constant_dynamic-slice_fusion.14), channel_id=1, source_target_pairs={{0,8},{8,16},{16,24},{24,0},{1,9},{9,17},{17,25},{25,1},{2,10},{10... | collective-permute-start | bytes 442376 | tf_op jit(solution)/shard_map/ppermute | solution.py:66
  11.3 67.9 %collective-permute-start.10 = (bf16[192,384]{1,0:T(8,128)(2,1)}, bf16[192,384]{1,0:T(8,128)(2,1)}, u32[]{:S(2)}, u32[]{:S(2)}) collective-permute-start(bf16[192,384]{1,0:T(8,128)(2,1)} %constant_dynamic-slice_fusion.14), channel_id=1, source_target_pairs={{0,16},{8,24},{16,0},{24,8},{1,17},{9,25},{17,1},{25,9},{2,18},{10... | collective-permute-start | bytes 442376 | tf_op jit(solution)/shard_map/ppermute | solution.py:66
  65.0 15.7 %collective-permute-start.11 = (bf16[192,384]{1,0:T(8,128)(2,1)}, bf16[192,384]{1,0:T(8,128)(2,1)S(1)}, u32[]{:S(2)}, u32[]{:S(2)}) collective-permute-start(bf16[192,384]{1,0:T(8,128)(2,1)} %constant_dynamic-slice_fusion.14), channel_id=1, source_target_pairs={{0,24},{8,0},{16,8},{24,16},{1,25},{9,1},{17,9},{25,17},{2,26},{10... | collective-permute-start | bytes 442376 | tf_op jit(solution)/shard_map/ppermute | solution.py:66
  65.9 18.2 %collective-permute-start.13 = (bf16[384,192]{0,1:T(8,128)(2,1)}, bf16[384,192]{0,1:T(8,128)(2,1)S(1)}, u32[]{:S(2)}, u32[]{:S(2)}) collective-permute-start(bf16[384,192]{0,1:T(8,128)(2,1)} %constant_dynamic-slice_fusion.13), channel_id=1, source_target_pairs={{0,8},{8,16},{16,24},{24,0},{1,9},{9,17},{17,25},{25,1},{2,10},{10... | collective-permute-start | bytes 442376 | tf_op jit(solution)/shard_map/ppermute | solution.py:66
  79.2 40.2 %collective-permute-start = (bf16[520,768]{1,0:T(8,128)(2,1)}, bf16[520,768]{1,0:T(8,128)(2,1)}, u32[]{:S(2)}, u32[]{:S(2)}) collective-permute-start(bf16[520,768]{1,0:T(8,128)(2,1)} %bitcast.348), channel_id=1, source_target_pairs={{0,4},{4,0},{1,5},{5,1},{2,6},{6,2},{3,7},{7,3},{8,12},{12,8},{9,1... | collective-permute-start | bytes 2396168 | tf_op jit(solution)/shard_map/ppermute | solution.py:60
  84.0 25.0 %collective-permute-start.12 = (bf16[3,192,384]{2,1,0:T(8,128)(2,1)}, bf16[3,192,384]{2,1,0:T(8,128)(2,1)}, u32[]{:S(2)}, u32[]{:S(2)}) collective-permute-start(bf16[3,192,384]{2,1,0:T(8,128)(2,1)} %pad_maximum_fusion.11), channel_id=1, source_target_pairs={{0,4},{4,0},{1,5},{5,1},{2,6},{6,2},{3,7},{7,3},{8,12},{12,8},{9,1... | collective-permute-start | bytes 1327112 | tf_op jit(solution)/shard_map/ppermute | solution.py:60
  86.4 27.4 %collective-permute-start.16 = (bf16[3,384,192]{1,2,0:T(8,128)(2,1)}, bf16[3,384,192]{1,2,0:T(8,128)(2,1)}, u32[]{:S(2)}, u32[]{:S(2)}) collective-permute-start(bf16[3,384,192]{1,2,0:T(8,128)(2,1)} %pad_maximum_fusion.12), channel_id=1, source_target_pairs={{0,4},{4,0},{1,5},{5,1},{2,6},{6,2},{3,7},{7,3},{8,12},{12,8},{9,1... | collective-permute-start | bytes 1327112 | tf_op jit(solution)/shard_map/ppermute | solution.py:60
  92.1 59.7 %collective-permute-start.8 = (bf16[2,192,768]{2,1,0:T(8,128)(2,1)}, bf16[2,192,768]{2,1,0:T(8,128)(2,1)}, u32[]{:S(2)}, u32[]{:S(2)}) collective-permute-start(bf16[2,192,768]{2,1,0:T(8,128)(2,1)} %pad_maximum_fusion.5), channel_id=1, source_target_pairs={{0,1},{1,0},{2,3},{3,2},{4,5},{5,4},{6,7},{7,6},{8,9},{9,8},{10,11... | collective-permute-start | bytes 1769480 | tf_op jit(solution)/shard_map/ppermute | solution.py:63
  187.5 20.3 %collective-permute-start.44 = (bf16[4,384,192]{1,2,0:T(8,128)(2,1)}, bf16[4,384,192]{1,2,0:T(8,128)(2,1)}, u32[]{:S(2)}, u32[]{:S(2)}) collective-permute-start(bf16[4,384,192]{1,2,0:T(8,128)(2,1)} %fusion.36), channel_id=1, source_target_pairs={{0,4},{4,0},{1,5},{5,1},{2,6},{6,2},{3,7},{7,3},{8,12},{12,8},{9,1... | collective-permute-start | bytes 1769480 | tf_op jit(solution)/shard_map/ppermute | solution.py:60
  191.2 24.6 %collective-permute-start.39 = (bf16[4,192,384]{2,1,0:T(8,128)(2,1)}, bf16[4,192,384]{2,1,0:T(8,128)(2,1)}, u32[]{:S(2)}, u32[]{:S(2)}) collective-permute-start(bf16[4,192,384]{2,1,0:T(8,128)(2,1)} %dynamic-slice_convert_fusion.1), channel_id=1, source_target_pairs={{0,4},{4,0},{1,5},{5,1},{2,6},{6,2},{3,7},{7,3},{8,12},{12,8},{9,1... | collective-permute-start | bytes 1769480 | tf_op jit(solution)/shard_map/ppermute | solution.py:60
  197.8 22.9 %collective-permute-start.22 = (bf16[520,192]{0,1:T(8,128)(2,1)S(1)}, bf16[520,192]{0,1:T(8,128)(2,1)S(1)}, u32[]{:S(2)}, u32[]{:S(2)}) collective-permute-start(bf16[520,192]{0,1:T(8,128)(2,1)S(1)} %fusion.38), channel_id=1, source_target_pairs={{0,2},{1,3},{2,0},{3,1},{4,6},{5,7},{6,4},{7,5},{8,10},{9,11},{10,... | collective-permute-start | bytes 599048 | tf_op jit(solution)/shard_map/ppermute | solution.py:63
  203.2 100.1 %collective-permute-start.20 = (bf16[130,768]{1,0:T(8,128)(2,1)}, bf16[130,768]{1,0:T(8,128)(2,1)}, u32[]{:S(2)}, u32[]{:S(2)}) collective-permute-start(bf16[130,768]{1,0:T(8,128)(2,1)} %fusion.68), channel_id=1, source_target_pairs={{0,2},{1,3},{2,0},{3,1},{4,6},{5,7},{6,4},{7,5},{8,10},{9,11},{10,... | collective-permute-start | bytes 599048 | tf_op jit(solution)/shard_map/ppermute | solution.py:63
  206.3 35.4 %collective-permute-start.18 = (bf16[130,768]{1,0:T(8,128)(2,1)}, bf16[130,768]{1,0:T(8,128)(2,1)}, u32[]{:S(2)}, u32[]{:S(2)}) collective-permute-start(bf16[130,768]{1,0:T(8,128)(2,1)} %fusion.67), channel_id=1, source_target_pairs={{0,2},{1,3},{2,0},{3,1},{4,6},{5,7},{6,4},{7,5},{8,10},{9,11},{10,... | collective-permute-start | bytes 599048 | tf_op jit(solution)/shard_map/ppermute | solution.py:63
  210.9 52.1 %collective-permute-start.45 = (bf16[384,192]{0,1:T(8,128)(2,1)}, bf16[384,192]{0,1:T(8,128)(2,1)}, u32[]{:S(2)}, u32[]{:S(2)}) collective-permute-start(bf16[384,192]{0,1:T(8,128)(2,1)} %get-tuple-element.79), channel_id=1, source_target_pairs={{0,8},{8,16},{16,24},{24,0},{1,9},{9,17},{17,25},{25,1},{2,10},{10... | collective-permute-start | bytes 442376 | tf_op jit(solution)/shard_map/ppermute | solution.py:66
  215.7 48.2 %collective-permute-start.46 = (bf16[384,192]{0,1:T(8,128)(2,1)}, bf16[384,192]{0,1:T(8,128)(2,1)}, u32[]{:S(2)}, u32[]{:S(2)}) collective-permute-start(bf16[384,192]{0,1:T(8,128)(2,1)} %get-tuple-element.81), channel_id=1, source_target_pairs={{0,16},{8,24},{16,0},{24,8},{1,17},{9,25},{17,1},{25,9},{2,18},{10... | collective-permute-start | bytes 442376 | tf_op jit(solution)/shard_map/ppermute | solution.py:66
  220.7 44.3 %collective-permute-start.47 = (bf16[384,192]{0,1:T(8,128)(2,1)}, bf16[384,192]{0,1:T(8,128)(2,1)}, u32[]{:S(2)}, u32[]{:S(2)}) collective-permute-start(bf16[384,192]{0,1:T(8,128)(2,1)} %get-tuple-element.80), channel_id=1, source_target_pairs={{0,24},{8,0},{16,8},{24,16},{1,25},{9,1},{17,9},{25,17},{2,26},{10... | collective-permute-start | bytes 442376 | tf_op jit(solution)/shard_map/ppermute | solution.py:66
  260.4 30.5 %collective-permute-start.23 = (bf16[4,130,768]{2,0,1:T(4,128)(2,1)}, bf16[4,130,768]{2,0,1:T(4,128)(2,1)S(1)}, u32[]{:S(2)}, u32[]{:S(2)}) collective-permute-start(bf16[4,130,768]{2,0,1:T(4,128)(2,1)} %copy.62), channel_id=1, source_target_pairs={{0,1},{1,0},{2,3},{3,2},{4,5},{5,4},{6,7},{7,6},{8,9},{9,8},{10,11... | collective-permute-start | bytes 2396168 | tf_op jit(solution)/shard_map/ppermute | solution.py:63
  271.6 39.7 %collective-permute-start.27 = (bf16[4,3,96,192]{3,2,0,1:T(8,128)(2,1)S(1)}, bf16[4,3,96,192]{3,2,0,1:T(8,128)(2,1)S(1)}, u32[]{:S(2)}, u32[]{:S(2)}) collective-permute-start(bf16[4,3,96,192]{3,2,0,1:T(8,128)(2,1)S(1)} %fusion.35), channel_id=1, source_target_pairs={{0,4},{4,0},{1,5},{5,1},{2,6},{6,2},{3,7},{7,3},{8,12},{12,8},{9,1... | collective-permute-start | bytes 1327112 | tf_op jit(solution)/shard_map/ppermute | solution.py:60
  280.0 16.3 %collective-permute-start.43 = (bf16[192,384]{1,0:T(8,128)(2,1)S(1)}, bf16[192,384]{1,0:T(8,128)(2,1)S(1)}, u32[]{:S(2)}, u32[]{:S(2)}) collective-permute-start(bf16[192,384]{1,0:T(8,128)(2,1)S(1)} %get-tuple-element.30), channel_id=1, source_target_pairs={{0,4},{4,0},{1,5},{5,1},{2,6},{6,2},{3,7},{7,3},{8,12},{12,8},{9,1... | collective-permute-start | bytes 442376 | tf_op jit(solution)/shard_map/ppermute | solution.py:60
  313.4 14.1 %collective-permute-start.29 = (bf16[3,96,192]{2,1,0:T(8,128)(2,1)}, bf16[3,96,192]{2,1,0:T(8,128)(2,1)S(1)}, u32[]{:S(2)}, u32[]{:S(2)}) collective-permute-start(bf16[3,96,192]{2,1,0:T(8,128)(2,1)} %get-tuple-element.87), channel_id=1, source_target_pairs={{0,16},{8,24},{16,0},{24,8},{1,17},{9,25},{17,1},{25,9},{2,18},{10... | collective-permute-start | bytes 331784 | tf_op jit(solution)/shard_map/ppermute | solution.py:66
  313.5 14.0 %collective-permute-start.30 = (bf16[3,96,192]{2,1,0:T(8,128)(2,1)}, bf16[3,96,192]{2,1,0:T(8,128)(2,1)}, u32[]{:S(2)}, u32[]{:S(2)}) collective-permute-start(bf16[3,96,192]{2,1,0:T(8,128)(2,1)} %get-tuple-element.86), channel_id=1, source_target_pairs={{0,24},{8,0},{16,8},{24,16},{1,25},{9,1},{17,9},{25,17},{2,26},{10... | collective-permute-start | bytes 331784 | tf_op jit(solution)/shard_map/ppermute | solution.py:66
  (110 other events, 646.2 us)

commit v2 on v1

v2 whole, which is shorter than its diff:
```python
import math

import jax
import jax.numpy as jnp
from jax import lax
from jax.experimental import pallas as pl
from jax.experimental.pallas import tpu as pltpu
from jax.sharding import PartitionSpec as P

HD = 64
EPS = 1e-06
NEG = -1e30
F32 = jnp.float32
LOW = jnp.bfloat16
VMEM = pl.BlockSpec(memory_space=pltpu.VMEM)
SMEM = pl.BlockSpec(memory_space=pltpu.SMEM)


def shape(dims, dtype=LOW):
    return jax.ShapeDtypeStruct(dims, dtype)


def call(body, name, out, args, scalars=0, scratch=(), cost=None):
    return pl.pallas_call(
        body,
        name=name,
        out_shape=out,
        in_specs=[SMEM] * scalars + [VMEM] * (len(args) - scalars),
        out_specs=[VMEM] * len(out),
        scratch_shapes=list(scratch),
        compiler_params=pltpu.CompilerParams(vmem_limit_bytes=60 * 2**20),
        cost_estimate=cost,
    )(*args)


def cost(flops, moved, exps=0):
    return pl.CostEstimate(flops=flops, bytes_accessed=moved, transcendentals=exps)


def dot(left, right, left_dim=1, right_dim=0):
    return lax.dot_general(
        left, right, (((left_dim,), (right_dim,)), ((), ())), preferred_element_type=F32
    )


def norm_stats(values):
    centred = values - jnp.mean(values, axis=-1, keepdims=True)
    rate = lax.rsqrt(jnp.mean(centred * centred, axis=-1, keepdims=True) + EPS)
    return centred * rate, rate


def norm_back(grad, scaled, rate, gain):
    e = grad * gain
    inner = jnp.mean(e * scaled, axis=-1, keepdims=True)
    return rate * (e - jnp.mean(e, axis=-1, keepdims=True) - scaled * inner)


def own_other(counts):
    ctx = lax.axis_index("ctx")
    first, second = counts[0, 0], counts[0, 1]
    return jnp.where(ctx == 0, first, second), jnp.where(ctx == 0, second, first)


def wide(blocks):
    return jnp.concatenate(blocks, axis=1)


def to_chunks(value, ref):
    tp = lax.axis_index("tp")
    count, rows = ref.shape[0], ref.shape[1]
    for g in range(count):
        ref[tp ^ g] = value[g * rows : (g + 1) * rows].astype(ref.dtype)


def to_blocks(value, ref, row):
    n, _, part = ref.shape
    for g in range(n):
        ref[g, row : row + value.shape[0], :] = value[:, g * part : (g + 1) * part].astype(ref.dtype)


def pack_body(qkv, gains, biases, proj, up, down, first, rest, rest_half, down_half):
    ctx = lax.axis_index("ctx")
    heads_width = qkv.shape[2]
    part = qkv.shape[1]
    for k in range(3):
        first[k * heads_width : (k + 1) * heads_width, :] = qkv[k].T
    vectors = jnp.concatenate(
        [gains[...].astype(F32), biases[...].astype(F32), jnp.zeros((10, part), F32)], axis=0
    )
    first[3 * heads_width :, :] = vectors.astype(LOW)
    rest[:heads_width, :] = proj[...]
    rest[heads_width:, :] = up[...].T
    size = rest_half.shape[0]
    rest_half[...] = rest[pl.ds(pl.multiple_of(ctx * size, 16), size), :]
    size = down_half.shape[0]
    down_half[...] = down[pl.ds(pl.multiple_of(ctx * size, 16), size), :]


def assemble(own, pairs, middle, held):
    n, rows, _ = held.shape
    shard, ctx = lax.axis_index("shard"), lax.axis_index("ctx")
    held[shard] = own[...]
    for k, (mine, other) in enumerate(pairs, 1):
        step = jnp.where(ctx == 0, n - k, k)
        held[(shard + step) % n] = mine[...]
        held[(shard + n - step) % n] = other[...]
    if middle:
        far = (shard + n // 2) % n
        size = rows // 2
        held[far, pl.ds(pl.multiple_of(ctx * size, 16), size), :] = middle[0][...]
        held[far, pl.ds(pl.multiple_of((1 - ctx) * size, 16), size), :] = middle[1][...]


def assemble_body(splits, n, *refs):
    outs, held = refs[-1 - len(splits) : -1], refs[-1]
    ins = refs[: -1 - len(splits)]
    count = (n - 1) // 2
    pairs = [(ins[1 + 2 * i], ins[2 + 2 * i]) for i in range(count)]
    assemble(ins[0], pairs, ins[1 + 2 * count :], held)
    row = 0
    for size, out in zip(splits, outs):
        out[...] = wide([held[g, row : row + size, :] for g in range(n)])
        row += size


def attend_body(
    counts, act, other, first, biases, mixed_out, turned_out, scale_out, normed_own,
    normed_other, q_out, k_out, v_out, e_out, w_out,
):
    n = first.shape[0]
    slots = act.shape[0]
    hw = biases.shape[1]
    weights = wide([first[g] for g in range(n)])
    w_out[...] = weights
    vectors = weights[3 * hw :].astype(F32)
    bias = biases[...].astype(F32)
    for src, dst in ((act, normed_own), (other, normed_other)):
        scaled, _ = norm_stats(src[...].astype(F32))
        dst[...] = (scaled * vectors[0:1] + vectors[2:3]).astype(LOW)
    queries = (dot(normed_own[...], weights[:hw], 1, 1) + bias[0:1]).astype(LOW)
    q_out[...] = (queries.astype(F32) * (1.0 / math.sqrt(HD))).astype(LOW)
    for i, src in enumerate((normed_own, normed_other)):
        both = dot(src[...], weights[hw : 3 * hw], 1, 1)
        k_out[i] = both[:, :hw].astype(LOW)
        v_out[i] = (both[:, hw:] + bias[1:2]).astype(LOW)
    ids = lax.broadcasted_iota(jnp.int32, (slots, 1), 0)
    outs, scales = [], []
    for h in range(hw // HD):
        cols = slice(h * HD, (h + 1) * HD)
        query = q_out[:, cols]
        scores = [
            jnp.where(ids < count, dot(k_out[i][:, cols], query, 1, 1), NEG)
            for i, count in enumerate(own_other(counts))
        ]
        peak = jnp.maximum(*[jnp.max(s, axis=0, keepdims=True) for s in scores])
        mixed, total = 0.0, 0.0
        for i in range(2):
            e = jnp.exp(scores[i] - peak)
            total = total + jnp.sum(e, axis=0, keepdims=True)
            e_out[h, i] = e.astype(LOW)
            mixed = mixed + dot(v_out[i][:, cols], e_out[h, i], 0, 0)
        scales.append(1.0 / total)
        outs.append(mixed * scales[-1])
    turned = jnp.concatenate(outs, axis=0)
    turned_out[...] = turned
    mixed_out[...] = turned.T.astype(LOW)
    scales.append(jnp.zeros((8 - len(scales), slots), F32))
    scale_out[...] = jnp.concatenate(scales, axis=0).T


def middle_body(
    counts, act, mixed0, mixed1, mixed2, mixed3, proj0, proj1, proj2, proj3, weights, up, down,
    hidden_bias, cot, back0, back1, back2, back3, two_out, gelu_out, hidden_out, branch_out,
    low_out, middle_out, sums,
):
    slots = act.shape[0]
    vectors = weights[weights.shape[0] - 16 :, :].astype(F32)
    own, _ = own_other(counts)
    valid = lax.broadcasted_iota(jnp.int32, (slots, 1), 0) < own
    branch = jnp.where(valid, cot[...].astype(F32), 0.0)
    branch_low = branch.astype(LOW)
    branch_out[...] = branch_low
    projs = (proj0, proj1, proj2, proj3)
    middle = act[...].astype(F32) + vectors[4:5]
    for mixed, proj in zip((mixed0, mixed1, mixed2, mixed3), projs):
        middle = middle + dot(mixed[...], proj[...])
    middle_out[...] = middle
    scaled, rate = norm_stats(middle)
    two = (scaled * vectors[1:2] + vectors[3:4]).astype(LOW)
    two_out[...] = two
    hidden = dot(two, up[...], 1, 1) + hidden_bias[...].astype(F32)
    share = 0.5 * (1.0 + lax.erf(hidden * math.sqrt(0.5)))
    gelu_out[...] = (hidden * share).astype(LOW)
    slope = share + hidden * (jnp.exp(hidden * hidden * -0.5) * (1.0 / math.sqrt(2.0 * math.pi)))
    grad_hidden = (dot(branch_low, down[...], 1, 1) * slope).astype(LOW)
    hidden_out[...] = grad_hidden
    grad_two = dot(grad_hidden, up[...])
    back = norm_back(grad_two, scaled, rate, vectors[1:2])
    low = back.astype(LOW)
    low_out[...] = low
    back0[...] = dot(low, proj0[...], 1, 1) + dot(branch_low, proj0[...], 1, 1)
    for proj, out in zip(projs[1:], (back1, back2, back3)):
        out[...] = dot(low, proj[...], 1, 1).astype(LOW)
    first_tp = jnp.where(lax.axis_index("tp") == 0, 1.0, 0.0)
    branch_sum = jnp.sum(branch, axis=0, keepdims=True) * first_tp
    sums[...] = jnp.concatenate(
        [
            jnp.sum(grad_two * scaled, axis=0, keepdims=True),
            jnp.sum(grad_two, axis=0, keepdims=True),
            branch_sum + jnp.sum(back, axis=0, keepdims=True),
            branch_sum,
            jnp.sum(grad_hidden.astype(F32), axis=0, keepdims=True),
            jnp.zeros((3, sums.shape[1]), F32),
        ],
        axis=0,
    )


def ffn_grads_body(
    two, gelu, hidden, branch, low, middle, down, near, keep, own_middle, own_branch, sent, kept,
    chunks,
):
    ctx = lax.axis_index("ctx")
    to_chunks(dot(gelu[...], down[...]), chunks)
    near[0] = chunks[1].astype(LOW)
    near[1] = chunks[3].astype(LOW)
    keep[0] = chunks[0]
    keep[2] = chunks[2]
    to_chunks(low[...].astype(F32), chunks)
    near[2] = chunks[1].astype(LOW)
    near[3] = chunks[3].astype(LOW)
    keep[1] = chunks[0]
    keep[3] = chunks[2]
    to_chunks(middle[...], chunks)
    own_middle[...] = chunks[0]
    to_chunks(branch[...].astype(F32), chunks)
    own_branch[...] = chunks[0]
    down_grad = dot(gelu[...], branch[...], 0, 0)
    up_grad = dot(hidden[...], two[...], 0, 0)

    @pl.when(ctx == 0)
    def _():
        to_blocks(down_grad, kept, 0)
        to_blocks(up_grad, sent, 0)

    @pl.when(ctx == 1)
    def _():
        to_blocks(up_grad, kept, 0)
        to_blocks(down_grad, sent, 0)


def attend_back_body(
    back0, back1, back2, q, k, v, e, scales, turned, weights, act, other, sums_in,
    gq_out, gk_out, gv_out, near, keep, own_act, sums, chunks,
):
    hw = q.shape[1]
    grad_mixed = (back0[...] + back1[...].astype(F32) + back2[...].astype(F32)).astype(LOW)
    grad_mixed = grad_mixed.astype(F32)
    scaled_grads = [
        grad_mixed[:, h * HD : (h + 1) * HD] * scales[:, h : h + 1] for h in range(hw // HD)
    ]
    scaled_grad = wide(scaled_grads)
    inner = scaled_grad.T * turned[...]
    scaled_low = scaled_grad.astype(LOW)
    scale = 1.0 / math.sqrt(HD)
    gq, gk, gv = [], ([], []), ([], [])
    for h in range(hw // HD):
        cols = slice(h * HD, (h + 1) * HD)
        grad = scaled_low[:, cols]
        row = jnp.sum(inner[cols], axis=0, keepdims=True)
        gq_head = 0.0
        for i in range(2):
            gv[i].append(dot(e[h, i], grad))
            probs_grad = dot(v[i][:, cols], grad, 1, 1)
            scores_grad = (e[h, i].astype(F32) * (probs_grad - row)).astype(LOW)
            gk[i].append(dot(scores_grad, q[:, cols]))
            gq_head = gq_head + dot(k[i][:, cols], scores_grad, 0, 0)
        gq.append(gq_head * scale)
    gq_low = jnp.concatenate(gq, axis=0).astype(LOW)
    gq_out[...] = gq_low
    for i in range(2):
        gk_out[i] = wide(gk[i]).astype(LOW)
        gv_out[i] = wide(gv[i]).astype(LOW)
    gain_sum, shift_sum = 0.0, 0.0
    for i, src in enumerate((act, other)):
        grad = dot(gk_out[i], weights[hw : 2 * hw]) + dot(gv_out[i], weights[2 * hw : 3 * hw])
        if i == 0:
            grad = grad + dot(gq_low, weights[:hw], 0, 0)
        scaled, _ = norm_stats(src[...].astype(F32))
        gain_sum = gain_sum + jnp.sum(grad * scaled, axis=0, keepdims=True)
        shift_sum = shift_sum + jnp.sum(grad, axis=0, keepdims=True)
        to_chunks(grad, chunks)
        near[2 * i] = chunks[1].astype(LOW)
        near[2 * i + 1] = chunks[3].astype(LOW)
        keep[2 * i] = chunks[0]
        keep[2 * i + 1] = chunks[2]
    to_chunks(act[...].astype(F32), chunks)
    own_act[...] = chunks[0]
    ones = jnp.ones((8, q.shape[0]), LOW)
    head_q = dot(ones, gq_low, 1, 1)[0:1]
    head_v = (dot(ones, gv_out[0]) + dot(ones, gv_out[1]))[0:1]
    pad = jnp.zeros((1, sums.shape[1] - 2 * hw), F32)
    sums[...] = jnp.concatenate(
        [
            gain_sum,
            sums_in[0:1],
            shift_sum,
            sums_in[1:2],
            sums_in[2:3],
            sums_in[3:4],
            sums_in[4:5],
            wide([head_q, head_v, pad]),
        ],
        axis=0,
    )


def head_grads_body(
    gq, gk, gv, normed_own, normed_other, mixed, attn0, attn1, attn2, attn3, sent, kept, chunks
):
    ctx = lax.axis_index("ctx")
    hw = mixed.shape[1]
    to_chunks(mixed[...].astype(F32), chunks)
    proj_grad = 0.0
    for j, attn in enumerate((attn0, attn1, attn2, attn3)):
        proj_grad = proj_grad + dot(chunks[j].astype(LOW), attn[...], 0, 0)
    q_grad = dot(gq[...], normed_own[...])
    k_grad = dot(gk[0], normed_own[...], 0, 0) + dot(gk[1], normed_other[...], 0, 0)
    v_grad = dot(gv[0], normed_own[...], 0, 0) + dot(gv[1], normed_other[...], 0, 0)

    def fill(here, there):
        to_blocks(proj_grad, here, 0)
        to_blocks(q_grad, here, hw)
        to_blocks(k_grad, there, 0)
        to_blocks(v_grad, there, hw)

    @pl.when(ctx == 0)
    def _():
        fill(kept, sent)

    @pl.when(ctx == 1)
    def _():
        fill(sent, kept)


def fold_body(kept, got, own, *outs):
    n = kept.shape[0]
    shard = lax.axis_index("shard")
    own[...] = kept[shard] + got[shard].astype(F32)
    for k, out in enumerate(outs, 1):
        owner = (shard + k) % n
        out[...] = (kept[owner] + got[owner].astype(F32)).astype(LOW)


def total_body(own, *refs):
    got, total, low = refs[:-2], refs[-2], refs[-1]
    value = own[...]
    for ref in got:
        value = value + ref[...].astype(F32)
    total[...] = value
    low[...] = value.astype(LOW)


def ffn_finish_body(mine, other, up_grad, down_grad):
    first = lax.axis_index("ctx") == 0
    theirs = other[...].astype(F32)
    down_grad[...] = jnp.where(first, mine[...], theirs)
    up_grad[...] = jnp.where(first, theirs, mine[...]).T


def head_finish_body(mine, other, qkv_grad, proj_grad):
    first = lax.axis_index("ctx") == 0
    theirs = other[...].astype(F32)
    early = jnp.where(first, mine[...], theirs)
    late = jnp.where(first, theirs, mine[...])
    hw = proj_grad.shape[0]
    proj_grad[...] = early[:hw]
    qkv_grad[0] = early[hw:].T
    qkv_grad[1] = late[:hw].T
    qkv_grad[2] = late[hw:].T


def rows_body(counts, keep, near, far, own_middle, own_branch, weights, layer_out, middle_grad, attn):
    vectors = weights[weights.shape[0] - 16 :, :].astype(F32)
    own, _ = own_other(counts)
    rows = layer_out.shape[0]
    ids = lax.broadcasted_iota(jnp.int32, (rows, 1), 0) + lax.axis_index("tp") * rows
    mlp = keep[0] + near[0].astype(F32) + far[0].astype(F32)
    value = own_middle[...] + mlp + vectors[5:6]
    layer_out[...] = jnp.where(ids < own, value, 0.0).astype(LOW)
    back = keep[1] + near[2].astype(F32) + far[1].astype(F32)
    grad = own_branch[...] + back
    middle_grad[...] = grad
    attn[...] = grad.astype(LOW)


def input_body(kept, near, from_tp, from_ctx, from_far, own_act, middle_grad, weights, out):
    vectors = weights[weights.shape[0] - 16 :, :].astype(F32)
    grad = kept[0] + near[0].astype(F32) + from_tp[...].astype(F32)
    grad = grad + from_ctx[...].astype(F32) + from_far[...].astype(F32)
    scaled, rate = norm_stats(own_act[...])
    out[...] = (middle_grad[...] + norm_back(grad, scaled, rate, vectors[0:1])).astype(LOW)


def per_device(
    activations,
    slot_counts,
    qkv_weight,
    proj_weight,
    up_weight,
    down_weight,
    norm_gains,
    row_biases,
    head_biases,
    hidden_bias,
    cotangent,
):
    images, slots, width = activations.shape
    n = lax.axis_size("shard")
    n_ctx = lax.axis_size("ctx")
    n_tp = lax.axis_size("tp")
    assert images == 1 and n_ctx == 2 and n_tp == 4 and n % 2 == 0
    part = width // n
    hw = qkv_weight.shape[2]
    ff = up_weight.shape[1]
    quarter = slots // n_tp

    def over_ctx(x):
        return lax.ppermute(x, "ctx", [(i, i ^ 1) for i in range(n_ctx)])

    def over_tp(x, bit):
        return lax.ppermute(x, "tp", [(i, i ^ bit) for i in range(n_tp)])

    def shift(x, k):
        return lax.ppermute(x, "shard", [(i, (i + k) % n) for i in range(n)])

    def shift_by_ctx(x, k):
        moves = [
            (i * n_ctx + r, ((i + (k if r == 0 else n - k)) % n) * n_ctx + r)
            for i in range(n)
            for r in range(n_ctx)
        ]
        return lax.ppermute(x, ("shard", "ctx"), moves)

    def fetch(pack, pack_half):
        mine = [shift_by_ctx(pack, k) for k in range(1, (n - 1) // 2 + 1)]
        middle = shift(pack_half, n // 2)
        pairs = [x for m in mine for x in (m, over_ctx(m))]
        return [pack] + pairs + [middle, over_ctx(middle)]

    def gather_body(splits):
        def body(*refs):
            assemble_body(splits, n, *refs)

        return body

    def spread_tp(x):
        far = over_tp(x, 2)
        return [x, over_tp(x, 1), far, over_tp(far, 1)]

    act = activations[0]
    other = over_ctx(act)
    first, rest, rest_half, down_half = call(
        pack_body,
        "pack",
        [
            shape((3 * hw + 16, part)),
            shape((hw + ff, part)),
            shape(((hw + ff) // 2, part)),
            shape((ff // 2, part)),
        ],
        [qkv_weight, norm_gains, row_biases, proj_weight, up_weight, down_weight],
    )
    first = lax.all_gather(first, "shard")
    rest_parts = fetch(rest, rest_half)
    down_parts = fetch(down_weight, down_half)

    heads = hw // HD
    (mixed, turned, scales, normed_own, normed_other, q, k, v, e, weights) = call(
        attend_body,
        "attend",
        [
            shape((slots, hw)),
            shape((hw, slots), F32),
            shape((slots, 8), F32),
            shape((slots, width)),
            shape((slots, width)),
            shape((slots, hw)),
            shape((2, slots, hw)),
            shape((2, slots, hw)),
            shape((heads, 2, slots, slots)),
            shape((3 * hw + 16, width)),
        ],
        [slot_counts, act, other, first, head_biases],
        scalars=1,
        cost=cost(3_000_000_000, 12_000_000, 2_000_000),
    )
    proj, up = call(
        gather_body((hw, ff)),
        "join",
        [shape((hw, width)), shape((ff, width))],
        rest_parts,
        scratch=[pltpu.VMEM((n, hw + ff, part), LOW)],
    )
    (down,) = call(
        gather_body((ff,)),
        "join_down",
        [shape((ff, width))],
        down_parts,
        scratch=[pltpu.VMEM((n, ff, part), LOW)],
    )
    projs = spread_tp(proj)
    mixes = spread_tp(mixed)
    back0, back1, back2, back3, two, gelu, hidden, branch, low, middle, sums = call(
        middle_body,
        "middle",
        [shape((slots, hw), F32)]
        + [shape((slots, hw))] * 3
        + [shape((slots, width)), shape((slots, ff)), shape((slots, ff))]
        + [shape((slots, width))] * 2
        + [shape((slots, width), F32), shape((8, width), F32)],
        [slot_counts, act, *mixes, *projs, weights, up, down, hidden_bias.reshape(1, ff)]
        + [cotangent[0]],
        scalars=1,
        cost=cost(4_000_000_000, 16_000_000, 1_000_000),
    )
    back1 = over_tp(back1, 1)
    back2 = (back2.astype(F32) + over_tp(back3, 1).astype(F32)).astype(LOW)
    back2 = over_tp(back2, 2)
    near, keep, own_middle, own_branch, sent, kept = call(
        ffn_grads_body,
        "ffn_grads",
        [
            shape((4, quarter, width)),
            shape((4, quarter, width), F32),
            shape((quarter, width), F32),
            shape((quarter, width), F32),
            shape((n, ff, part)),
            shape((n, ff, part), F32),
        ],
        [two, gelu, hidden, branch, low, middle, down],
        scratch=[pltpu.VMEM((n_tp, quarter, width), F32)],
        cost=cost(2_000_000_000, 14_000_000),
    )

    def owned(sent, kept):
        rows = kept.shape[1]
        own, *outs = call(
            fold_body,
            "fold",
            [shape((rows, part), F32)] + [shape((rows, part))] * (n - 1),
            [kept, over_ctx(sent)],
        )
        got = [shift(x, k) for k, x in enumerate(outs, 1)]
        total, low = call(
            total_body, "total", [shape((rows, part), F32), shape((rows, part))], [own, *got]
        )
        return [total, over_ctx(low)]

    ffn_totals = owned(sent, kept)
    near = over_tp(near, 1)
    far = jnp.stack(
        [
            (keep[2] + near[1].astype(F32)).astype(LOW),
            (keep[3] + near[3].astype(F32)).astype(LOW),
        ]
    )
    far = over_tp(far, 2)
    layer_out, middle_grad, attn = call(
        rows_body,
        "rows",
        [shape((quarter, width)), shape((quarter, width), F32), shape((quarter, width))],
        [slot_counts, keep, near, far, own_middle, own_branch, weights],
        scalars=1,
    )
    attns = spread_tp(attn)

    gq, gk, gv, near, keep, own_act, sums = call(
        attend_back_body,
        "attend_back",
        [
            shape((hw, slots)),
            shape((2, slots, hw)),
            shape((2, slots, hw)),
            shape((4, quarter, width)),
            shape((4, quarter, width), F32),
            shape((quarter, width), F32),
            shape((8, width), F32),
        ],
        [back0, back1, back2, q, k, v, e, scales, turned, weights, act, other, sums],
        scratch=[pltpu.VMEM((n_tp, quarter, width), F32)],
        cost=cost(4_000_000_000, 16_000_000),
    )
    near = over_tp(near, 1)
    sent, kept = call(
        head_grads_body,
        "head_grads",
        [shape((n, 2 * hw, part)), shape((n, 2 * hw, part), F32)],
        [gq, gk, gv, normed_own, normed_other, mixed, *attns],
        scratch=[pltpu.VMEM((n_tp, quarter, hw), F32)],
        cost=cost(1_000_000_000, 6_000_000),
    )
    head_totals = owned(sent, kept)
    from_tp = over_tp((keep[1] + near[1].astype(F32)).astype(LOW), 2)
    from_ctx = over_ctx((keep[2] + near[2].astype(F32)).astype(LOW))
    pairs = [(i, i ^ (n_tp + 2)) for i in range(n_ctx * n_tp)]
    from_far = (keep[3] + near[3].astype(F32)).astype(LOW)
    from_far = lax.ppermute(from_far, ("ctx", "tp"), pairs)
    (input_grad,) = call(
        input_body,
        "input",
        [shape((quarter, width))],
        [keep, near, from_tp, from_ctx, from_far, own_act, middle_grad, weights],
    )
    up_grad, down_grad = call(
        ffn_finish_body, "ffn_finish", [shape((part, ff), F32), shape((ff, part), F32)], ffn_totals
    )
    qkv_grad, proj_grad = call(
        head_finish_body,
        "head_finish",
        [shape((3, part, hw), F32), shape((hw, part), F32)],
        head_totals,
    )

    shared = sums[:6]
    for bit in (1, 2):
        shared = shared + over_tp(shared, bit)
    sums = jnp.concatenate([shared, sums[6:]])
    sums = sums + over_ctx(sums)
    bit = 1
    while bit < n:
        sums = sums + lax.ppermute(sums, "shard", [(i, i ^ bit) for i in range(n)])
        bit *= 2
    vector_grads = lax.dynamic_slice_in_dim(sums[:6], lax.axis_index("shard") * part, part, 1)
    return (
        layer_out[None],
        input_grad[None],
        qkv_grad,
        proj_grad,
        up_grad,
        down_grad,
        vector_grads[:2],
        vector_grads[2:],
        sums[7, : 2 * hw].reshape(2, hw),
        sums[6],
    )


def solution(mesh):
    placed = (
        P("shard", "ctx", None),
        P("shard", None),
        P(None, "shard", "tp"),
        P("tp", "shard"),
        P("shard", "tp"),
        P("tp", "shard"),
        P(None, "shard"),
        P(None, "shard"),
        P(None, "tp"),
        P("tp"),
        P("shard", "ctx", None),
    )
    return jax.shard_map(
        per_device,
        mesh=mesh,
        in_specs=placed,
        out_specs=(
            P("shard", ("ctx", "tp"), None),
            P("shard", ("ctx", "tp"), None),
            P(None, "shard", "tp"),
            P("tp", "shard"),
            P("shard", "tp"),
            P("tp", "shard"),
            P(None, "shard"),
            P(None, "shard"),
            P(None, "tp"),
            P("tp"),
        ),
        check_vma=False,
    )
```

time: 349 us -> 269 us (0.77)
  Pallas kernels: 0 us -> 79.9 us
  other arithmetic: 64.9 us -> 1.89 us
  matrix products: 43.9 us -> 0 us
  local copies, waits for them, and re-layouts: 71.8 us -> 29.3 us
  starting transfers between devices: 61.7 us -> 50.5 us
  waiting for transfers between devices: 74.9 us -> 82.2 us
  between operations: 4.82 us -> 1.02 us
    pallas_call x0 -> x16, Pallas kernels: none -> 79.9 us  [call(): pl.pallas_call(body, name=name, out_shape=out, in_specs=[SMEM] * scalars...]
    ppermute x24 -> x13, waiting for transfers between devices: 24.3 us -> 63.5 us  [the longest x8 46 us: shift(): return lax.ppermute(x, 'shard', [(i, (i + k) % n) for i in range(n)])]
    dot_general x24 -> x0, matrix products: 37.5 us -> none  [the longest x19 31.9 us: dot(): lax.dot_general(left, right, (((left_dim,), (right_dim,)), ((), ())), pre...]
    ppermute x14 -> x11, waiting for transfers between devices: 40.2 us -> 7.55 us  [over_ctx(): return lax.ppermute(x, 'ctx', [(i, i ^ 1) for i in range(n_ctx)])]
    convert_element_type x22 -> x3, other arithmetic: 24.9 us -> 0.29 us  [the longest x1 0.12 us: per_device(): from_far = (keep[3] + near[3].astype(F32)).astype(LOW)]
    another operation x13 -> x1, other arithmetic: 11.6 us -> 0.82 us  [per_device(): jnp.stack([(keep[2] + near[1].astype(F32)).astype(LOW), (keep[3] + near[3...]
    reduce_sum x12 -> x0, other arithmetic: 9.12 us -> none  [the longest x1 3.3 us: per_device(): jnp.sum(back_two, axis=0)]
    reshape x9 -> x1, local copies, waits for them, and re-layouts: 9.12 us -> 0.58 us  [per_device(): hidden_bias.reshape(1, ff)]
  transfers between devices with their start and end apart: 54 -> 42, of which waited for: 21 -> 14; matrix products, arithmetic and copies ran while one was open for 41% -> 8% of each run, Pallas kernels for 0% -> 21%
where the time goes in v2:
time: 269 us; the launch traced here: 267 us
  waiting for transfers between devices  82.2 us (31%)
  Pallas kernels  79.9 us (30%)
  starting transfers between devices  50.5 us (19%)
  local copies, waits for them, and re-layouts  29.3 us (11%)
  blocking collectives  22.3 us (8%)
    pallas_call x16, Pallas kernels, call(): pl.pallas_call(body, name=name, out_shape=out, in_specs=[SMEM] * scalars...  79.9 us
    ppermute x8, waiting for transfers between devices, shift(): return lax.ppermute(x, 'shard', [(i, (i + k) % n) for i in range(n)])  46 us
    all_gather x1, blocking collectives, per_device(): first = lax.all_gather(first, 'shard')  22.3 us
    ppermute x8, starting transfers between devices, shift(): return lax.ppermute(x, 'shard', [(i, (i + k) % n) for i in range(n)])  19.4 us
    unnamed x79, local copies, waits for them, and re-layouts  12.9 us
    ppermute x11, starting transfers between devices, over_ctx(): return lax.ppermute(x, 'ctx', [(i, i ^ 1) for i in range(n_ctx)])  12.8 us
    ppermute x2, waiting for transfers between devices, shift_by_ctx(): return lax.ppermute(x, ('shard', 'ctx'), moves)  12.1 us
    ppermute x18, waiting for transfers between devices, over_tp(): return lax.ppermute(x, 'tp', [(i, i ^ bit) for i in range(n_tp)])  11.2 us
  transfers between devices with their start and end apart: 42, of which 14 were waited for; matrix products, arithmetic and copies ran while one was open for 8% of the time, Pallas kernels for 21%

profile of v2, /device:TPU:0, one launch (start us, length us, event | category | flops | bytes accessed | tf_op | source)
XLA Modules:
  0.0 267.2 jit_solution(3514171967076251569)
XLA Ops:
  0.6 3.0 %collective-permute-start = (bf16[520,768]{1,0:T(8,128)(2,1)}, bf16[520,768]{1,0:T(8,128)(2,1)}, u32[]{:S(2)}, u32[]{:S(2)}) collective-permute-start(bf16[520,768]{1,0:T(8,128)(2,1)} %bitcast.19), channel_id=1, source_target_pairs={{0,4},{4,0},{1,5},{5,1},{2,6},{6,2},{3,7},{7,3},{8,12},{12,8},{9,1... | collective-permute-start | bytes 2396168 | tf_op jit(solution)/shard_map/ppermute | solution.py:429
  12.2 12.1 %collective-permute-done.4.refs_1_ = bf16[960,192]{1,0:T(8,128)(2,1)S(1)} collective-permute-done((bf16[960,192]{1,0:T(8,128)(2,1)}, bf16[960,192]{1,0:T(8,128)(2,1)S(1)}, u32[]{:S(2)}, u32[]{:S(2)}) %collective-permute-start.4) | collective-permute-done | bytes 368672 | tf_op jit(solution)/shard_map/ppermute | solution.py:443
  24.3 4.4 %collective-permute-start.11 = (bf16[768,192]{1,0:T(8,128)(2,1)}, bf16[768,192]{1,0:T(8,128)(2,1)S(1)}, u32[]{:S(2)}, u32[]{:S(2)}) collective-permute-start(bf16[768,192]{1,0:T(8,128)(2,1)} %copy.25.down.refs_0_), channel_id=1, source_target_pairs={{0,8},{4,28},{8,16},{12,4},{16,24},{20,12},{24,0},{28,20},{1,9},{5... | collective-permute-start | bytes 884744 | tf_op jit(solution)/shard_map/ppermute | solution.py:443
  31.4 14.6 %collective-permute-done.6.refs_3_ = bf16[480,192]{1,0:T(8,128)(2,1)S(1)} collective-permute-done((bf16[480,192]{1,0:T(8,128)(2,1)}, bf16[480,192]{1,0:T(8,128)(2,1)S(1)}, u32[]{:S(2)}, u32[]{:S(2)}) %collective-permute-start.6) | collective-permute-done | bytes 184352 | tf_op jit(solution)/shard_map/ppermute | solution.py:435
  46.0 22.3 %all-gather.1 = bf16[4,592,192]{1,2,0:T(8,128)(2,1)S(1)} all-gather(bf16[1,592,192]{1,2,0:T(8,128)(2,1)S(1)} %copy.26), channel_id=2, replica_groups=mesh['shard'=4,'ctx'=2,'tp'=4] {'shard'}, dimensions={0}, use_global_device_ids=true | all-gather | bytes 1136640 | tf_op jit(solution)/shard_map/all_gather | solution.py:474
  71.3 3.0 %join.1 = (bf16[192,768]{1,0:T(8,128)(2,1)}, bf16[768,768]{1,0:T(8,128)(2,1)}) custom-call(bf16[960,192]{1,0:T(8,128)(2,1)} %get-tuple-element.73.refs_0_, bf16[960,192]{1,0:T(8,128)(2,1)} %copy-done.5, bf16[960,192]{1,0:T(8,128)(2,1)} %copy-done.6, bf16[480,192]{1,0:T(8,128)(2,1)} %copy-done.15, bf16[480,192]{1,0:T(8,128)(2,1)} %copy-done.16), custom_call_target="tpu_custom_call" | custom-call | tf_op jit(solution)/shard_map/join/pallas_call | solution.py:24
  75.7 10.6 %attend.1 = (bf16[520,192]{1,0:T(8,128)(2,1)}, f32[192,520]{1,0:T(8,128)}, f32[520,8]{1,0:T(8,128)}, bf16[520,768]{1,0:T(8,128)(2,1)}, bf16[520,768]{1,0:T(8,128...) custom-call(s32[1,2]{1,0:T(1,128)} %counts.5, ...), custom_call_target="tpu_custom_call" | custom-call | flops 3000000000 | bytes 12000000 | tf_op jit(solution)/shard_map/attend/pallas_call | solution.py:24
  89.4 4.4 %collective-permute-done.14.refs_4_ = bf16[384,192]{1,0:T(8,128)(2,1)S(1)} collective-permute-done((bf16[384,192]{1,0:T(8,128)(2,1)S(1)}, bf16[384,192]{1,0:T(8,128)(2,1)S(1)}, u32[]{:S(2)}, u32[]{:S(2)}) %collective-permute-start.14) | collective-permute-done | bytes 147488 | tf_op jit(solution)/shard_map/ppermute | solution.py:429
  94.9 3.1 %collective-permute-done.12.refs_2_ = bf16[768,192]{1,0:T(8,128)(2,1)S(1)} collective-permute-done((bf16[768,192]{1,0:T(8,128)(2,1)S(1)}, bf16[768,192]{1,0:T(8,128)(2,1)S(1)}, u32[]{:S(2)}, u32[]{:S(2)}) %collective-permute-start.12) | collective-permute-done | bytes 294944 | tf_op jit(solution)/shard_map/ppermute | solution.py:429
  102.6 10.0 %middle.1 = (f32[520,192]{1,0:T(8,128)}, bf16[520,192]{1,0:T(8,128)(2,1)}, bf16[520,192]{1,0:T(8,128)(2,1)}, bf16[520,192]{1,0:T(8,128)(2,1)}, bf16[520,768]{1,0...) custom-call(s32[1,2]{1,0:T(1,128)} %counts.5, ...), custom_call_target="tpu_custom_call" | custom-call | flops 4000000000 | bytes 16000000 | tf_op jit(solution)/shard_map/middle/pallas_call | solution.py:24
  112.6 10.5 %ffn_grads.1 = (bf16[4,130,768]{2,1,0:T(8,128)(2,1)}, f32[4,130,768]{2,1,0:T(8,128)}, f32[130,768]{1,0:T(8,128)}, f32[130,768]{1,0:T(8,128)}, bf16[4,768,192]{2,1,0:T(8,128)(2,1)}, /*index=5*/f32[4,768,192]{2,1,0:T(8,128)}) custom-call(bf16[520,768]{1,0:T(8,128)(2,1)} %get-tuple-element.79.two, bf16[520,768]{1,0:T(8,128)(2,1)} %get-tuple-element.80.gelu, ...), custom_call_target="tpu_custom_call" | custom-call | flops 2000000000 | bytes 14000000 | tf_op jit(solution)/shard_map/ffn_grads/pallas_call | solution.py:24
  132.8 8.0 %collective-permute-done.16.far = bf16[2,130,768]{2,1,0:T(8,128)(2,1)S(1)} collective-permute-done((bf16[2,130,768]{2,1,0:T(8,128)(2,1)}, bf16[2,130,768]{2,1,0:T(8,128)(2,1)S(1)}, u32[]{:S(2)}, u32[]{:S(2)}) %collective-permute-start.16) | collective-permute-done | bytes 399392 | tf_op jit(solution)/shard_map/ppermute | solution.py:432
  141.6 3.3 %rows.1 = (bf16[130,768]{1,0:T(8,128)(2,1)}, f32[130,768]{1,0:T(8,128)}, bf16[130,768]{1,0:T(8,128)(2,1)}) custom-call(s32[1,2]{1,0:T(1,128)} %counts.5, f32[4,130,768]{2,1,0:T(8,128)} %get-tuple-element.85.keep, bf16[4,130,768]{2,1,0:T(8,128)(2,1)} %copy-done.1, bf16[2,130,768]{2,1,0:T(8,128)(2,1)} %copy-done.7, f32[130,768]{1,0:T(8,128)} %get-tuple-element.87.own_middle, ...), custom_call_target="tpu_custom_call" | custom-call | tf_op jit(solution)/shard_map/rows/pallas_call | solution.py:24
  146.4 12.5 %attend_back.1 = (bf16[192,520]{1,0:T(8,128)(2,1)}, bf16[2,520,192]{2,1,0:T(8,128)(2,1)}, bf16[2,520,192]{2,1,0:T(8,128)(2,1)}, bf16[4,130,768]{2,1,0:T(8,128)(2...) custom-call(f32[520,192]{1,0:T(8,128)} %get-tuple-element.90.back0, ...), custom_call_target="tpu_custom_call" | custom-call | flops 4000000000 | bytes 16000000 | tf_op jit(solution)/shard_map/attend_back/pallas_call | solution.py:24
  167.5 5.6 %head_grads.1 = (bf16[4,384,192]{2,1,0:T(8,128)(2,1)}, f32[4,384,192]{2,1,0:T(8,128)}) custom-call(bf16[192,520]{1,0:T(8,128)(2,1)} %get-tuple-element.105.gq, bf16[2,520,192]{2,1,0:T(8,128)(2,1)} %get-tuple-element.106.gk, bf16[2,520,192]{2,1,0:T(8,128)(2,1)} %get-tuple-element.107.gv, bf16[520,768]{1,0:T(8,128)(2,1)} %get-tuple-element.108.normed_own, ...), custom_call_target="tpu_custom_call" | custom-call | flops 1000000000 | bytes 6000000 | tf_op jit(solution)/shard_map/head_grads/pallas_call | solution.py:24
  175.7 3.8 %collective-permute-done.40 = f32[8,768]{1,0:T(8,128)S(1)} collective-permute-done((f32[8,768]{1,0:T(8,128)S(1)}, f32[8,768]{1,0:T(8,128)S(1)}, u32[]{:S(2)}, u32[]{:S(2)}) %collective-permute-start.40) | collective-permute-done | bytes 24608 | tf_op jit(solution)/shard_map/ppermute | solution.py:632
  182.3 3.8 %fold.3 = (f32[768,192]{1,0:T(8,128)}, bf16[768,192]{1,0:T(8,128)(2,1)}, bf16[768,192]{1,0:T(8,128)(2,1)}, bf16[768,192]{1,0:T(8,128)(2,1)}) custom-call(f32[4,768,192]{2,1,0:T(8,128)} %get-tuple-element.121.kept, bf16[4,768,192]{2,1,0:T(8,128)(2,1)} %copy.42.got), custom_call_target="tpu_custom_call" | custom-call | tf_op jit(solution)/shard_map/fold/pallas_call | solution.py:24
  187.9 2.9 %collective-permute-start.35 = (bf16[768,192]{1,0:T(8,128)(2,1)}, bf16[768,192]{1,0:T(8,128)(2,1)S(1)}, u32[]{:S(2)}, u32[]{:S(2)}) collective-permute-start(bf16[768,192]{1,0:T(8,128)(2,1)} %get-tuple-element.126), channel_id=1, source_target_pairs={{0,24},{8,0},{16,8},{24,16},{1,25},{9,1},{17,9},{25,17},{2,26},{10... | collective-permute-start | bytes 884744 | tf_op jit(solution)/shard_map/ppermute | solution.py:435
  192.0 8.2 %collective-permute-done.33.refs_0_ = bf16[768,192]{1,0:T(8,128)(2,1)S(1)} collective-permute-done((bf16[768,192]{1,0:T(8,128)(2,1)}, bf16[768,192]{1,0:T(8,128)(2,1)S(1)}, u32[]{:S(2)}, u32[]{:S(2)}) %collective-permute-start.33) | collective-permute-done | bytes 294944 | tf_op jit(solution)/shard_map/ppermute | solution.py:435
  200.3 13.9 %collective-permute-done.34.refs_1_ = bf16[768,192]{1,0:T(8,128)(2,1)S(1)} collective-permute-done((bf16[768,192]{1,0:T(8,128)(2,1)}, bf16[768,192]{1,0:T(8,128)(2,1)S(1)}, u32[]{:S(2)}, u32[]{:S(2)}) %collective-permute-start.34) | collective-permute-done | bytes 294944 | tf_op jit(solution)/shard_map/ppermute | solution.py:435
  224.7 8.2 %collective-permute-start.28 = (bf16[384,192]{1,0:T(8,128)(2,1)}, bf16[384,192]{1,0:T(8,128)(2,1)S(1)}, u32[]{:S(2)}, u32[]{:S(2)}) collective-permute-start(bf16[384,192]{1,0:T(8,128)(2,1)} %get-tuple-element.114), channel_id=1, source_target_pairs={{0,8},{8,16},{16,24},{24,0},{1,9},{9,17},{17,25},{25,1},{2,10},{10... | collective-permute-start | bytes 442376 | tf_op jit(solution)/shard_map/ppermute | solution.py:435
  236.6 3.2 %collective-permute-done.28.refs_0_ = bf16[384,192]{1,0:T(8,128)(2,1)S(1)} collective-permute-done((bf16[384,192]{1,0:T(8,128)(2,1)}, bf16[384,192]{1,0:T(8,128)(2,1)S(1)}, u32[]{:S(2)}, u32[]{:S(2)}) %collective-permute-start.28) | collective-permute-done | bytes 147488 | tf_op jit(solution)/shard_map/ppermute | solution.py:435
  239.9 6.0 %collective-permute-done.29.refs_1_ = bf16[384,192]{1,0:T(8,128)(2,1)S(1)} collective-permute-done((bf16[384,192]{1,0:T(8,128)(2,1)}, bf16[384,192]{1,0:T(8,128)(2,1)S(1)}, u32[]{:S(2)}, u32[]{:S(2)}) %collective-permute-start.29) | collective-permute-done | bytes 147488 | tf_op jit(solution)/shard_map/ppermute | solution.py:435
  255.5 3.5 %input.1 = bf16[130,768]{1,0:T(8,128)(2,1)} custom-call(f32[4,130,768]{2,1,0:T(8,128)} %get-tuple-element.101.kept, bf16[4,130,768]{2,1,0:T(8,128)(2,1)} %copy-done, bf16[130,768]{1,0:T(8,128)(2,1)} %copy-done.19, bf16[130,768]{1,0:T(8,128)(2,1)} %copy-done.21, bf16[130,768]{1,0:T(8,128)(2,1)} %copy-done.23, f32[130,768]{1,0:T(8,128)} %get-tuple-element.103.own_act, ...), custom_call_target="tpu_custom_call" | custom-call | tf_op jit(solution)/shard_map/input/pallas_call | solution.py:24
  (182 shorter events, 85.3 us)
Async XLA Ops:
  0.6 75.1 %collective-permute-start = (bf16[520,768]{1,0:T(8,128)(2,1)}, bf16[520,768]{1,0:T(8,128)(2,1)}, u32[]{:S(2)}, u32[]{:S(2)}) collective-permute-start(bf16[520,768]{1,0:T(8,128)(2,1)} %bitcast.19), channel_id=1, source_target_pairs={{0,4},{4,0},{1,5},{5,1},{2,6},{6,2},{3,7},{7,3},{8,12},{12,8},{9,1... | collective-permute-start | bytes 2396168 | tf_op jit(solution)/shard_map/ppermute | solution.py:429
  8.0 16.2 %collective-permute-start.4 = (bf16[960,192]{1,0:T(8,128)(2,1)}, bf16[960,192]{1,0:T(8,128)(2,1)S(1)}, u32[]{:S(2)}, u32[]{:S(2)}) collective-permute-start(bf16[960,192]{1,0:T(8,128)(2,1)} %get-tuple-element.73.refs_0_), channel_id=1, source_target_pairs={{0,8},{4,28},{8,16},{12,4},{16,24},{20,12},{24,0},{28,20},{1,9},{5... | collective-permute-start | bytes 1105928 | tf_op jit(solution)/shard_map/ppermute | solution.py:443
  9.6 36.4 %collective-permute-start.6 = (bf16[480,192]{1,0:T(8,128)(2,1)}, bf16[480,192]{1,0:T(8,128)(2,1)S(1)}, u32[]{:S(2)}, u32[]{:S(2)}) collective-permute-start(bf16[480,192]{1,0:T(8,128)(2,1)} %get-tuple-element.74), channel_id=1, source_target_pairs={{0,16},{8,24},{16,0},{24,8},{1,17},{9,25},{17,1},{25,9},{2,18},{10... | collective-permute-start | bytes 552968 | tf_op jit(solution)/shard_map/ppermute | solution.py:435
  24.3 45.6 %collective-permute-start.5 = (bf16[960,192]{1,0:T(8,128)(2,1)S(1)}, bf16[960,192]{1,0:T(8,128)(2,1)S(1)}, u32[]{:S(2)}, u32[]{:S(2)}) collective-permute-start(bf16[960,192]{1,0:T(8,128)(2,1)S(1)} %collective-permute-done.4.refs_1_), channel_id=1, source_target_pairs={{0,4},{4,0},{1,5},{5,1},{2,6},{6,2},{3,7},{7,3},{8,12},{12,8},{9,1... | collective-permute-start | bytes 1105928 | tf_op jit(solution)/shard_map/ppermute | solution.py:429
  24.3 62.6 %collective-permute-start.11 = (bf16[768,192]{1,0:T(8,128)(2,1)}, bf16[768,192]{1,0:T(8,128)(2,1)S(1)}, u32[]{:S(2)}, u32[]{:S(2)}) collective-permute-start(bf16[768,192]{1,0:T(8,128)(2,1)} %copy.25.down.refs_0_), channel_id=1, source_target_pairs={{0,8},{4,28},{8,16},{12,4},{16,24},{20,12},{24,0},{28,20},{1,9},{5... | collective-permute-start | bytes 884744 | tf_op jit(solution)/shard_map/ppermute | solution.py:443
  28.7 58.2 %collective-permute-start.13 = (bf16[384,192]{1,0:T(8,128)(2,1)}, bf16[384,192]{1,0:T(8,128)(2,1)S(1)}, u32[]{:S(2)}, u32[]{:S(2)}) collective-permute-start(bf16[384,192]{1,0:T(8,128)(2,1)} %get-tuple-element.78), channel_id=1, source_target_pairs={{0,16},{8,24},{16,0},{24,8},{1,17},{9,25},{17,1},{25,9},{2,18},{10... | collective-permute-start | bytes 442376 | tf_op jit(solution)/shard_map/ppermute | solution.py:435
  46.0 23.8 %collective-permute-start.7 = (bf16[480,192]{1,0:T(8,128)(2,1)S(1)}, bf16[480,192]{1,0:T(8,128)(2,1)S(1)}, u32[]{:S(2)}, u32[]{:S(2)}) collective-permute-start(bf16[480,192]{1,0:T(8,128)(2,1)S(1)} %collective-permute-done.6.refs_3_), channel_id=1, source_target_pairs={{0,4},{4,0},{1,5},{5,1},{2,6},{6,2},{3,7},{7,3},{8,12},{12,8},{9,1... | collective-permute-start | bytes 552968 | tf_op jit(solution)/shard_map/ppermute | solution.py:429
  74.2 14.7 %collective-permute-start.9 = (bf16[192,768]{1,0:T(8,128)(2,1)}, bf16[192,768]{1,0:T(8,128)(2,1)S(1)}, u32[]{:S(2)}, u32[]{:S(2)}) collective-permute-start(bf16[192,768]{1,0:T(8,128)(2,1)} %get-tuple-element.75.proj0), channel_id=1, source_target_pairs={{0,2},{1,3},{2,0},{3,1},{4,6},{5,7},{6,4},{7,5},{8,10},{9,11},{10,... | collective-permute-start | bytes 884744 | tf_op jit(solution)/shard_map/ppermute | solution.py:432
  88.9 12.7 %collective-permute-start.10 = (bf16[192,768]{1,0:T(8,128)(2,1)S(1)}, bf16[192,768]{1,0:T(8,128)(2,1)S(1)}, u32[]{:S(2)}, u32[]{:S(2)}) collective-permute-start(bf16[192,768]{1,0:T(8,128)(2,1)S(1)} %collective-permute-done.9.proj2), channel_id=1, source_target_pairs={{0,1},{1,0},{2,3},{3,2},{4,5},{5,4},{6,7},{7,6},{8,9},{9,8},{10,11... | collective-permute-start | bytes 884744 | tf_op jit(solution)/shard_map/ppermute | solution.py:432
  125.3 21.1 %collective-permute-start.17 = (bf16[520,192]{1,0:T(8,128)(2,1)}, bf16[520,192]{1,0:T(8,128)(2,1)}, u32[]{:S(2)}, u32[]{:S(2)}) collective-permute-start(bf16[520,192]{1,0:T(8,128)(2,1)} %get-tuple-element.91), channel_id=1, source_target_pairs={{0,1},{1,0},{2,3},{3,2},{4,5},{5,4},{6,7},{7,6},{8,9},{9,8},{10,11... | collective-permute-start | bytes 599048 | tf_op jit(solution)/shard_map/ppermute | solution.py:432
  129.7 16.7 %collective-permute-start.19 = (bf16[520,192]{1,0:T(8,128)(2,1)S(1)}, bf16[520,192]{1,0:T(8,128)(2,1)}, u32[]{:S(2)}, u32[]{:S(2)}) collective-permute-start(bf16[520,192]{1,0:T(8,128)(2,1)S(1)} %add_convert_fusion), channel_id=1, source_target_pairs={{0,2},{1,3},{2,0},{3,1},{4,6},{5,7},{6,4},{7,5},{8,10},{9,11},{10,... | collective-permute-start | bytes 599048 | tf_op jit(solution)/shard_map/ppermute | solution.py:432
  131.0 49.8 %collective-permute-start.32 = (bf16[4,768,192]{1,2,0:T(8,128)(2,1)S(1)}, bf16[4,768,192]{1,2,0:T(8,128)(2,1)S(1)}, u32[]{:S(2)}, u32[]{:S(2)}) collective-permute-start(bf16[4,768,192]{1,2,0:T(8,128)(2,1)S(1)} %copy.41), channel_id=1, source_target_pairs={{0,4},{4,0},{1,5},{5,1},{2,6},{6,2},{3,7},{7,3},{8,12},{12,8},{9,1... | collective-permute-start | bytes 3538952 | tf_op jit(solution)/shard_map/ppermute | solution.py:429
  144.9 14.6 %collective-permute-start.25 = (bf16[130,768]{1,0:T(8,128)(2,1)}, bf16[130,768]{1,0:T(8,128)(2,1)S(1)}, u32[]{:S(2)}, u32[]{:S(2)}) collective-permute-start(bf16[130,768]{1,0:T(8,128)(2,1)} %get-tuple-element.110.attn0), channel_id=1, source_target_pairs={{0,2},{1,3},{2,0},{3,1},{4,6},{5,7},{6,4},{7,5},{8,10},{9,11},{10,... | collective-permute-start | bytes 599048 | tf_op jit(solution)/shard_map/ppermute | solution.py:432
  163.5 27.3 %collective-permute-start.20 = (bf16[4,130,768]{2,0,1:T(4,128)(2,1)S(1)}, bf16[4,130,768]{2,0,1:T(4,128)(2,1)}, u32[]{:S(2)}, u32[]{:S(2)}) collective-permute-start(bf16[4,130,768]{2,0,1:T(4,128)(2,1)S(1)} %copy.34), channel_id=1, source_target_pairs={{0,1},{1,0},{2,3},{3,2},{4,5},{5,4},{6,7},{7,6},{8,9},{9,8},{10,11... | collective-permute-start | bytes 2396168 | tf_op jit(solution)/shard_map/ppermute | solution.py:432
  175.4 44.5 %collective-permute-start.27 = (bf16[4,384,192]{1,2,0:T(8,128)(2,1)}, bf16[4,384,192]{1,2,0:T(8,128)(2,1)}, u32[]{:S(2)}, u32[]{:S(2)}) collective-permute-start(bf16[4,384,192]{1,2,0:T(8,128)(2,1)} %copy.39), channel_id=1, source_target_pairs={{0,4},{4,0},{1,5},{5,1},{2,6},{6,2},{3,7},{7,3},{8,12},{12,8},{9,1... | collective-permute-start | bytes 1769480 | tf_op jit(solution)/shard_map/ppermute | solution.py:429
  186.1 14.1 %collective-permute-start.33 = (bf16[768,192]{1,0:T(8,128)(2,1)}, bf16[768,192]{1,0:T(8,128)(2,1)S(1)}, u32[]{:S(2)}, u32[]{:S(2)}) collective-permute-start(bf16[768,192]{1,0:T(8,128)(2,1)} %get-tuple-element.124), channel_id=1, source_target_pairs={{0,8},{8,16},{16,24},{24,0},{1,9},{9,17},{17,25},{25,1},{2,10},{10... | collective-permute-start | bytes 884744 | tf_op jit(solution)/shard_map/ppermute | solution.py:435
  187.0 27.2 %collective-permute-start.34 = (bf16[768,192]{1,0:T(8,128)(2,1)}, bf16[768,192]{1,0:T(8,128)(2,1)S(1)}, u32[]{:S(2)}, u32[]{:S(2)}) collective-permute-start(bf16[768,192]{1,0:T(8,128)(2,1)} %get-tuple-element.125), channel_id=1, source_target_pairs={{0,16},{8,24},{16,0},{24,8},{1,17},{9,25},{17,1},{25,9},{2,18},{10... | collective-permute-start | bytes 884744 | tf_op jit(solution)/shard_map/ppermute | solution.py:435
  187.9 26.4 %collective-permute-start.35 = (bf16[768,192]{1,0:T(8,128)(2,1)}, bf16[768,192]{1,0:T(8,128)(2,1)S(1)}, u32[]{:S(2)}, u32[]{:S(2)}) collective-permute-start(bf16[768,192]{1,0:T(8,128)(2,1)} %get-tuple-element.126), channel_id=1, source_target_pairs={{0,24},{8,0},{16,8},{24,16},{1,25},{9,1},{17,9},{25,17},{2,26},{10... | collective-permute-start | bytes 884744 | tf_op jit(solution)/shard_map/ppermute | solution.py:435
  217.8 41.2 %collective-permute-start.36 = (bf16[768,192]{1,0:T(8,128)(2,1)}, bf16[768,192]{1,0:T(8,128)(2,1)S(1)}, u32[]{:S(2)}, u32[]{:S(2)}) collective-permute-start(bf16[768,192]{1,0:T(8,128)(2,1)} %get-tuple-element.128), channel_id=1, source_target_pairs={{0,4},{4,0},{1,5},{5,1},{2,6},{6,2},{3,7},{7,3},{8,12},{12,8},{9,1... | collective-permute-start | bytes 884744 | tf_op jit(solution)/shard_map/ppermute | solution.py:429
  224.7 15.1 %collective-permute-start.28 = (bf16[384,192]{1,0:T(8,128)(2,1)}, bf16[384,192]{1,0:T(8,128)(2,1)S(1)}, u32[]{:S(2)}, u32[]{:S(2)}) collective-permute-start(bf16[384,192]{1,0:T(8,128)(2,1)} %get-tuple-element.114), channel_id=1, source_target_pairs={{0,8},{8,16},{16,24},{24,0},{1,9},{9,17},{17,25},{25,1},{2,10},{10... | collective-permute-start | bytes 442376 | tf_op jit(solution)/shard_map/ppermute | solution.py:435
  232.9 13.0 %collective-permute-start.29 = (bf16[384,192]{1,0:T(8,128)(2,1)}, bf16[384,192]{1,0:T(8,128)(2,1)S(1)}, u32[]{:S(2)}, u32[]{:S(2)}) collective-permute-start(bf16[384,192]{1,0:T(8,128)(2,1)} %get-tuple-element.115), channel_id=1, source_target_pairs={{0,16},{8,24},{16,0},{24,8},{1,17},{9,25},{17,1},{25,9},{2,18},{10... | collective-permute-start | bytes 442376 | tf_op jit(solution)/shard_map/ppermute | solution.py:435
  235.4 17.7 %collective-permute-start.21 = (bf16[130,768]{1,0:T(8,128)(2,1)S(1)}, bf16[130,768]{1,0:T(8,128)(2,1)S(1)}, u32[]{:S(2)}, u32[]{:S(2)}) collective-permute-start(bf16[130,768]{1,0:T(8,128)(2,1)S(1)} %get-tuple-element.154), channel_id=1, source_target_pairs={{0,2},{1,3},{2,0},{3,1},{4,6},{5,7},{6,4},{7,5},{8,10},{9,11},{10,... | collective-permute-start | bytes 599048 | tf_op jit(solution)/shard_map/ppermute | solution.py:432
  239.8 13.3 %collective-permute-start.22 = (bf16[130,768]{1,0:T(8,128)(2,1)S(1)}, bf16[130,768]{1,0:T(8,128)(2,1)S(1)}, u32[]{:S(2)}, u32[]{:S(2)}) collective-permute-start(bf16[130,768]{1,0:T(8,128)(2,1)S(1)} %get-tuple-element.153), channel_id=1, source_target_pairs={{0,4},{4,0},{1,5},{5,1},{2,6},{6,2},{3,7},{7,3},{8,12},{12,8},{9,1... | collective-permute-start | bytes 599048 | tf_op jit(solution)/shard_map/ppermute | solution.py:429
  248.9 15.5 %collective-permute-start.31 = (bf16[384,192]{1,0:T(8,128)(2,1)}, bf16[384,192]{1,0:T(8,128)(2,1)S(1)}, u32[]{:S(2)}, u32[]{:S(2)}) collective-permute-start(bf16[384,192]{1,0:T(8,128)(2,1)} %get-tuple-element.118), channel_id=1, source_target_pairs={{0,4},{4,0},{1,5},{5,1},{2,6},{6,2},{3,7},{7,3},{8,12},{12,8},{9,1... | collective-permute-start | bytes 442376 | tf_op jit(solution)/shard_map/ppermute | solution.py:429
  (56 other events, 421.9 us)

commit v3 on v2

v3 whole, which is shorter than its diff:
```python
import math

import jax
import jax.numpy as jnp
from jax import lax
from jax.experimental import pallas as pl
from jax.experimental.pallas import tpu as pltpu
from jax.sharding import PartitionSpec as P

HD = 64
EPS = 1e-06
NEG = -1e30
F32 = jnp.float32
LOW = jnp.bfloat16
VMEM = pl.BlockSpec(memory_space=pltpu.VMEM)
SMEM = pl.BlockSpec(memory_space=pltpu.SMEM)


def shape(dims, dtype=LOW):
    return jax.ShapeDtypeStruct(dims, dtype)


def call(body, name, out, args, scalars=0, scratch=(), cost=None):
    return pl.pallas_call(
        body,
        name=name,
        out_shape=out,
        in_specs=[SMEM] * scalars + [VMEM] * (len(args) - scalars),
        out_specs=[VMEM] * len(out),
        scratch_shapes=list(scratch),
        compiler_params=pltpu.CompilerParams(vmem_limit_bytes=24 * 2**20),
        cost_estimate=cost,
    )(*args)


def cost(flops, moved, exps=0):
    return pl.CostEstimate(flops=flops, bytes_accessed=moved, transcendentals=exps)


def dot(left, right, left_dim=1, right_dim=0):
    return lax.dot_general(
        left, right, (((left_dim,), (right_dim,)), ((), ())), preferred_element_type=F32
    )


def norm_stats(values):
    centred = values - jnp.mean(values, axis=-1, keepdims=True)
    rate = lax.rsqrt(jnp.mean(centred * centred, axis=-1, keepdims=True) + EPS)
    return centred * rate, rate


def norm_back(grad, scaled, rate, gain):
    e = grad * gain
    inner = jnp.mean(e * scaled, axis=-1, keepdims=True)
    return rate * (e - jnp.mean(e, axis=-1, keepdims=True) - scaled * inner)


def own_other(counts):
    ctx = lax.axis_index("ctx")
    first, second = counts[0, 0], counts[0, 1]
    return jnp.where(ctx == 0, first, second), jnp.where(ctx == 0, second, first)


def wide(blocks):
    return jnp.concatenate(blocks, axis=1)


def to_chunks(value, ref):
    tp = lax.axis_index("tp")
    count = ref.shape[0]
    rows = value.shape[0] // count
    for g in range(count):
        ref[tp ^ g, :rows, :] = value[g * rows : (g + 1) * rows].astype(ref.dtype)


def folded_rows(rows):
    return (rows // 2 + 7) // 8 * 8


def fold_rows(value):
    top = folded_rows(value.shape[0])
    rest = value[top:]
    pad = jnp.zeros((top - rest.shape[0], value.shape[1]), value.dtype)
    if pad.shape[0]:
        rest = jnp.concatenate([rest, pad], axis=0)
    return wide([value[:top], rest])


def unfold_rows(value, rows):
    cols = value.shape[1] // 2
    return jnp.concatenate([value[:, :cols], value[: rows - value.shape[0], cols:]], axis=0)


def pack_body(qkv, gains, biases, proj, act, pack, pack_half, act_half):
    ctx = lax.axis_index("ctx")
    part, hw = qkv.shape[1], qkv.shape[2]
    width = pack.shape[1]
    pack[:part, :] = wide([qkv[0], qkv[1], qkv[2], proj[...].T])
    spare = pack.shape[0] - part
    vectors = jnp.concatenate(
        [gains[...].astype(F32), biases[...].astype(F32), jnp.zeros((spare - 6, part), F32)],
        axis=0,
    )
    pack[part:, :] = wide([vectors, jnp.zeros((spare, width - part), F32)]).astype(LOW)
    size = pack_half.shape[0]
    pack_half[...] = pack[pl.ds(pl.multiple_of(ctx * size, 16), size), :]
    size = act_half.shape[1]
    core = lax.axis_index("tp") % 2
    act_half[...] = act[:, pl.ds(pl.multiple_of(core * size, 128), size)]


def assemble(parts, held):
    n, rows, _ = held.shape
    shard, ctx = lax.axis_index("shard"), lax.axis_index("ctx")
    held[shard] = parts[0][...]
    for k in range(1, (n - 1) // 2 + 1):
        step = jnp.where(ctx == 0, n - k, k)
        held[(shard + step) % n] = parts[2 * k - 1][...]
        held[(shard + n - step) % n] = parts[2 * k][...]
    far = (shard + n // 2) % n
    size = rows // 2
    held[far, pl.ds(pl.multiple_of(ctx * size, 8), size), :] = parts[-2][...]
    held[far, pl.ds(pl.multiple_of((1 - ctx) * size, 8), size), :] = parts[-1][...]


def join_body(n, *refs):
    parts, (weights, proj, vectors, held) = refs[:-4], refs[-4:]
    assemble(parts, held)
    part = weights.shape[0] // n
    for g in range(n):
        weights[g * part : (g + 1) * part, :] = held[g, :part, :]
    vectors[...] = wide([held[g, part : part + 16, :part].astype(F32) for g in range(n)])[:8]
    cols = weights.shape[1] // 4
    half = weights.shape[0] // 2
    proj[...] = wide([weights[:half, 3 * cols :], weights[half:, 3 * cols :]])


def attend_body(
    counts, act, half_far, half_near, weights, vectors, biases, mixed_out, turned_out, scale_out,
    other, normed_own, normed_other, q_out, k_out, v_out, e_out,
):
    slots = act.shape[0]
    hw = biases.shape[1]
    core = lax.axis_index("tp") % 2
    size = half_far.shape[1]
    other[:, pl.ds(pl.multiple_of(core * size, 128), size)] = half_far[...]
    other[:, pl.ds(pl.multiple_of((1 - core) * size, 128), size)] = half_near[...]
    bias = biases[...].astype(F32)
    for src, dst in ((act, normed_own), (other, normed_other)):
        scaled, _ = norm_stats(src[...].astype(F32))
        dst[...] = (scaled * vectors[0:1] + vectors[2:3]).astype(LOW)
    queries = (dot(normed_own[...], weights[:, :hw]) + bias[0:1]).astype(LOW)
    q_out[...] = (queries.astype(F32) * (1.0 / math.sqrt(HD))).astype(LOW)
    for i, src in enumerate((normed_own, normed_other)):
        both = dot(src[...], weights[:, hw : 3 * hw])
        k_out[i] = both[:, :hw].astype(LOW)
        v_out[i] = (both[:, hw:] + bias[1:2]).astype(LOW)
    ids = lax.broadcasted_iota(jnp.int32, (slots, 1), 0)
    outs, scales = [], []
    for h in range(hw // HD):
        cols = slice(h * HD, (h + 1) * HD)
        query = q_out[:, cols]
        scores = [
            jnp.where(ids < count, dot(k_out[i][:, cols], query, 1, 1), NEG)
            for i, count in enumerate(own_other(counts))
        ]
        peak = jnp.maximum(*[jnp.max(s, axis=0, keepdims=True) for s in scores])
        mixed, total = 0.0, 0.0
        for i in range(2):
            e = jnp.exp(scores[i] - peak)
            total = total + jnp.sum(e, axis=0, keepdims=True)
            e_out[h, i] = e.astype(LOW)
            mixed = mixed + dot(v_out[i][:, cols], e_out[h, i], 0, 0)
        scales.append(1.0 / total)
        outs.append(mixed * scales[-1])
    turned = jnp.concatenate(outs, axis=0)
    turned_out[...] = turned
    mixed_out[...] = fold_rows(turned.T).astype(LOW)
    scales.append(jnp.zeros((8 - len(scales), slots), F32))
    scale_out[...] = jnp.concatenate(scales, axis=0).T


def middle_body(n, *refs):
    (counts, act, *rest) = refs
    mixes, projs, rest = rest[:4], rest[4:8], rest[8:]
    vectors, hidden_bias, cot, *rest = rest
    count = n + (n % 2 == 0)
    ups, downs, rest = rest[:count], rest[count : 2 * count], rest[2 * count :]
    (back0, back1, back2, back3, two_out, gelu_out, hidden_out, branch_out, low_out, middle_out,
     down_out, sums, held, proj) = rest
    slots = act.shape[0]
    width = act.shape[1]
    own, _ = own_other(counts)
    valid = lax.broadcasted_iota(jnp.int32, (slots, 1), 0) < own
    branch = jnp.where(valid, cot[...].astype(F32), 0.0)
    branch_low = branch.astype(LOW)
    branch_out[...] = branch_low
    top, bottom = 0.0, 0.0
    for j, (mixed, packed) in enumerate(zip(mixes, projs)):
        cols = packed.shape[1] // 2
        half = packed.shape[0]
        proj[j, :half, :] = packed[:, :cols]
        proj[j, half:, :] = packed[:, cols:]
        top = top + dot(mixed[:, :cols], proj[j], 1, 1)
        bottom = bottom + dot(mixed[:, cols:], proj[j], 1, 1)
    rows = slots - top.shape[0]
    middle = jnp.concatenate([top, bottom[:rows]], axis=0) + act[...].astype(F32) + vectors[4:5]
    middle_out[...] = middle
    scaled, rate = norm_stats(middle)
    two = (scaled * vectors[1:2] + vectors[3:4]).astype(LOW)
    two_out[...] = two
    assemble(downs, held)
    down_out[...] = held[...].reshape(width, -1)
    assemble(ups, held)
    up = held[...].reshape(width, -1)
    hidden = dot(two, up) + hidden_bias[...].astype(F32)
    share = 0.5 * (1.0 + lax.erf(hidden * math.sqrt(0.5)))
    gelu_out[...] = (hidden * share).astype(LOW)
    slope = share + hidden * (jnp.exp(hidden * hidden * -0.5) * (1.0 / math.sqrt(2.0 * math.pi)))
    grad_hidden = (dot(branch_low, down_out[...]) * slope).astype(LOW)
    hidden_out[...] = grad_hidden
    grad_two = dot(grad_hidden, up, 1, 1)
    back = norm_back(grad_two, scaled, rate, vectors[1:2])
    low = back.astype(LOW)
    low_out[...] = low
    back0[...] = fold_rows(dot(low, proj[0]) + dot(branch_low, proj[0]))
    for j, out in enumerate((back1, back2, back3), 1):
        out[...] = fold_rows(dot(low, proj[j])).astype(LOW)
    first_tp = jnp.where(lax.axis_index("tp") == 0, 1.0, 0.0)
    branch_sum = jnp.sum(branch, axis=0, keepdims=True) * first_tp
    sums[...] = jnp.concatenate(
        [
            jnp.sum(grad_two * scaled, axis=0, keepdims=True),
            jnp.sum(grad_two, axis=0, keepdims=True),
            branch_sum + jnp.sum(back, axis=0, keepdims=True),
            branch_sum,
            jnp.sum(grad_hidden.astype(F32), axis=0, keepdims=True),
            jnp.zeros((3, sums.shape[1]), F32),
        ],
        axis=0,
    )


def ffn_grads_body(two, gelu, hidden, branch, down, sent, kept):
    ctx = lax.axis_index("ctx")
    down_grad = dot(branch[...], gelu[...], 0, 0)
    up_grad = dot(two[...], hidden[...], 0, 0)

    @pl.when(ctx == 0)
    def _():
        kept[...] = down_grad
        sent[...] = up_grad.astype(LOW)

    @pl.when(ctx == 1)
    def _():
        kept[...] = up_grad
        sent[...] = down_grad.astype(LOW)


def ffn_rows_body(gelu, branch, low, middle, down, near, keep, own_middle, own_branch, chunks):
    rows = own_middle.shape[0]
    chunks[:, rows - 2 :, :] = jnp.zeros_like(chunks[:, rows - 2 :, :])
    to_chunks(dot(gelu[...], down[...], 1, 1), chunks)
    near[0] = chunks[1].astype(LOW)
    near[1] = chunks[3].astype(LOW)
    keep[0] = chunks[0]
    keep[2] = chunks[2]
    to_chunks(low[...].astype(F32), chunks)
    near[2] = chunks[1].astype(LOW)
    near[3] = chunks[3].astype(LOW)
    keep[1] = chunks[0]
    keep[3] = chunks[2]
    to_chunks(middle[...], chunks)
    own_middle[...] = chunks[0, :rows, :]
    to_chunks(branch[...].astype(F32), chunks)
    own_branch[...] = chunks[0, :rows, :]


def attend_back_body(
    back0, back1, back2, q, k, v, e, scales, turned, weights, act, other, sums_in,
    own_out, other_out, near, keep, own_act, sums, chunks,
):
    slots, hw = q.shape
    grad_mixed = back0[...] + back1[...].astype(F32) + back2[...].astype(F32)
    grad_mixed = unfold_rows(grad_mixed, slots).astype(LOW).astype(F32)
    scaled_grads = [
        grad_mixed[:, h * HD : (h + 1) * HD] * scales[:, h : h + 1] for h in range(hw // HD)
    ]
    scaled_grad = wide(scaled_grads)
    inner = scaled_grad.T * turned[...]
    scaled_low = scaled_grad.astype(LOW)
    scale = 1.0 / math.sqrt(HD)
    gq, gk, gv = [], ([], []), ([], [])
    for h in range(hw // HD):
        cols = slice(h * HD, (h + 1) * HD)
        grad = scaled_low[:, cols]
        row = jnp.sum(inner[cols], axis=0, keepdims=True)
        gq_head = 0.0
        for i in range(2):
            gv[i].append(dot(e[h, i], grad))
            probs_grad = dot(v[i][:, cols], grad, 1, 1)
            scores_grad = (e[h, i].astype(F32) * (probs_grad - row)).astype(LOW)
            gk[i].append(dot(scores_grad, q[:, cols]))
            gq_head = gq_head + dot(k[i][:, cols], scores_grad, 0, 0)
        gq.append(gq_head * scale)
    gq = jnp.concatenate(gq, axis=0).T
    own_out[...] = wide([gq, *gk[0], *gv[0]]).astype(LOW)
    other_out[...] = wide([*gk[1], *gv[1]]).astype(LOW)
    rows = own_act.shape[0]
    chunks[:, rows - 2 :, :] = jnp.zeros_like(chunks[:, rows - 2 :, :])
    gain_sum, shift_sum = 0.0, 0.0
    for i, src in enumerate((act, other)):
        if i == 0:
            grad = dot(own_out[...], weights[:, : 3 * hw], 1, 1)
        else:
            grad = dot(other_out[...], weights[:, hw : 3 * hw], 1, 1)
        scaled, _ = norm_stats(src[...].astype(F32))
        gain_sum = gain_sum + jnp.sum(grad * scaled, axis=0, keepdims=True)
        shift_sum = shift_sum + jnp.sum(grad, axis=0, keepdims=True)
        to_chunks(grad, chunks)
        near[2 * i] = chunks[1].astype(LOW)
        near[2 * i + 1] = chunks[3].astype(LOW)
        keep[2 * i] = chunks[0]
        keep[2 * i + 1] = chunks[2]
    to_chunks(act[...].astype(F32), chunks)
    own_act[...] = chunks[0, :rows, :]
    ones = jnp.ones((8, slots), LOW)
    own_sums = dot(ones, own_out[...])[0:1]
    other_sums = dot(ones, other_out[...])[0:1]
    head_v = own_sums[:, 2 * hw :] + other_sums[:, hw:]
    pad = jnp.zeros((1, sums.shape[1] - 2 * hw), F32)
    sums[...] = jnp.concatenate(
        [
            gain_sum,
            sums_in[0:1],
            shift_sum,
            sums_in[1:2],
            sums_in[2:3],
            sums_in[3:4],
            sums_in[4:5],
            wide([own_sums[:, :hw], head_v, pad]),
        ],
        axis=0,
    )


def head_grads_body(
    own, other, normed_own, normed_other, mixed, attn0, attn1, attn2, attn3, sent, kept, chunks
):
    ctx = lax.axis_index("ctx")
    hw = own.shape[1] // 3
    to_chunks(unfold_rows(mixed[...].astype(F32), own.shape[0]), chunks)
    proj_grad = 0.0
    for j, attn in enumerate((attn0, attn1, attn2, attn3)):
        proj_grad = proj_grad + dot(attn[...], chunks[j].astype(LOW), 0, 0)
    from_own = dot(normed_own[...], own[...], 0, 0)
    from_other = dot(normed_other[...], other[...], 0, 0)
    k_grad = from_own[:, hw : 2 * hw] + from_other[:, :hw]
    v_grad = from_own[:, 2 * hw :] + from_other[:, hw:]
    early = wide([from_own[:, :hw], k_grad])
    late = wide([v_grad, proj_grad])

    @pl.when(ctx == 0)
    def _():
        kept[...] = early
        sent[...] = late.astype(LOW)

    @pl.when(ctx == 1)
    def _():
        kept[...] = late
        sent[...] = early.astype(LOW)


def fold_body(n, kept, got, own, *outs):
    shard = lax.axis_index("shard")
    rows = own.shape[0]

    def summed(owner):
        at = pl.ds(pl.multiple_of(owner * rows, 16), rows)
        return kept[at, :] + got[at, :].astype(F32)

    own[...] = summed(shard)
    for k, out in enumerate(outs, 1):
        out[...] = summed((shard + k) % n).astype(LOW)


def total_body(own, *refs):
    got, total, low = refs[:-2], refs[-2], refs[-1]
    value = own[...]
    for ref in got:
        value = value + ref[...].astype(F32)
    total[...] = value
    low[...] = value.astype(LOW)


def ffn_finish_body(mine, other, up_grad, down_grad):
    first = lax.axis_index("ctx") == 0
    theirs = other[...].astype(F32)
    down_grad[...] = jnp.where(first, mine[...], theirs)
    up_grad[...] = jnp.where(first, theirs, mine[...])


def head_finish_body(mine, other, qkv_grad, proj_grad):
    first = lax.axis_index("ctx") == 0
    theirs = other[...].astype(F32)
    early = jnp.where(first, mine[...], theirs)
    late = jnp.where(first, theirs, mine[...])
    hw = early.shape[1] // 2
    qkv_grad[0] = early[:, :hw]
    qkv_grad[1] = early[:, hw:]
    qkv_grad[2] = late[:, :hw]
    proj_grad[...] = late[:, hw:].T


def rows_body(counts, keep, near, far, own_middle, own_branch, vectors, layer_out, middle_grad, attn):
    own, _ = own_other(counts)
    rows = layer_out.shape[0]
    ids = lax.broadcasted_iota(jnp.int32, (rows, 1), 0) + lax.axis_index("tp") * rows
    mlp = keep[0] + near[0].astype(F32) + far[0].astype(F32)
    value = own_middle[...] + mlp[:rows] + vectors[5:6]
    layer_out[...] = jnp.where(ids < own, value, 0.0).astype(LOW)
    back = keep[1] + near[2].astype(F32) + far[1].astype(F32)
    grad = own_branch[...] + back[:rows]
    middle_grad[...] = grad
    attn[...] = grad.astype(LOW)


def halfway_body(keep, near, *outs):
    for out, (i, j) in zip(outs, PAIRS[len(outs)]):
        out[...] = (keep[i] + near[j].astype(F32)).astype(LOW).reshape(out.shape)


def input_body(kept, near, from_tp, from_ctx, from_far, own_act, middle_grad, vectors, out):
    rows = out.shape[0]
    grad = kept[0] + near[0].astype(F32) + from_tp[...].astype(F32)
    grad = grad + from_ctx[...].astype(F32) + from_far[...].astype(F32)
    scaled, rate = norm_stats(own_act[...])
    back = norm_back(grad[:rows], scaled, rate, vectors[0:1])
    out[...] = (middle_grad[...] + back).astype(LOW)


PAIRS = {3: ((1, 1), (2, 2), (3, 3))}


def per_device(
    activations,
    slot_counts,
    qkv_weight,
    proj_weight,
    up_weight,
    down_weight,
    norm_gains,
    row_biases,
    head_biases,
    hidden_bias,
    cotangent,
):
    images, slots, width = activations.shape
    n = lax.axis_size("shard")
    n_ctx = lax.axis_size("ctx")
    n_tp = lax.axis_size("tp")
    assert images == 1 and n_ctx == 2 and n_tp == 4 and n % 2 == 0
    part = width // n
    hw = qkv_weight.shape[2]
    ff = up_weight.shape[1]
    quarter = slots // n_tp
    padded = (quarter + 7) // 8 * 8
    fold = folded_rows(slots)
    heads = hw // HD
    ctx = lax.axis_index("ctx")

    def over_ctx(x):
        return lax.ppermute(x, "ctx", [(i, i ^ 1) for i in range(n_ctx)])

    def over_tp(x, bit):
        return lax.ppermute(x, "tp", [(i, i ^ bit) for i in range(n_tp)])

    def shift(x, k):
        return lax.ppermute(x, "shard", [(i, (i + k) % n) for i in range(n)])

    def shift_by_ctx(x, k):
        moves = [
            (i * n_ctx + r, ((i + (k if r == 0 else n - k)) % n) * n_ctx + r)
            for i in range(n)
            for r in range(n_ctx)
        ]
        return lax.ppermute(x, ("shard", "ctx"), moves)

    def fetch(pack, pack_half):
        mine = [shift_by_ctx(pack, k) for k in range(1, (n - 1) // 2 + 1)]
        middle = shift(pack_half, n // 2)
        pairs = [x for m in mine for x in (m, over_ctx(m))]
        return [pack] + pairs + [middle, over_ctx(middle)]

    def with_n(body):
        def run(*refs):
            body(n, *refs)

        return run

    def spread_tp(x):
        far = over_tp(x, 2)
        return [x, over_tp(x, 1), far, over_tp(far, 1)]

    def row_half(x):
        size = x.shape[0] // 2
        return lax.dynamic_slice_in_dim(x, ctx * size, size, 0)

    act = activations[0]
    rows = -(-(part + 6) // 32) * 32
    pack, pack_half, act_half = call(
        pack_body,
        "pack",
        [shape((rows, width)), shape((rows // 2, width)), shape((slots, width // 2))],
        [qkv_weight, norm_gains, row_biases, proj_weight, act],
    )
    half_far = over_ctx(act_half)
    half_near = over_tp(half_far, 1)
    pack_parts = fetch(pack, pack_half)
    down_turned = down_weight.T
    up_late, down_late, _ = lax.optimization_barrier((up_weight, down_turned, pack_parts[1]))
    up_parts = fetch(up_late, row_half(up_late))
    down_late, _ = lax.optimization_barrier((down_late, up_parts[1]))
    down_parts = fetch(down_late, row_half(down_late))

    weights, proj, vectors = call(
        with_n(join_body),
        "join",
        [shape((width, width)), shape((width // 2, 2 * hw)), shape((8, width), F32)],
        pack_parts,
        scratch=[pltpu.VMEM((n, rows, width), LOW)],
    )
    (mixed, turned, scales, other, normed_own, normed_other, q, k, v, e) = call(
        attend_body,
        "attend",
        [
            shape((fold, 2 * hw)),
            shape((hw, slots), F32),
            shape((slots, 8), F32),
            shape((slots, width)),
            shape((slots, width)),
            shape((slots, width)),
            shape((slots, hw)),
            shape((2, slots, hw)),
            shape((2, slots, hw)),
            shape((heads, 2, slots, slots)),
        ],
        [slot_counts, act, half_far, half_near, weights, vectors, head_biases],
        scalars=1,
        cost=cost(3_000_000_000, 12_000_000, 2_000_000),
    )
    projs = spread_tp(proj)
    mixes = spread_tp(mixed)
    (back0, back1, back2, back3, two, gelu, hidden, branch, low, middle, down, sums) = call(
        with_n(middle_body),
        "middle",
        [shape((fold, 2 * hw), F32)]
        + [shape((fold, 2 * hw))] * 3
        + [shape((slots, width)), shape((slots, ff)), shape((slots, ff))]
        + [shape((slots, width))] * 2
        + [shape((slots, width), F32), shape((width, ff)), shape((8, width), F32)],
        [slot_counts, act, *mixes, *projs, vectors, hidden_bias.reshape(1, ff), cotangent[0]]
        + up_parts
        + down_parts,
        scalars=1,
        scratch=[pltpu.VMEM((n, part, ff), LOW), pltpu.VMEM((n_tp, width, hw), LOW)],
        cost=cost(4_000_000_000, 16_000_000, 1_000_000),
    )
    back1 = over_tp(back1, 1)
    back2 = (back2.astype(F32) + over_tp(back3, 1).astype(F32)).astype(LOW)
    back2 = over_tp(back2, 2)
    sent, kept = call(
        ffn_grads_body,
        "ffn_grads",
        [shape((width, ff)), shape((width, ff), F32)],
        [two, gelu, hidden, branch, down],
        cost=cost(1_300_000_000, 7_000_000),
    )
    near, keep, own_middle, own_branch = call(
        ffn_rows_body,
        "ffn_rows",
        [
            shape((4, padded, width)),
            shape((4, padded, width), F32),
            shape((quarter, width), F32),
            shape((quarter, width), F32),
        ],
        [gelu, branch, low, middle, down],
        scratch=[pltpu.VMEM((n_tp, padded, width), F32)],
        cost=cost(700_000_000, 7_000_000),
    )

    def owned(sent, kept):
        cols = kept.shape[1]
        own, *outs = call(
            with_n(fold_body),
            "fold",
            [shape((part, cols), F32)] + [shape((part, cols))] * (n - 1),
            [kept, over_ctx(sent)],
        )
        got = [shift(x, k) for k, x in enumerate(outs, 1)]
        total, low = call(
            total_body, "total", [shape((part, cols), F32), shape((part, cols))], [own, *got]
        )
        return [total, over_ctx(low)]

    ffn_totals = owned(sent, kept)
    near = over_tp(near, 1)
    far = jnp.stack(
        [
            (keep[2] + near[1].astype(F32)).astype(LOW),
            (keep[3] + near[3].astype(F32)).astype(LOW),
        ]
    )
    far = over_tp(far, 2)
    layer_out, middle_grad, attn = call(
        rows_body,
        "rows",
        [shape((quarter, width)), shape((quarter, width), F32), shape((quarter, width))],
        [slot_counts, keep, near, far, own_middle, own_branch, vectors],
        scalars=1,
    )
    attns = spread_tp(attn)

    own_grads, other_grads, near, keep, own_act, sums = call(
        attend_back_body,
        "attend_back",
        [
            shape((slots, 3 * hw)),
            shape((slots, 2 * hw)),
            shape((4, padded, width)),
            shape((4, padded, width), F32),
            shape((quarter, width), F32),
            shape((8, width), F32),
        ],
        [back0, back1, back2, q, k, v, e, scales, turned, weights, act, other, sums],
        scratch=[pltpu.VMEM((n_tp, padded, width), F32)],
        cost=cost(4_000_000_000, 16_000_000),
    )
    near = over_tp(near, 1)
    sent, kept = call(
        head_grads_body,
        "head_grads",
        [shape((width, 2 * hw)), shape((width, 2 * hw), F32)],
        [own_grads, other_grads, normed_own, normed_other, mixed, *attns],
        scratch=[pltpu.VMEM((n_tp, quarter, hw), F32)],
        cost=cost(1_000_000_000, 6_000_000),
    )
    head_totals = owned(sent, kept)
    to_tp, to_ctx, to_far = call(
        halfway_body, "halfway", [shape((padded, width))] * 3, [keep, near]
    )
    from_tp = over_tp(to_tp, 2)
    from_ctx = over_ctx(to_ctx)
    pairs = [(i, i ^ (n_tp + 2)) for i in range(n_ctx * n_tp)]
    from_far = lax.ppermute(to_far, ("ctx", "tp"), pairs)
    (input_grad,) = call(
        input_body,
        "input",
        [shape((quarter, width))],
        [keep, near, from_tp, from_ctx, from_far, own_act, middle_grad, vectors],
    )
    up_grad, down_grad = call(
        ffn_finish_body, "ffn_finish", [shape((part, ff), F32), shape((part, ff), F32)], ffn_totals
    )
    qkv_grad, proj_grad = call(
        head_finish_body,
        "head_finish",
        [shape((3, part, hw), F32), shape((hw, part), F32)],
        head_totals,
    )

    shared = sums[:6]
    for bit in (1, 2):
        shared = shared + over_tp(shared, bit)
    sums = jnp.concatenate([shared, sums[6:]])
    sums = sums + over_ctx(sums)
    bit = 1
    while bit < n:
        sums = sums + lax.ppermute(sums, "shard", [(i, i ^ bit) for i in range(n)])
        bit *= 2
    vector_grads = lax.dynamic_slice_in_dim(sums[:6], lax.axis_index("shard") * part, part, 1)
    return (
        layer_out[None],
        input_grad[None],
        qkv_grad,
        proj_grad,
        up_grad,
        down_grad.T,
        vector_grads[:2],
        vector_grads[2:],
        sums[7, : 2 * hw].reshape(2, hw),
        sums[6],
    )


def solution(mesh):
    placed = (
        P("shard", "ctx", None),
        P("shard", None),
        P(None, "shard", "tp"),
        P("tp", "shard"),
        P("shard", "tp"),
        P("tp", "shard"),
        P(None, "shard"),
        P(None, "shard"),
        P(None, "tp"),
        P("tp"),
        P("shard", "ctx", None),
    )
    return jax.shard_map(
        per_device,
        mesh=mesh,
        in_specs=placed,
        out_specs=(
            P("shard", ("ctx", "tp"), None),
            P("shard", ("ctx", "tp"), None),
            P(None, "shard", "tp"),
            P("tp", "shard"),
            P("shard", "tp"),
            P("tp", "shard"),
            P(None, "shard"),
            P(None, "shard"),
            P(None, "tp"),
            P("tp"),
        ),
        check_vma=False,
    )
```

time: 269 us -> 188 us (0.70)
  Pallas kernels: 79.9 us -> 42.5 us
  blocking collectives: 22.3 us -> 0 us
  local copies, waits for them, and re-layouts: 29.3 us -> 16.3 us
  starting transfers between devices: 50.5 us -> 47.5 us
  waiting for transfers between devices: 82.2 us -> 79.4 us
    pallas_call x16 -> x17, Pallas kernels: 79.9 us -> 42.5 us  [call(): pl.pallas_call(body, name=name, out_shape=out, in_specs=[SMEM] * scalars...]
    ppermute x8 -> x9, waiting for transfers between devices: 46 us -> 18.7 us  [shift(): return lax.ppermute(x, 'shard', [(i, (i + k) % n) for i in range(n)])]
    all_gather x1 -> x0, blocking collectives: 22.3 us -> none  [per_device(): first = lax.all_gather(first, 'shard')]
    ppermute x11 -> x13, waiting for transfers between devices: 7.55 us -> 19.9 us  [over_ctx(): return lax.ppermute(x, 'ctx', [(i, i ^ 1) for i in range(n_ctx)])]
    ppermute x2, waiting for transfers between devices: 3.82 us -> 11.8 us  [per_device(): sums = sums + lax.ppermute(sums, 'shard', [(i, i ^ bit) for i in range(n)])]
    pallas_call x4 -> x0, local copies, waits for them, and re-layouts: 5.94 us -> none  [call(): pl.pallas_call(body, name=name, out_shape=out, in_specs=[SMEM] * scalars...]
    ppermute x4 -> x0, local copies, waits for them, and re-layouts: 5.07 us -> none  [the longest x2 3.76 us: over_ctx(): return lax.ppermute(x, 'ctx', [(i, i ^ 1) for i in range(n_ctx)])]
    ppermute x18 -> x19, waiting for transfers between devices: 11.2 us -> 16 us  [over_tp(): return lax.ppermute(x, 'tp', [(i, i ^ bit) for i in range(n_tp)])]
  transfers between devices with their start and end apart: 42 -> 47, of which waited for: 14 -> 18; matrix products, arithmetic and copies ran while one was open for 8% -> 3% of each run, Pallas kernels for 21% -> 17%
where the time goes in v3:
time: 188 us
  waiting for transfers between devices  79.4 us (42%)
  starting transfers between devices  47.5 us (25%)
  Pallas kernels  42.5 us (23%)
  local copies, waits for them, and re-layouts  16.3 us (9%)
    pallas_call x17, Pallas kernels, call(): pl.pallas_call(body, name=name, out_shape=out, in_specs=[SMEM] * scalars...  42.5 us
    ppermute x13, waiting for transfers between devices, over_ctx(): return lax.ppermute(x, 'ctx', [(i, i ^ 1) for i in range(n_ctx)])  19.9 us
    ppermute x9, starting transfers between devices, shift(): return lax.ppermute(x, 'shard', [(i, (i + k) % n) for i in range(n)])  19.7 us
    ppermute x9, waiting for transfers between devices, shift(): return lax.ppermute(x, 'shard', [(i, (i + k) % n) for i in range(n)])  18.7 us
    ppermute x19, waiting for transfers between devices, over_tp(): return lax.ppermute(x, 'tp', [(i, i ^ bit) for i in range(n_tp)])  16 us
    ppermute x13, starting transfers between devices, over_ctx(): return lax.ppermute(x, 'ctx', [(i, i ^ 1) for i in range(n_ctx)])  13.2 us
    unnamed x52, local copies, waits for them, and re-layouts  12 us
    ppermute x2, waiting for transfers between devices, per_device(): sums = sums + lax.ppermute(sums, 'shard', [(i, i ^ bit) for i in range(n)])  11.8 us
  transfers between devices with their start and end apart: 47, of which 18 were waited for; matrix products, arithmetic and copies ran while one was open for 3% of the time, Pallas kernels for 17%

profile of v3, /device:TPU:0, one launch (start us, length us, event | category | flops | bytes accessed | tf_op | source)
XLA Modules:
  0.0 187.6 jit_solution(11693736805571687990)
XLA Ops:
  5.2 3.0 %collective-permute-start = (bf16[520,384]{1,0:T(8,128)(2,1)S(1)}, bf16[520,384]{1,0:T(8,128)(2,1)S(1)}, u32[]{:S(2)}, u32[]{:S(2)}) collective-permute-start(bf16[520,384]{1,0:T(8,128)(2,1)S(1)} %get-tuple-element.77), channel_id=1, source_target_pairs={{0,4},{4,0},{1,5},{5,1},{2,6},{6,2},{3,7},{7,3},{8,12},{12,8},{9,1... | collective-permute-start | bytes 1198088 | tf_op jit(solution)/shard_map/ppermute | solution.py:473
  9.8 9.8 %collective-permute-done.2.refs_1_ = bf16[224,768]{1,0:T(8,128)(2,1)S(1)} collective-permute-done((bf16[224,768]{1,0:T(8,128)(2,1)S(1)}, bf16[224,768]{1,0:T(8,128)(2,1)S(1)}, u32[]{:S(2)}, u32[]{:S(2)}) %collective-permute-start.2) | collective-permute-done | bytes 344096 | tf_op jit(solution)/shard_map/ppermute | solution.py:487
  19.6 2.3 %collective-permute-start.4 = (bf16[112,768]{1,0:T(8,128)(2,1)S(1)}, bf16[112,768]{1,0:T(8,128)(2,1)S(1)}, u32[]{:S(2)}, u32[]{:S(2)}) collective-permute-start(bf16[112,768]{1,0:T(8,128)(2,1)S(1)} %get-tuple-element.79), channel_id=1, source_target_pairs={{0,16},{8,24},{16,0},{24,8},{1,17},{9,25},{17,1},{25,9},{2,18},{10... | collective-permute-start | bytes 516104 | tf_op jit(solution)/shard_map/ppermute | solution.py:479
  24.7 2.9 %collective-permute-start.14 = (bf16[96,768]{1,0:T(8,128)(2,1)S(1)}, bf16[96,768]{1,0:T(8,128)(2,1)S(1)}, u32[]{:S(2)}, u32[]{:S(2)}) collective-permute-start(bf16[96,768]{1,0:T(8,128)(2,1)S(1)} %constant_dynamic-slice_fusion.2), channel_id=1, source_target_pairs={{0,16},{8,24},{16,0},{24,8},{1,17},{9,25},{17,1},{25,9},{2,18},{10... | collective-permute-start | bytes 442376 | tf_op jit(solution)/shard_map/ppermute | solution.py:479
  27.6 12.2 %collective-permute-done.4.refs_3_ = bf16[112,768]{1,0:T(8,128)(2,1)S(1)} collective-permute-done((bf16[112,768]{1,0:T(8,128)(2,1)S(1)}, bf16[112,768]{1,0:T(8,128)(2,1)S(1)}, u32[]{:S(2)}, u32[]{:S(2)}) %collective-permute-start.4) | collective-permute-done | bytes 172064 | tf_op jit(solution)/shard_map/ppermute | solution.py:479
  39.8 3.1 %collective-permute-done.14.refs_16_ = bf16[96,768]{1,0:T(8,128)(2,1)S(1)} collective-permute-done((bf16[96,768]{1,0:T(8,128)(2,1)S(1)}, bf16[96,768]{1,0:T(8,128)(2,1)S(1)}, u32[]{:S(2)}, u32[]{:S(2)}) %collective-permute-start.14) | collective-permute-done | bytes 147488 | tf_op jit(solution)/shard_map/ppermute | solution.py:479
  44.2 2.4 %collective-permute-done.5.refs_4_ = bf16[112,768]{1,0:T(8,128)(2,1)S(1)} collective-permute-done((bf16[112,768]{1,0:T(8,128)(2,1)S(1)}, bf16[112,768]{1,0:T(8,128)(2,1)S(1)}, u32[]{:S(2)}, u32[]{:S(2)}) %collective-permute-start.5) | collective-permute-done | bytes 172064 | tf_op jit(solution)/shard_map/ppermute | solution.py:473
  49.5 7.0 %attend.1 = (bf16[264,384]{1,0:T(8,128)(2,1)S(1)}, f32[192,520]{1,0:T(8,128)S(1)}, f32[520,8]{1,0:T(8,128)S(1)}, bf16[520,768]{1,0:T(8,128)(2,1)S(1)}, bf16[520,...) custom-call(s32[1,2]{1,0:T(1,128)S(1)} %copy-done.20, ...), custom_call_target="tpu_custom_call" | custom-call | flops 3000000000 | bytes 12000000 | tf_op jit(solution)/shard_map/attend/pallas_call | solution.py:24
  57.1 3.4 %collective-permute-done.18.refs_21_ = bf16[96,768]{1,0:T(8,128)(2,1)S(1)} collective-permute-done((bf16[96,768]{1,0:T(8,128)(2,1)S(1)}, bf16[96,768]{1,0:T(8,128)(2,1)S(1)}, u32[]{:S(2)}, u32[]{:S(2)}) %collective-permute-start.18) | collective-permute-done | bytes 147488 | tf_op jit(solution)/shard_map/ppermute | solution.py:479
  62.7 4.4 %collective-permute-done.19.refs_22_ = bf16[96,768]{1,0:T(8,128)(2,1)S(1)} collective-permute-done((bf16[96,768]{1,0:T(8,128)(2,1)S(1)}, bf16[96,768]{1,0:T(8,128)(2,1)S(1)}, u32[]{:S(2)}, u32[]{:S(2)}) %collective-permute-start.19) | collective-permute-done | bytes 147488 | tf_op jit(solution)/shard_map/ppermute | solution.py:473
  68.9 3.6 %collective-permute-done.17.refs_20_ = bf16[192,768]{1,0:T(8,128)(2,1)S(1)} collective-permute-done((bf16[192,768]{1,0:T(8,128)(2,1)S(1)}, bf16[192,768]{1,0:T(8,128)(2,1)S(1)}, u32[]{:S(2)}, u32[]{:S(2)}) %collective-permute-start.17) | collective-permute-done | bytes 294944 | tf_op jit(solution)/shard_map/ppermute | solution.py:473
  72.5 6.2 %middle.1 = (f32[264,384]{1,0:T(8,128)S(1)}, bf16[264,384]{1,0:T(8,128)(2,1)S(1)}, bf16[264,384]{1,0:T(8,128)(2,1)S(1)}, bf16[264,384]{1,0:T(8,128)(2,1)S(1)}, b...) custom-call(s32[1,2]{1,0:T(1,128)S(1)} %copy-done.20, ...), custom_call_target="tpu_custom_call" | custom-call | flops 4000000000 | bytes 16000000 | tf_op jit(solution)/shard_map/middle/pallas_call | solution.py:24
  86.0 10.3 %collective-permute-done.21.far = bf16[2,136,768]{2,1,0:T(8,128)(2,1)S(1)} collective-permute-done((bf16[2,136,768]{2,1,0:T(8,128)(2,1)S(1)}, bf16[2,136,768]{2,1,0:T(8,128)(2,1)S(1)}, u32[]{:S(2)}, u32[]{:S(2)}) %collective-permute-start.21) | collective-permute-done | bytes 417824 | tf_op jit(solution)/shard_map/ppermute | solution.py:476
  100.7 8.7 %attend_back.1 = (bf16[520,576]{1,0:T(8,128)(2,1)S(1)}, bf16[520,384]{1,0:T(8,128)(2,1)S(1)}, bf16[4,136,768]{2,1,0:T(8,128)(2,1)}, f32[4,136,768]{2,1,0:T(8,128...) custom-call(f32[264,384]{1,0:T(8,128)S(1)} %get-tuple-element.97.back0, ...), custom_call_target="tpu_custom_call" | custom-call | flops 4000000000 | bytes 16000000 | tf_op jit(solution)/shard_map/attend_back/pallas_call | solution.py:24
  112.8 2.3 %collective-permute-done.43 = f32[6,768]{1,0:T(8,128)S(1)} collective-permute-done((f32[6,768]{1,0:T(8,128)S(1)}, f32[6,768]{1,0:T(8,128)S(1)}, u32[]{:S(2)}, u32[]{:S(2)}) %collective-permute-start.43) | collective-permute-done | bytes 18464 | tf_op jit(solution)/shard_map/ppermute | solution.py:476
  115.2 2.5 %head_grads.1 = (bf16[768,384]{1,0:T(8,128)(2,1)S(1)}, f32[768,384]{1,0:T(8,128)S(1)}) custom-call(bf16[520,576]{1,0:T(8,128)(2,1)S(1)} %get-tuple-element.116.own, bf16[520,384]{1,0:T(8,128)(2,1)S(1)} %get-tuple-element.117.other, bf16[520,768]{1,0:T(8,128)(2,1)S(1)} %get-tuple-element.118.normed_own, bf16[520,768]{1,0:T(8,128)(2,1)S(1)} %get-tuple-element.119.normed_other, ...), custom_call_target="tpu_custom_call" | custom-call | flops 1000000000 | bytes 6000000 | tf_op jit(solution)/shard_map/head_grads/pallas_call | solution.py:24
  121.4 3.4 %collective-permute-start.39 = (bf16[192,768]{1,0:T(8,128)(2,1)S(1)}, bf16[192,768]{1,0:T(8,128)(2,1)S(1)}, u32[]{:S(2)}, u32[]{:S(2)}) collective-permute-start(bf16[192,768]{1,0:T(8,128)(2,1)S(1)} %get-tuple-element.137), channel_id=1, source_target_pairs={{0,16},{8,24},{16,0},{24,8},{1,17},{9,25},{17,1},{25,9},{2,18},{10... | collective-permute-start | bytes 884744 | tf_op jit(solution)/shard_map/ppermute | solution.py:479
  124.8 7.7 %collective-permute-done.44 = f32[8,768]{1,0:T(8,128)S(1)} collective-permute-done((f32[8,768]{1,0:T(8,128)S(1)}, f32[8,768]{1,0:T(8,128)S(1)}, u32[]{:S(2)}, u32[]{:S(2)}) %collective-permute-start.44) | collective-permute-done | bytes 24608 | tf_op jit(solution)/shard_map/ppermute | solution.py:473
  133.3 8.6 %collective-permute-done.45 = f32[8,768]{1,0:T(8,128)S(1)} collective-permute-done((f32[8,768]{1,0:T(8,128)S(1)}, f32[8,768]{1,0:T(8,128)S(1)}, u32[]{:S(2)}, u32[]{:S(2)}) %collective-permute-start.45) | collective-permute-done | bytes 24608 | tf_op jit(solution)/shard_map/ppermute | solution.py:680
  141.9 3.1 %collective-permute-start.40 = (bf16[192,768]{1,0:T(8,128)(2,1)}, bf16[192,768]{1,0:T(8,128)(2,1)}, u32[]{:S(2)}, u32[]{:S(2)}) collective-permute-start(bf16[192,768]{1,0:T(8,128)(2,1)} %get-tuple-element.138), channel_id=1, source_target_pairs={{0,24},{8,0},{16,8},{24,16},{1,25},{9,1},{17,9},{25,17},{2,26},{10... | collective-permute-start | bytes 884744 | tf_op jit(solution)/shard_map/ppermute | solution.py:479
  146.6 3.2 %collective-permute-done.46 = f32[8,768]{1,0:T(8,128)} collective-permute-done((f32[8,768]{1,0:T(8,128)S(1)}, f32[8,768]{1,0:T(8,128)}, u32[]{:S(2)}, u32[]{:S(2)}) %collective-permute-start.46) | collective-permute-done | bytes 24608 | tf_op jit(solution)/shard_map/ppermute | solution.py:680
  151.5 2.5 %collective-permute-start.34 = (bf16[192,384]{1,0:T(8,128)(2,1)}, bf16[192,384]{1,0:T(8,128)(2,1)}, u32[]{:S(2)}, u32[]{:S(2)}) collective-permute-start(bf16[192,384]{1,0:T(8,128)(2,1)} %get-tuple-element.125), channel_id=1, source_target_pairs={{0,16},{8,24},{16,0},{24,8},{1,17},{9,25},{17,1},{25,9},{2,18},{10... | collective-permute-start | bytes 442376 | tf_op jit(solution)/shard_map/ppermute | solution.py:479
  154.7 2.9 %collective-permute-start.35 = (bf16[192,384]{1,0:T(8,128)(2,1)}, bf16[192,384]{1,0:T(8,128)(2,1)}, u32[]{:S(2)}, u32[]{:S(2)}) collective-permute-start(bf16[192,384]{1,0:T(8,128)(2,1)} %get-tuple-element.126), channel_id=1, source_target_pairs={{0,24},{8,0},{16,8},{24,16},{1,25},{9,1},{17,9},{25,17},{2,26},{10... | collective-permute-start | bytes 442376 | tf_op jit(solution)/shard_map/ppermute | solution.py:479
  177.2 3.2 %collective-permute-done.28.from_far = bf16[136,768]{1,0:T(8,128)(2,1)} collective-permute-done((bf16[136,768]{1,0:T(8,128)(2,1)}, bf16[136,768]{1,0:T(8,128)(2,1)}, u32[]{:S(2)}, u32[]{:S(2)}) %collective-permute-start.28) | collective-permute-done | bytes 208928 | tf_op jit(solution)/shard_map/ppermute | solution.py:656
  (157 shorter events, 67.9 us)
Async XLA Ops:
  5.2 14.4 %collective-permute-start = (bf16[520,384]{1,0:T(8,128)(2,1)S(1)}, bf16[520,384]{1,0:T(8,128)(2,1)S(1)}, u32[]{:S(2)}, u32[]{:S(2)}) collective-permute-start(bf16[520,384]{1,0:T(8,128)(2,1)S(1)} %get-tuple-element.77), channel_id=1, source_target_pairs={{0,4},{4,0},{1,5},{5,1},{2,6},{6,2},{3,7},{7,3},{8,12},{12,8},{9,1... | collective-permute-start | bytes 1198088 | tf_op jit(solution)/shard_map/ppermute | solution.py:473
  19.6 23.3 %collective-permute-start.12 = (bf16[192,768]{1,0:T(8,128)(2,1)}, bf16[192,768]{1,0:T(8,128)(2,1)S(1)}, u32[]{:S(2)}, u32[]{:S(2)}) collective-permute-start(bf16[192,768]{1,0:T(8,128)(2,1)} %refs_13_), channel_id=1, source_target_pairs={{0,8},{4,28},{8,16},{12,4},{16,24},{20,12},{24,0},{28,20},{1,9},{5... | collective-permute-start | bytes 884744 | tf_op jit(solution)/shard_map/ppermute | solution.py:487
  19.6 28.2 %collective-permute-start.1 = (bf16[520,384]{1,0:T(8,128)(2,1)S(1)}, bf16[520,384]{1,0:T(8,128)(2,1)S(1)}, u32[]{:S(2)}, u32[]{:S(2)}) collective-permute-start(bf16[520,384]{1,0:T(8,128)(2,1)S(1)} %collective-permute-done.half_far), channel_id=1, source_target_pairs={{0,1},{1,0},{2,3},{3,2},{4,5},{5,4},{6,7},{7,6},{8,9},{9,8},{10,11... | collective-permute-start | bytes 1198088 | tf_op jit(solution)/shard_map/ppermute | solution.py:476
  19.6 20.2 %collective-permute-start.4 = (bf16[112,768]{1,0:T(8,128)(2,1)S(1)}, bf16[112,768]{1,0:T(8,128)(2,1)S(1)}, u32[]{:S(2)}, u32[]{:S(2)}) collective-permute-start(bf16[112,768]{1,0:T(8,128)(2,1)S(1)} %get-tuple-element.79), channel_id=1, source_target_pairs={{0,16},{8,24},{16,0},{24,8},{1,17},{9,25},{17,1},{25,9},{2,18},{10... | collective-permute-start | bytes 516104 | tf_op jit(solution)/shard_map/ppermute | solution.py:479
  21.9 25.7 %collective-permute-start.3 = (bf16[224,768]{1,0:T(8,128)(2,1)S(1)}, bf16[224,768]{1,0:T(8,128)(2,1)S(1)}, u32[]{:S(2)}, u32[]{:S(2)}) collective-permute-start(bf16[224,768]{1,0:T(8,128)(2,1)S(1)} %collective-permute-done.2.refs_1_), channel_id=1, source_target_pairs={{0,4},{4,0},{1,5},{5,1},{2,6},{6,2},{3,7},{7,3},{8,12},{12,8},{9,1... | collective-permute-start | bytes 1032200 | tf_op jit(solution)/shard_map/ppermute | solution.py:473
  24.7 18.2 %collective-permute-start.14 = (bf16[96,768]{1,0:T(8,128)(2,1)S(1)}, bf16[96,768]{1,0:T(8,128)(2,1)S(1)}, u32[]{:S(2)}, u32[]{:S(2)}) collective-permute-start(bf16[96,768]{1,0:T(8,128)(2,1)S(1)} %constant_dynamic-slice_fusion.2), channel_id=1, source_target_pairs={{0,16},{8,24},{16,0},{24,8},{1,17},{9,25},{17,1},{25,9},{2,18},{10... | collective-permute-start | bytes 442376 | tf_op jit(solution)/shard_map/ppermute | solution.py:479
  42.9 13.6 %collective-permute-start.15 = (bf16[96,768]{1,0:T(8,128)(2,1)S(1)}, bf16[96,768]{1,0:T(8,128)(2,1)S(1)}, u32[]{:S(2)}, u32[]{:S(2)}) collective-permute-start(bf16[96,768]{1,0:T(8,128)(2,1)S(1)} %collective-permute-done.14.refs_16_), channel_id=1, source_target_pairs={{0,4},{4,0},{1,5},{5,1},{2,6},{6,2},{3,7},{7,3},{8,12},{12,8},{9,1... | collective-permute-start | bytes 442376 | tf_op jit(solution)/shard_map/ppermute | solution.py:473
  42.9 17.5 %collective-permute-start.16 = (bf16[192,768]{1,0:T(8,128)(2,1)}, bf16[192,768]{1,0:T(8,128)(2,1)S(1)}, u32[]{:S(2)}, u32[]{:S(2)}) collective-permute-start(bf16[192,768]{1,0:T(8,128)(2,1)} %bitcast.12), channel_id=1, source_target_pairs={{0,8},{4,28},{8,16},{12,4},{16,24},{20,12},{24,0},{28,20},{1,9},{5... | collective-permute-start | bytes 884744 | tf_op jit(solution)/shard_map/ppermute | solution.py:487
  46.6 13.9 %collective-permute-start.18 = (bf16[96,768]{1,0:T(8,128)(2,1)S(1)}, bf16[96,768]{1,0:T(8,128)(2,1)S(1)}, u32[]{:S(2)}, u32[]{:S(2)}) collective-permute-start(bf16[96,768]{1,0:T(8,128)(2,1)S(1)} %constant_dynamic-slice_fusion.1), channel_id=1, source_target_pairs={{0,16},{8,24},{16,0},{24,8},{1,17},{9,25},{17,1},{25,9},{2,18},{10... | collective-permute-start | bytes 442376 | tf_op jit(solution)/shard_map/ppermute | solution.py:479
  47.9 14.7 %collective-permute-start.10 = (bf16[384,384]{1,0:T(8,128)(2,1)S(1)}, bf16[384,384]{1,0:T(8,128)(2,1)S(1)}, u32[]{:S(2)}, u32[]{:S(2)}) collective-permute-start(bf16[384,384]{1,0:T(8,128)(2,1)S(1)} %get-tuple-element.83.refs_6_), channel_id=1, source_target_pairs={{0,2},{1,3},{2,0},{3,1},{4,6},{5,7},{6,4},{7,5},{8,10},{9,11},{10,... | collective-permute-start | bytes 884744 | tf_op jit(solution)/shard_map/ppermute | solution.py:476
  80.4 18.8 %collective-permute-start.22 = (bf16[264,384]{1,0:T(8,128)(2,1)S(1)}, bf16[264,384]{1,0:T(8,128)(2,1)S(1)}, u32[]{:S(2)}, u32[]{:S(2)}) collective-permute-start(bf16[264,384]{1,0:T(8,128)(2,1)S(1)} %get-tuple-element.98), channel_id=1, source_target_pairs={{0,1},{1,0},{2,3},{3,2},{4,5},{5,4},{6,7},{7,6},{8,9},{9,8},{10,11... | collective-permute-start | bytes 608264 | tf_op jit(solution)/shard_map/ppermute | solution.py:476
  83.3 36.6 %collective-permute-start.37 = (bf16[768,768]{1,0:T(8,128)(2,1)S(1)}, bf16[768,768]{1,0:T(8,128)(2,1)S(1)}, u32[]{:S(2)}, u32[]{:S(2)}) collective-permute-start(bf16[768,768]{1,0:T(8,128)(2,1)S(1)} %get-tuple-element.134), channel_id=1, source_target_pairs={{0,4},{4,0},{1,5},{5,1},{2,6},{6,2},{3,7},{7,3},{8,12},{12,8},{9,1... | collective-permute-start | bytes 3538952 | tf_op jit(solution)/shard_map/ppermute | solution.py:473
  85.4 15.2 %collective-permute-start.24 = (bf16[264,384]{1,0:T(8,128)(2,1)S(1)}, bf16[264,384]{1,0:T(8,128)(2,1)S(1)}, u32[]{:S(2)}, u32[]{:S(2)}) collective-permute-start(bf16[264,384]{1,0:T(8,128)(2,1)S(1)} %add_convert_fusion.2), channel_id=1, source_target_pairs={{0,2},{1,3},{2,0},{3,1},{4,6},{5,7},{6,4},{7,5},{8,10},{9,11},{10,... | collective-permute-start | bytes 608264 | tf_op jit(solution)/shard_map/ppermute | solution.py:476
  112.8 50.8 %collective-permute-start.25 = (bf16[4,136,768]{2,1,0:T(8,128)(2,1)}, bf16[4,136,768]{2,1,0:T(8,128)(2,1)S(1)}, u32[]{:S(2)}, u32[]{:S(2)}) collective-permute-start(bf16[4,136,768]{2,1,0:T(8,128)(2,1)} %get-tuple-element.110), channel_id=1, source_target_pairs={{0,1},{1,0},{2,3},{3,2},{4,5},{5,4},{6,7},{7,6},{8,9},{9,8},{10,11... | collective-permute-start | bytes 2506760 | tf_op jit(solution)/shard_map/ppermute | solution.py:476
  117.7 27.3 %collective-permute-start.32 = (bf16[768,384]{1,0:T(8,128)(2,1)S(1)}, bf16[768,384]{1,0:T(8,128)(2,1)S(1)}, u32[]{:S(2)}, u32[]{:S(2)}) collective-permute-start(bf16[768,384]{1,0:T(8,128)(2,1)S(1)} %get-tuple-element.122), channel_id=1, source_target_pairs={{0,4},{4,0},{1,5},{5,1},{2,6},{6,2},{3,7},{7,3},{8,12},{12,8},{9,1... | collective-permute-start | bytes 1769480 | tf_op jit(solution)/shard_map/ppermute | solution.py:473
  119.5 13.0 %collective-permute-start.44 = (f32[8,768]{1,0:T(8,128)S(1)}, f32[8,768]{1,0:T(8,128)S(1)}, u32[]{:S(2)}, u32[]{:S(2)}) collective-permute-start(f32[8,768]{1,0:T(8,128)S(1)} %pad_maximum_fusion.1), channel_id=1, source_target_pairs={{0,4},{4,0},{1,5},{5,1},{2,6},{6,2},{3,7},{7,3},{8,12},{12,8},{9,1... | collective-permute-start | bytes 73736 | tf_op jit(solution)/shard_map/ppermute | solution.py:473
  120.7 30.1 %collective-permute-start.38 = (bf16[192,768]{1,0:T(8,128)(2,1)S(1)}, bf16[192,768]{1,0:T(8,128)(2,1)S(1)}, u32[]{:S(2)}, u32[]{:S(2)}) collective-permute-start(bf16[192,768]{1,0:T(8,128)(2,1)S(1)} %get-tuple-element.136), channel_id=1, source_target_pairs={{0,8},{8,16},{16,24},{24,0},{1,9},{9,17},{17,25},{25,1},{2,10},{10... | collective-permute-start | bytes 884744 | tf_op jit(solution)/shard_map/ppermute | solution.py:479
  121.4 32.6 %collective-permute-start.39 = (bf16[192,768]{1,0:T(8,128)(2,1)S(1)}, bf16[192,768]{1,0:T(8,128)(2,1)S(1)}, u32[]{:S(2)}, u32[]{:S(2)}) collective-permute-start(bf16[192,768]{1,0:T(8,128)(2,1)S(1)} %get-tuple-element.137), channel_id=1, source_target_pairs={{0,16},{8,24},{16,0},{24,8},{1,17},{9,25},{17,1},{25,9},{2,18},{10... | collective-permute-start | bytes 884744 | tf_op jit(solution)/shard_map/ppermute | solution.py:479
  141.9 16.5 %collective-permute-start.40 = (bf16[192,768]{1,0:T(8,128)(2,1)}, bf16[192,768]{1,0:T(8,128)(2,1)}, u32[]{:S(2)}, u32[]{:S(2)}) collective-permute-start(bf16[192,768]{1,0:T(8,128)(2,1)} %get-tuple-element.138), channel_id=1, source_target_pairs={{0,24},{8,0},{16,8},{24,16},{1,25},{9,1},{17,9},{25,17},{2,26},{10... | collective-permute-start | bytes 884744 | tf_op jit(solution)/shard_map/ppermute | solution.py:479
  149.9 16.2 %collective-permute-start.33 = (bf16[192,384]{1,0:T(8,128)(2,1)}, bf16[192,384]{1,0:T(8,128)(2,1)}, u32[]{:S(2)}, u32[]{:S(2)}) collective-permute-start(bf16[192,384]{1,0:T(8,128)(2,1)} %get-tuple-element.124), channel_id=1, source_target_pairs={{0,8},{8,16},{16,24},{24,0},{1,9},{9,17},{17,25},{25,1},{2,10},{10... | collective-permute-start | bytes 442376 | tf_op jit(solution)/shard_map/ppermute | solution.py:479
  151.5 16.2 %collective-permute-start.34 = (bf16[192,384]{1,0:T(8,128)(2,1)}, bf16[192,384]{1,0:T(8,128)(2,1)}, u32[]{:S(2)}, u32[]{:S(2)}) collective-permute-start(bf16[192,384]{1,0:T(8,128)(2,1)} %get-tuple-element.125), channel_id=1, source_target_pairs={{0,16},{8,24},{16,0},{24,8},{1,17},{9,25},{17,1},{25,9},{2,18},{10... | collective-permute-start | bytes 442376 | tf_op jit(solution)/shard_map/ppermute | solution.py:479
  154.7 13.3 %collective-permute-start.35 = (bf16[192,384]{1,0:T(8,128)(2,1)}, bf16[192,384]{1,0:T(8,128)(2,1)}, u32[]{:S(2)}, u32[]{:S(2)}) collective-permute-start(bf16[192,384]{1,0:T(8,128)(2,1)} %get-tuple-element.126), channel_id=1, source_target_pairs={{0,24},{8,0},{16,8},{24,16},{1,25},{9,1},{17,9},{25,17},{2,26},{10... | collective-permute-start | bytes 442376 | tf_op jit(solution)/shard_map/ppermute | solution.py:479
  163.2 20.4 %collective-permute-start.41 = (bf16[192,768]{1,0:T(8,128)(2,1)}, bf16[192,768]{1,0:T(8,128)(2,1)}, u32[]{:S(2)}, u32[]{:S(2)}) collective-permute-start(bf16[192,768]{1,0:T(8,128)(2,1)} %get-tuple-element.140), channel_id=1, source_target_pairs={{0,4},{4,0},{1,5},{5,1},{2,6},{6,2},{3,7},{7,3},{8,12},{12,8},{9,1... | collective-permute-start | bytes 884744 | tf_op jit(solution)/shard_map/ppermute | solution.py:473
  170.5 15.2 %collective-permute-start.36 = (bf16[192,384]{1,0:T(8,128)(2,1)}, bf16[192,384]{1,0:T(8,128)(2,1)}, u32[]{:S(2)}, u32[]{:S(2)}) collective-permute-start(bf16[192,384]{1,0:T(8,128)(2,1)} %get-tuple-element.128), channel_id=1, source_target_pairs={{0,4},{4,0},{1,5},{5,1},{2,6},{6,2},{3,7},{7,3},{8,12},{12,8},{9,1... | collective-permute-start | bytes 442376 | tf_op jit(solution)/shard_map/ppermute | solution.py:473
  (49 other events, 493.0 us)

commit v4 on v3

--- a/solution.py
+++ b/solution.py
@@ -20,7 +20,7 @@
     return jax.ShapeDtypeStruct(dims, dtype)
 
 
-def call(body, name, out, args, scalars=0, scratch=(), cost=None):
+def call(body, name, out, args, scalars=0, scratch=(), cost=None, room=24):
     return pl.pallas_call(
         body,
         name=name,
@@ -28,7 +28,7 @@
         in_specs=[SMEM] * scalars + [VMEM] * (len(args) - scalars),
         out_specs=[VMEM] * len(out),
         scratch_shapes=list(scratch),
-        compiler_params=pltpu.CompilerParams(vmem_limit_bytes=24 * 2**20),
+        compiler_params=pltpu.CompilerParams(vmem_limit_bytes=room * 2**20),
         cost_estimate=cost,
     )(*args)
 
@@ -112,15 +112,30 @@
 def assemble(parts, held):
     n, rows, _ = held.shape
     shard, ctx = lax.axis_index("shard"), lax.axis_index("ctx")
+    swapped = parts[-1]
+    pairs = (n - 1) // 2
     held[shard] = parts[0][...]
-    for k in range(1, (n - 1) // 2 + 1):
+    for k in range(1, pairs + 1):
         step = jnp.where(ctx == 0, n - k, k)
-        held[(shard + step) % n] = parts[2 * k - 1][...]
-        held[(shard + n - step) % n] = parts[2 * k][...]
+        held[(shard + step) % n] = parts[k][...]
+        held[(shard + n - step) % n] = swapped[(k - 1) * rows : k * rows, :]
     far = (shard + n // 2) % n
     size = rows // 2
     held[far, pl.ds(pl.multiple_of(ctx * size, 8), size), :] = parts[-2][...]
-    held[far, pl.ds(pl.multiple_of((1 - ctx) * size, 8), size), :] = parts[-1][...]
+    held[far, pl.ds(pl.multiple_of((1 - ctx) * size, 8), size), :] = swapped[pairs * rows :, :]
+
+
+def split_sums(value):
+    half = value.shape[1] // 2
+    stacked = jnp.concatenate([value[:, :half], value[:, half:]], axis=0)
+    high = stacked.astype(LOW)
+    rest = (stacked - high.astype(F32)).astype(LOW)
+    return jnp.concatenate([high, rest], axis=0)
+
+
+def joined_sums(value):
+    stacked = value[:16].astype(F32) + value[16:].astype(F32)
+    return wide([stacked[:8], stacked[8:]])
 
 
 def join_body(n, *refs):
@@ -180,21 +195,17 @@
     scale_out[...] = jnp.concatenate(scales, axis=0).T
 
 
-def middle_body(n, *refs):
+def hidden_body(n, *refs):
     (counts, act, *rest) = refs
     mixes, projs, rest = rest[:4], rest[4:8], rest[8:]
     vectors, hidden_bias, cot, *rest = rest
-    count = n + (n % 2 == 0)
-    ups, downs, rest = rest[:count], rest[count : 2 * count], rest[2 * count :]
-    (back0, back1, back2, back3, two_out, gelu_out, hidden_out, branch_out, low_out, middle_out,
-     down_out, sums, held, proj) = rest
+    ups, rest = rest[: n // 2 + 2], rest[n // 2 + 2 :]
+    two_out, gelu_out, slope_out, branch_out, middle_out, up_out, proj, held = rest
     slots = act.shape[0]
     width = act.shape[1]
     own, _ = own_other(counts)
     valid = lax.broadcasted_iota(jnp.int32, (slots, 1), 0) < own
-    branch = jnp.where(valid, cot[...].astype(F32), 0.0)
-    branch_low = branch.astype(LOW)
-    branch_out[...] = branch_low
+    branch_out[...] = jnp.where(valid, cot[...].astype(F32), 0.0).astype(LOW)
     top, bottom = 0.0, 0.0
     for j, (mixed, packed) in enumerate(zip(mixes, projs)):
         cols = packed.shape[1] // 2
@@ -206,20 +217,43 @@
     rows = slots - top.shape[0]
     middle = jnp.concatenate([top, bottom[:rows]], axis=0) + act[...].astype(F32) + vectors[4:5]
     middle_out[...] = middle
-    scaled, rate = norm_stats(middle)
+    scaled, _ = norm_stats(middle)
     two = (scaled * vectors[1:2] + vectors[3:4]).astype(LOW)
     two_out[...] = two
-    assemble(downs, held)
-    down_out[...] = held[...].reshape(width, -1)
     assemble(ups, held)
     up = held[...].reshape(width, -1)
+    up_out[...] = up
     hidden = dot(two, up) + hidden_bias[...].astype(F32)
     share = 0.5 * (1.0 + lax.erf(hidden * math.sqrt(0.5)))
     gelu_out[...] = (hidden * share).astype(LOW)
-    slope = share + hidden * (jnp.exp(hidden * hidden * -0.5) * (1.0 / math.sqrt(2.0 * math.pi)))
-    grad_hidden = (dot(branch_low, down_out[...]) * slope).astype(LOW)
+    bell = jnp.exp(hidden * hidden * -0.5) * (1.0 / math.sqrt(2.0 * math.pi))
+    slope_out[...] = share + hidden * bell
+
+
+def down_grads_body(n, branch, gelu, own, *rest):
+    outs, total = rest[:-1], rest[-1]
+    shard = lax.axis_index("shard")
+    rows = own.shape[0]
+    total[...] = dot(branch[...], gelu[...], 0, 0)
+    own[...] = total[pl.ds(pl.multiple_of(shard * rows, 16), rows), :]
+    for k, out in enumerate(outs, 1):
+        at = (shard + k) % n * rows
+        out[...] = total[pl.ds(pl.multiple_of(at, 16), rows), :].astype(LOW)
+
+
+def middle_back_body(n, *refs):
+    branch, slope, up, middle, vectors, proj, *rest = refs
+    downs, rest = rest[: n // 2 + 2], rest[n // 2 + 2 :]
+    back0, back1, back2, back3, hidden_out, low_out, down_out, sums, held = rest
+    width = up.shape[0]
+    assemble(downs, held)
+    down = held[...].reshape(width, -1)
+    down_out[...] = down
+    branch_low = branch[...]
+    grad_hidden = (dot(branch_low, down) * slope[...]).astype(LOW)
     hidden_out[...] = grad_hidden
-    grad_two = dot(grad_hidden, up, 1, 1)
+    grad_two = dot(grad_hidden, up[...], 1, 1)
+    scaled, rate = norm_stats(middle[...])
     back = norm_back(grad_two, scaled, rate, vectors[1:2])
     low = back.astype(LOW)
     low_out[...] = low
@@ -227,7 +261,7 @@
     for j, out in enumerate((back1, back2, back3), 1):
         out[...] = fold_rows(dot(low, proj[j])).astype(LOW)
     first_tp = jnp.where(lax.axis_index("tp") == 0, 1.0, 0.0)
-    branch_sum = jnp.sum(branch, axis=0, keepdims=True) * first_tp
+    branch_sum = jnp.sum(branch_low.astype(F32), axis=0, keepdims=True) * first_tp
     sums[...] = jnp.concatenate(
         [
             jnp.sum(grad_two * scaled, axis=0, keepdims=True),
@@ -241,20 +275,38 @@
     )
 
 
-def ffn_grads_body(two, gelu, hidden, branch, down, sent, kept):
+def up_grads_body(two, hidden, low, branch, mix0, mix1, mix2, mix3, sent, kept, near, keep):
     ctx = lax.axis_index("ctx")
-    down_grad = dot(branch[...], gelu[...], 0, 0)
+    slots = two.shape[0]
     up_grad = dot(two[...], hidden[...], 0, 0)
+    half = up_grad.shape[1] // 2
 
     @pl.when(ctx == 0)
     def _():
-        kept[...] = down_grad
-        sent[...] = up_grad.astype(LOW)
+        kept[...] = up_grad[:, :half]
+        sent[...] = up_grad[:, half:].astype(LOW)
 
     @pl.when(ctx == 1)
     def _():
-        kept[...] = up_grad
-        sent[...] = down_grad.astype(LOW)
+        kept[...] = up_grad[:, half:]
+        sent[...] = up_grad[:, :half].astype(LOW)
+
+    first_tp = jnp.where(lax.axis_index("tp") == 0, 1.0, 0.0)
+    attn = (low[...].astype(F32) + first_tp * branch[...].astype(F32)).astype(LOW)
+    grads = [
+        dot(attn, unfold_rows(mix[...].astype(F32), slots).astype(LOW), 0, 0)
+        for mix in (mix0, mix1, mix2, mix3)
+    ]
+    near[...] = wide([grads[1], grads[3]]).astype(LOW)
+    keep[...] = wide([grads[0], grads[2]])
+
+
+def proj_half_body(keep, near, own, out):
+    cols = own.shape[1]
+    half = out.shape[0]
+    total = keep[...] + near[...].astype(F32)
+    own[...] = total[:, :cols]
+    out[...] = wide([total[:half, cols:], total[half:, cols:]]).astype(LOW)
 
 
 def ffn_rows_body(gelu, branch, low, middle, down, near, keep, own_middle, own_branch, chunks):
@@ -274,6 +326,22 @@
     own_middle[...] = chunks[0, :rows, :]
     to_chunks(branch[...].astype(F32), chunks)
     own_branch[...] = chunks[0, :rows, :]
+
+
+def rows_half_body(keep, near, out):
+    for i, j in ((0, 1), (1, 3)):
+        out[i] = (keep[2 + i] + near[j].astype(F32)).astype(LOW)
+
+
+def rows_body(counts, keep, near, far, own_middle, own_branch, vectors, layer_out, middle_grad):
+    own, _ = own_other(counts)
+    rows = layer_out.shape[0]
+    ids = lax.broadcasted_iota(jnp.int32, (rows, 1), 0) + lax.axis_index("tp") * rows
+    mlp = keep[0] + near[0].astype(F32) + far[0].astype(F32)
+    value = own_middle[...] + mlp[:rows] + vectors[5:6]
+    layer_out[...] = jnp.where(ids < own, value, 0.0).astype(LOW)
+    back = keep[1] + near[2].astype(F32) + far[1].astype(F32)
+    middle_grad[...] = own_branch[...] + back[:rows]
 
 
 def attend_back_body(
@@ -345,30 +413,30 @@
 
 
 def head_grads_body(
-    own, other, normed_own, normed_other, mixed, attn0, attn1, attn2, attn3, sent, kept, chunks
+    own, other, normed_own, normed_other, proj_own, proj_far, sums, sent, kept
 ):
     ctx = lax.axis_index("ctx")
     hw = own.shape[1] // 3
-    to_chunks(unfold_rows(mixed[...].astype(F32), own.shape[0]), chunks)
-    proj_grad = 0.0
-    for j, attn in enumerate((attn0, attn1, attn2, attn3)):
-        proj_grad = proj_grad + dot(attn[...], chunks[j].astype(LOW), 0, 0)
+    rows = kept.shape[0]
+    far = jnp.concatenate([proj_far[:, :hw], proj_far[:, hw:]], axis=0)
+    proj_grad = proj_own[...] + far.astype(F32)
     from_own = dot(normed_own[...], own[...], 0, 0)
     from_other = dot(normed_other[...], other[...], 0, 0)
     k_grad = from_own[:, hw : 2 * hw] + from_other[:, :hw]
     v_grad = from_own[:, 2 * hw :] + from_other[:, hw:]
     early = wide([from_own[:, :hw], k_grad])
     late = wide([v_grad, proj_grad])
+    sent[rows:, :] = split_sums(sums[...])
 
     @pl.when(ctx == 0)
     def _():
         kept[...] = early
-        sent[...] = late.astype(LOW)
+        sent[:rows, :] = late.astype(LOW)
 
     @pl.when(ctx == 1)
     def _():
         kept[...] = late
-        sent[...] = early.astype(LOW)
+        sent[:rows, :] = early.astype(LOW)
 
 
 def fold_body(n, kept, got, own, *outs):
@@ -382,6 +450,23 @@
     own[...] = summed(shard)
     for k, out in enumerate(outs, 1):
         out[...] = summed((shard + k) % n).astype(LOW)
+
+
+def head_fold_body(n, kept, got, sums, own, own_sums, *outs):
+    shard = lax.axis_index("shard")
+    rows = own.shape[0]
+    total = sums[...] + joined_sums(got[n * rows :, :])
+    own_sums[...] = total
+    packed = split_sums(total)
+
+    def summed(owner):
+        at = pl.ds(pl.multiple_of(owner * rows, 16), rows)
+        return kept[at, :] + got[at, :].astype(F32)
+
+    own[...] = summed(shard)
+    for k, out in enumerate(outs, 1):
+        out[:rows, :] = summed((shard + k) % n).astype(LOW)
+        out[rows:, :] = packed
 
 
 def total_body(own, *refs):
@@ -393,15 +478,34 @@
     low[...] = value.astype(LOW)
 
 
-def ffn_finish_body(mine, other, up_grad, down_grad):
+def head_total_body(own, sums, *refs):
+    got, (total, low, total_sums) = refs[:-3], refs[-3:]
+    rows = own.shape[0]
+    value = own[...]
+    vectors = sums[...]
+    for ref in got:
+        value = value + ref[:rows, :].astype(F32)
+        vectors = vectors + joined_sums(ref[rows:, :])
+    total[...] = value
+    low[...] = value.astype(LOW)
+    total_sums[...] = vectors
+
+
+def ffn_finish_body(down_mine, down_other, up_mine, up_other, up_grad, down_grad):
     first = lax.axis_index("ctx") == 0
-    theirs = other[...].astype(F32)
-    down_grad[...] = jnp.where(first, mine[...], theirs)
-    up_grad[...] = jnp.where(first, theirs, mine[...])
-
-
-def head_finish_body(mine, other, qkv_grad, proj_grad):
+    half = up_mine.shape[1]
+    theirs = up_other[...].astype(F32)
+    mine = up_mine[...]
+    up_grad[:, :half] = jnp.where(first, mine, theirs)
+    up_grad[:, half:] = jnp.where(first, theirs, mine)
+    down_grad[...] = down_mine[...] + down_other[...].astype(F32)
+
+
+def finish_body(
+    n, mine, other, sums_near, sums_far, qkv_grad, proj_grad, gains, biases, heads, hidden
+):
     first = lax.axis_index("ctx") == 0
+    shard = lax.axis_index("shard")
     theirs = other[...].astype(F32)
     early = jnp.where(first, mine[...], theirs)
     late = jnp.where(first, theirs, mine[...])
@@ -410,36 +514,33 @@
     qkv_grad[1] = early[:, hw:]
     qkv_grad[2] = late[:, :hw]
     proj_grad[...] = late[:, hw:].T
-
-
-def rows_body(counts, keep, near, far, own_middle, own_branch, vectors, layer_out, middle_grad, attn):
-    own, _ = own_other(counts)
-    rows = layer_out.shape[0]
-    ids = lax.broadcasted_iota(jnp.int32, (rows, 1), 0) + lax.axis_index("tp") * rows
-    mlp = keep[0] + near[0].astype(F32) + far[0].astype(F32)
-    value = own_middle[...] + mlp[:rows] + vectors[5:6]
-    layer_out[...] = jnp.where(ids < own, value, 0.0).astype(LOW)
-    back = keep[1] + near[2].astype(F32) + far[1].astype(F32)
-    grad = own_branch[...] + back[:rows]
-    middle_grad[...] = grad
-    attn[...] = grad.astype(LOW)
-
-
-def halfway_body(keep, near, *outs):
-    for out, (i, j) in zip(outs, PAIRS[len(outs)]):
-        out[...] = (keep[i] + near[j].astype(F32)).astype(LOW).reshape(out.shape)
-
-
-def input_body(kept, near, from_tp, from_ctx, from_far, own_act, middle_grad, vectors, out):
+    shared = sums_near[...] + sums_far[...]
+    part = gains.shape[1]
+    own = 0.0
+    for g in range(n):
+        own = own + jnp.where(shard == g, shared[:, g * part : (g + 1) * part], 0.0)
+    gains[...] = own[0:2]
+    biases[...] = own[2:6]
+
+
+def input_half_body(keep, near, own, out):
+    own[0] = keep[0] + near[0].astype(F32)
+    own[1] = keep[2] + near[2].astype(F32)
+    out[0] = (keep[1] + near[1].astype(F32)).astype(LOW)
+    out[1] = (keep[3] + near[3].astype(F32)).astype(LOW)
+
+
+def input_cross_body(own, far, kept, out):
+    kept[...] = own[0] + far[0].astype(F32)
+    out[...] = (own[1] + far[1].astype(F32)).astype(LOW)
+
+
+def input_body(kept, cross, own_act, middle_grad, vectors, out):
     rows = out.shape[0]
-    grad = kept[0] + near[0].astype(F32) + from_tp[...].astype(F32)
-    grad = grad + from_ctx[...].astype(F32) + from_far[...].astype(F32)
+    grad = kept[...] + cross[...].astype(F32)
     scaled, rate = norm_stats(own_act[...])
     back = norm_back(grad[:rows], scaled, rate, vectors[0:1])
     out[...] = (middle_grad[...] + back).astype(LOW)
-
-
-PAIRS = {3: ((1, 1), (2, 2), (3, 3))}
 
 
 def per_device(
@@ -488,9 +589,8 @@
 
     def fetch(pack, pack_half):
         mine = [shift_by_ctx(pack, k) for k in range(1, (n - 1) // 2 + 1)]
-        middle = shift(pack_half, n // 2)
-        pairs = [x for m in mine for x in (m, over_ctx(m))]
-        return [pack] + pairs + [middle, over_ctx(middle)]
+        mine.append(shift(pack_half, n // 2))
+        return [pack] + mine + [over_ctx(jnp.concatenate(mine, axis=0))]
 
     def with_n(body):
         def run(*refs):
@@ -505,6 +605,9 @@
     def row_half(x):
         size = x.shape[0] // 2
         return lax.dynamic_slice_in_dim(x, ctx * size, size, 0)
+
+    def after(x, *others):
+        return lax.optimization_barrier((x, *others))[0]
 
     act = activations[0]
     rows = -(-(part + 6) // 32) * 32
@@ -513,14 +616,14 @@
         "pack",
         [shape((rows, width)), shape((rows // 2, width)), shape((slots, width // 2))],
         [qkv_weight, norm_gains, row_biases, proj_weight, act],
+        room=58,
     )
     half_far = over_ctx(act_half)
     half_near = over_tp(half_far, 1)
     pack_parts = fetch(pack, pack_half)
-    down_turned = down_weight.T
-    up_late, down_late, _ = lax.optimization_barrier((up_weight, down_turned, pack_parts[1]))
+    up_late = after(up_weight, half_far)
     up_parts = fetch(up_late, row_half(up_late))
-    down_late, _ = lax.optimization_barrier((down_late, up_parts[1]))
+    down_late = after(down_weight.T, up_parts[1])
     down_parts = fetch(down_late, row_half(down_late))
 
     weights, proj, vectors = call(
@@ -551,31 +654,64 @@
     )
     projs = spread_tp(proj)
     mixes = spread_tp(mixed)
-    (back0, back1, back2, back3, two, gelu, hidden, branch, low, middle, down, sums) = call(
-        with_n(middle_body),
-        "middle",
+    two, gelu, slope, branch, middle, up, proj_full = call(
+        with_n(hidden_body),
+        "hidden",
+        [
+            shape((slots, width)),
+            shape((slots, ff)),
+            shape((slots, ff), F32),
+            shape((slots, width)),
+            shape((slots, width), F32),
+            shape((width, ff)),
+            shape((n_tp, width, hw)),
+        ],
+        [slot_counts, act, *mixes, *projs, vectors, hidden_bias.reshape(1, ff), cotangent[0]]
+        + up_parts,
+        scalars=1,
+        scratch=[pltpu.VMEM((n, part, ff), LOW)],
+        cost=cost(1_500_000_000, 8_000_000, 1_000_000),
+    )
+    own, *outs = call(
+        with_n(down_grads_body),
+        "down_grads",
+        [shape((part, ff), F32)] + [shape((part, ff))] * (n - 1),
+        [branch, gelu],
+        scratch=[pltpu.VMEM((width, ff), F32)],
+        cost=cost(600_000_000, 3_000_000),
+    )
+    got = [shift(x, k) for k, x in enumerate(outs, 1)]
+    down_mine, low = call(
+        total_body, "down_total", [shape((part, ff), F32), shape((part, ff))], [own, *got]
+    )
+    down_other = over_ctx(low)
+    back0, back1, back2, back3, hidden, low, down, sums = call(
+        with_n(middle_back_body),
+        "middle_back",
         [shape((fold, 2 * hw), F32)]
         + [shape((fold, 2 * hw))] * 3
-        + [shape((slots, width)), shape((slots, ff)), shape((slots, ff))]
-        + [shape((slots, width))] * 2
-        + [shape((slots, width), F32), shape((width, ff)), shape((8, width), F32)],
-        [slot_counts, act, *mixes, *projs, vectors, hidden_bias.reshape(1, ff), cotangent[0]]
-        + up_parts
-        + down_parts,
-        scalars=1,
-        scratch=[pltpu.VMEM((n, part, ff), LOW), pltpu.VMEM((n_tp, width, hw), LOW)],
-        cost=cost(4_000_000_000, 16_000_000, 1_000_000),
+        + [shape((slots, ff)), shape((slots, width)), shape((width, ff)), shape((8, width), F32)],
+        [branch, slope, up, middle, vectors, proj_full] + down_parts,
+        scratch=[pltpu.VMEM((n, part, ff), LOW)],
+        cost=cost(2_000_000_000, 8_000_000),
     )
     back1 = over_tp(back1, 1)
     back2 = (back2.astype(F32) + over_tp(back3, 1).astype(F32)).astype(LOW)
     back2 = over_tp(back2, 2)
-    sent, kept = call(
-        ffn_grads_body,
-        "ffn_grads",
-        [shape((width, ff)), shape((width, ff), F32)],
-        [two, gelu, hidden, branch, down],
+    sent, kept, proj_near, proj_keep = call(
+        up_grads_body,
+        "up_grads",
+        [
+            shape((width, ff // 2)),
+            shape((width, ff // 2), F32),
+            shape((width, 2 * hw)),
+            shape((width, 2 * hw), F32),
+        ],
+        [two, hidden, low, branch, *mixes],
         cost=cost(1_300_000_000, 7_000_000),
     )
+    up_got = over_ctx(sent)
+    proj_near = over_tp(proj_near, 1)
     near, keep, own_middle, own_branch = call(
         ffn_rows_body,
         "ffn_rows",
@@ -589,38 +725,34 @@
         scratch=[pltpu.VMEM((n_tp, padded, width), F32)],
         cost=cost(700_000_000, 7_000_000),
     )
-
-    def owned(sent, kept):
-        cols = kept.shape[1]
-        own, *outs = call(
-            with_n(fold_body),
-            "fold",
-            [shape((part, cols), F32)] + [shape((part, cols))] * (n - 1),
-            [kept, over_ctx(sent)],
-        )
-        got = [shift(x, k) for k, x in enumerate(outs, 1)]
-        total, low = call(
-            total_body, "total", [shape((part, cols), F32), shape((part, cols))], [own, *got]
-        )
-        return [total, over_ctx(low)]
-
-    ffn_totals = owned(sent, kept)
-    near = over_tp(near, 1)
-    far = jnp.stack(
-        [
-            (keep[2] + near[1].astype(F32)).astype(LOW),
-            (keep[3] + near[3].astype(F32)).astype(LOW),
-        ]
-    )
+    proj_own, proj_far = call(
+        proj_half_body,
+        "proj_half",
+        [shape((width, hw), F32), shape((width // 2, 2 * hw))],
+        [proj_keep, proj_near],
+    )
+    proj_far = over_tp(after(proj_far, back2), 2)
+    near = over_tp(after(near, back2), 1)
+    (far,) = call(rows_half_body, "rows_half", [shape((2, padded, width))], [keep, near])
     far = over_tp(far, 2)
-    layer_out, middle_grad, attn = call(
+    layer_out, middle_grad = call(
         rows_body,
         "rows",
-        [shape((quarter, width)), shape((quarter, width), F32), shape((quarter, width))],
+        [shape((quarter, width)), shape((quarter, width), F32)],
         [slot_counts, keep, near, far, own_middle, own_branch, vectors],
         scalars=1,
     )
-    attns = spread_tp(attn)
+    up_own, *outs = call(
+        with_n(fold_body),
+        "up_fold",
+        [shape((part, ff // 2), F32)] + [shape((part, ff // 2))] * (n - 1),
+        [kept, up_got],
+    )
+    got = [shift(x, k) for k, x in enumerate(outs, 1)]
+    up_mine, low = call(
+        total_body, "up_total", [shape((part, ff // 2), F32), shape((part, ff // 2))], [up_own, *got]
+    )
+    up_other = over_ctx(low)
 
     own_grads, other_grads, near, keep, own_act, sums = call(
         attend_back_body,
@@ -637,49 +769,67 @@
         scratch=[pltpu.VMEM((n_tp, padded, width), F32)],
         cost=cost(4_000_000_000, 16_000_000),
     )
-    near = over_tp(near, 1)
     sent, kept = call(
         head_grads_body,
         "head_grads",
-        [shape((width, 2 * hw)), shape((width, 2 * hw), F32)],
-        [own_grads, other_grads, normed_own, normed_other, mixed, *attns],
-        scratch=[pltpu.VMEM((n_tp, quarter, hw), F32)],
+        [shape((width + 32, 2 * hw)), shape((width, 2 * hw), F32)],
+        [own_grads, other_grads, normed_own, normed_other, proj_own, proj_far, sums],
         cost=cost(1_000_000_000, 6_000_000),
     )
-    head_totals = owned(sent, kept)
-    to_tp, to_ctx, to_far = call(
-        halfway_body, "halfway", [shape((padded, width))] * 3, [keep, near]
-    )
-    from_tp = over_tp(to_tp, 2)
-    from_ctx = over_ctx(to_ctx)
-    pairs = [(i, i ^ (n_tp + 2)) for i in range(n_ctx * n_tp)]
-    from_far = lax.ppermute(to_far, ("ctx", "tp"), pairs)
+    head_own, head_sums, *outs = call(
+        with_n(head_fold_body),
+        "head_fold",
+        [shape((part, 2 * hw), F32), shape((8, width), F32)]
+        + [shape((part + 32, 2 * hw))] * (n - 1),
+        [kept, over_ctx(sent), sums],
+    )
+    got = [shift(x, k) for k, x in enumerate(outs, 1)]
+    head_mine, low, head_sums = call(
+        head_total_body,
+        "head_total",
+        [shape((part, 2 * hw), F32), shape((part, 2 * hw)), shape((8, width), F32)],
+        [head_own, head_sums, *got],
+    )
+    head_other = over_ctx(low)
+    sums_near = head_sums + over_tp(head_sums, 1)
+    sums_far = over_tp(sums_near, 2)
+
+    near = over_tp(near, 1)
+    own, far = call(
+        input_half_body,
+        "input_half",
+        [shape((2, padded, width), F32), shape((2, padded, width))],
+        [keep, near],
+    )
+    kept, cross = call(
+        input_cross_body,
+        "input_cross",
+        [shape((padded, width), F32), shape((padded, width))],
+        [own, over_tp(far, 2)],
+    )
     (input_grad,) = call(
         input_body,
         "input",
         [shape((quarter, width))],
-        [keep, near, from_tp, from_ctx, from_far, own_act, middle_grad, vectors],
+        [kept, over_ctx(cross), own_act, middle_grad, vectors],
     )
     up_grad, down_grad = call(
-        ffn_finish_body, "ffn_finish", [shape((part, ff), F32), shape((part, ff), F32)], ffn_totals
-    )
-    qkv_grad, proj_grad = call(
-        head_finish_body,
-        "head_finish",
-        [shape((3, part, hw), F32), shape((hw, part), F32)],
-        head_totals,
-    )
-
-    shared = sums[:6]
-    for bit in (1, 2):
-        shared = shared + over_tp(shared, bit)
-    sums = jnp.concatenate([shared, sums[6:]])
-    sums = sums + over_ctx(sums)
-    bit = 1
-    while bit < n:
-        sums = sums + lax.ppermute(sums, "shard", [(i, i ^ bit) for i in range(n)])
-        bit *= 2
-    vector_grads = lax.dynamic_slice_in_dim(sums[:6], lax.axis_index("shard") * part, part, 1)
+        ffn_finish_body,
+        "ffn_finish",
+        [shape((part, ff), F32), shape((part, ff), F32)],
+        [down_mine, down_other, up_mine, up_other],
+    )
+    qkv_grad, proj_grad, gains_grad, biases_grad = call(
+        with_n(lambda n, *refs: finish_body(n, *refs, None, None)),
+        "finish",
+        [
+            shape((3, part, hw), F32),
+            shape((hw, part), F32),
+            shape((2, part), F32),
+            shape((4, part), F32),
+        ],
+        [head_mine, head_other, sums_near, sums_far],
+    )
     return (
         layer_out[None],
         input_grad[None],
@@ -687,10 +837,10 @@
         proj_grad,
         up_grad,
         down_grad.T,
-        vector_grads[:2],
-        vector_grads[2:],
-        sums[7, : 2 * hw].reshape(2, hw),
-        sums[6],
+        gains_grad,
+        biases_grad,
+        head_sums[7, : 2 * hw].reshape(2, hw),
+        head_sums[6],
     )
 
 

time: 188 us -> 167 us (0.89)
  local copies, waits for them, and re-layouts: 16.3 us -> 1.35 us
  Pallas kernels: 42.5 us -> 38.2 us
    ppermute x9 -> x12, waiting for transfers between devices: 18.7 us -> 42 us  [shift(): return lax.ppermute(x, 'shard', [(i, (i + k) % n) for i in range(n)])]
    ppermute x3 -> x0, waiting for transfers between devices: 15 us -> none  [the longest x2 11.8 us: per_device(): sums = sums + lax.ppermute(sums, 'shard', [(i, i ^ bit) for i in range(n)])]
    unnamed x52 -> x16, local copies, waits for them, and re-layouts: 12 us -> 0.04 us
    ppermute x13 -> x10, starting transfers between devices: 13.2 us -> 7.81 us  [over_ctx(): return lax.ppermute(x, 'ctx', [(i, i ^ 1) for i in range(n_ctx)])]
    pallas_call x17 -> x23, Pallas kernels: 42.5 us -> 38.2 us  [call(): pl.pallas_call(body, name=name, out_shape=out, in_specs=[SMEM] * scalars...]
    ppermute x9 -> x12, starting transfers between devices: 19.7 us -> 23.6 us  [shift(): return lax.ppermute(x, 'shard', [(i, (i + k) % n) for i in range(n)])]
    ppermute x13 -> x10, waiting for transfers between devices: 19.9 us -> 16 us  [over_ctx(): return lax.ppermute(x, 'ctx', [(i, i ^ 1) for i in range(n_ctx)])]
    ppermute x19 -> x18, waiting for transfers between devices: 16 us -> 12.6 us  [over_tp(): return lax.ppermute(x, 'tp', [(i, i ^ bit) for i in range(n_tp)])]
  transfers between devices with their start and end apart: 47 -> 43, of which waited for: 18 -> 17; matrix products, arithmetic and copies ran while one was open for 3% -> 1% of each run, Pallas kernels for 17% -> 19%
where the time goes in v4:
time: 167 us
  waiting for transfers between devices  78.1 us (47%)
  starting transfers between devices  47.1 us (28%)
  Pallas kernels  38.2 us (23%)
    ppermute x12, waiting for transfers between devices, shift(): return lax.ppermute(x, 'shard', [(i, (i + k) % n) for i in range(n)])  42 us
    pallas_call x23, Pallas kernels, call(): pl.pallas_call(body, name=name, out_shape=out, in_specs=[SMEM] * scalars...  38.2 us
    ppermute x12, starting transfers between devices, shift(): return lax.ppermute(x, 'shard', [(i, (i + k) % n) for i in range(n)])  23.6 us
    ppermute x10, waiting for transfers between devices, over_ctx(): return lax.ppermute(x, 'ctx', [(i, i ^ 1) for i in range(n_ctx)])  16 us
    ppermute x18, waiting for transfers between devices, over_tp(): return lax.ppermute(x, 'tp', [(i, i ^ bit) for i in range(n_tp)])  12.6 us
    ppermute x18, starting transfers between devices, over_tp(): return lax.ppermute(x, 'tp', [(i, i ^ bit) for i in range(n_tp)])  11.7 us
    ppermute x10, starting transfers between devices, over_ctx(): return lax.ppermute(x, 'ctx', [(i, i ^ 1) for i in range(n_ctx)])  7.81 us
    ppermute x3, waiting for transfers between devices, shift_by_ctx(): return lax.ppermute(x, ('shard', 'ctx'), moves)  7.52 us
  transfers between devices with their start and end apart: 43, of which 17 were waited for; matrix products, arithmetic and copies ran while one was open for 1% of the time, Pallas kernels for 19%

profile of v4, /device:TPU:0, one launch (start us, length us, event | category | flops | bytes accessed | tf_op | source)
XLA Modules:
  0.0 166.7 jit_solution(12981513804255209501)
XLA Ops:
  0.7 2.5 %pack.1 = (bf16[224,768]{1,0:T(8,128)(2,1)}, bf16[112,768]{1,0:T(8,128)(2,1)}, bf16[520,384]{1,0:T(8,128)(2,1)}) custom-call(bf16[3,192,192]{2,1,0:T(8,128)(2,1)} %qkv.1, bf16[2,192]{1,0:T(2,128)(2,1)} %gains.1, bf16[4,192]{1,0:T(4,128)(2,1)} %biases.2, bf16[192,192]{1,0:T(8,128)(2,1)} %proj.1, bf16[520,768]{1,0:T(8,128)(2,1)} %bitcast.6), custom_call_target="tpu_custom_call" | custom-call | tf_op jit(solution)/shard_map/pack/pallas_call | solution.py:24
  3.2 3.1 %collective-permute-start.2 = (bf16[224,768]{1,0:T(8,128)(2,1)}, bf16[224,768]{1,0:T(8,128)(2,1)S(1)}, u32[]{:S(2)}, u32[]{:S(2)}) collective-permute-start(bf16[224,768]{1,0:T(8,128)(2,1)} %get-tuple-element.96.refs_0_), channel_id=1, source_target_pairs={{0,8},{4,28},{8,16},{12,4},{16,24},{20,12},{24,0},{28,20},{1,9},{5... | collective-permute-start | bytes 1032200 | tf_op jit(solution)/shard_map/ppermute | solution.py:588
  6.2 2.6 %collective-permute-start.3 = (bf16[112,768]{1,0:T(8,128)(2,1)}, bf16[112,768]{1,0:T(8,128)(2,1)S(1)}, u32[]{:S(2)}, u32[]{:S(2)}) collective-permute-start(bf16[112,768]{1,0:T(8,128)(2,1)} %get-tuple-element.97), channel_id=1, source_target_pairs={{0,16},{8,24},{16,0},{24,8},{1,17},{9,25},{17,1},{25,9},{2,18},{10... | collective-permute-start | bytes 516104 | tf_op jit(solution)/shard_map/ppermute | solution.py:580
  9.8 14.1 %collective-permute-done.3.refs_2_ = bf16[112,768]{1,0:T(8,128)(2,1)S(1)} collective-permute-done((bf16[112,768]{1,0:T(8,128)(2,1)}, bf16[112,768]{1,0:T(8,128)(2,1)S(1)}, u32[]{:S(2)}, u32[]{:S(2)}) %collective-permute-start.3) | collective-permute-done | bytes 172064 | tf_op jit(solution)/shard_map/ppermute | solution.py:580
  26.3 3.3 %collective-permute-start.12 = (bf16[96,768]{1,0:T(8,128)(2,1)S(1)}, bf16[96,768]{1,0:T(8,128)(2,1)S(1)}, u32[]{:S(2)}, u32[]{:S(2)}) collective-permute-start(bf16[96,768]{1,0:T(8,128)(2,1)S(1)} %constant_dynamic-slice_fusion.1), channel_id=1, source_target_pairs={{0,16},{8,24},{16,0},{24,8},{1,17},{9,25},{17,1},{25,9},{2,18},{10... | collective-permute-start | bytes 442376 | tf_op jit(solution)/shard_map/ppermute | solution.py:580
  29.7 7.5 %collective-permute-done.11.refs_14_ = bf16[192,768]{1,0:T(8,128)(2,1)S(1)} collective-permute-done((bf16[192,768]{1,0:T(8,128)(2,1)S(1)}, bf16[192,768]{1,0:T(8,128)(2,1)S(1)}, u32[]{:S(2)}, u32[]{:S(2)}) %collective-permute-start.11) | collective-permute-done | bytes 294944 | tf_op jit(solution)/shard_map/ppermute | solution.py:588
  40.8 7.5 %attend.1 = (bf16[264,384]{1,0:T(8,128)(2,1)S(1)}, f32[192,520]{1,0:T(8,128)S(1)}, f32[520,8]{1,0:T(8,128)S(1)}, bf16[520,768]{1,0:T(8,128)(2,1)S(1)}, bf16[520,...) custom-call(s32[1,2]{1,0:T(1,128)S(1)} %copy-done.4, ...), custom_call_target="tpu_custom_call" | custom-call | flops 3000000000 | bytes 12000000 | tf_op jit(solution)/shard_map/attend/pallas_call | solution.py:24
  48.9 2.5 %collective-permute-done.12.refs_15_ = bf16[96,768]{1,0:T(8,128)(2,1)S(1)} collective-permute-done((bf16[96,768]{1,0:T(8,128)(2,1)S(1)}, bf16[96,768]{1,0:T(8,128)(2,1)S(1)}, u32[]{:S(2)}, u32[]{:S(2)}) %collective-permute-start.12) | collective-permute-done | bytes 147488 | tf_op jit(solution)/shard_map/ppermute | solution.py:580
  51.4 3.0 %collective-permute-done.15.refs_8_ = bf16[96,768]{1,0:T(8,128)(2,1)S(1)} collective-permute-done((bf16[96,768]{1,0:T(8,128)(2,1)S(1)}, bf16[96,768]{1,0:T(8,128)(2,1)S(1)}, u32[]{:S(2)}, u32[]{:S(2)}) %collective-permute-start.15) | collective-permute-done | bytes 147488 | tf_op jit(solution)/shard_map/ppermute | solution.py:580
  56.1 8.4 %collective-permute-done.13.refs_16_ = bf16[288,768]{1,0:T(8,128)(2,1)S(1)} collective-permute-done((bf16[288,768]{1,0:T(8,128)(2,1)S(1)}, bf16[288,768]{1,0:T(8,128)(2,1)S(1)}, u32[]{:S(2)}, u32[]{:S(2)}) %collective-permute-start.13) | collective-permute-done | bytes 442400 | tf_op jit(solution)/shard_map/ppermute | solution.py:574
  64.5 3.6 %hidden.1 = (bf16[520,768]{1,0:T(8,128)(2,1)S(1)}, bf16[520,768]{1,0:T(8,128)(2,1)S(1)}, f32[520,768]{1,0:T(8,128)S(1)}, bf16[520,768]{1,0:T(8,128)(2,1)S(1)}, f...) custom-call(s32[1,2]{1,0:T(1,128)S(1)} %copy-done.4, ...), custom_call_target="tpu_custom_call" | custom-call | flops 1500000000 | bytes 8000000 | tf_op jit(solution)/shard_map/hidden/pallas_call | solution.py:24
  68.1 5.0 %collective-permute-done.16.refs_9_ = bf16[288,768]{1,0:T(8,128)(2,1)S(1)} collective-permute-done((bf16[288,768]{1,0:T(8,128)(2,1)S(1)}, bf16[288,768]{1,0:T(8,128)(2,1)S(1)}, u32[]{:S(2)}, u32[]{:S(2)}) %collective-permute-start.16) | collective-permute-done | bytes 442400 | tf_op jit(solution)/shard_map/ppermute | solution.py:574
  73.1 3.4 %middle_back.1 = (f32[264,384]{1,0:T(8,128)S(1)}, bf16[264,384]{1,0:T(8,128)(2,1)S(1)}, bf16[264,384]{1,0:T(8,128)(2,1)S(1)}, bf16[264,384]{1,0:T(8,128)(2,1)S(1...) custom-call(bf16[520,768]{1,0:T(8,128)(2,1)S(1)} %get-tuple-element., ...), custom_call_target="tpu_custom_call" | custom-call | flops 2000000000 | bytes 8000000 | tf_op jit(solution)/shard_map/middle_back/pallas_call | solution.py:24
  79.7 2.9 %up_grads.1 = (bf16[768,384]{1,0:T(8,128)(2,1)S(1)}, f32[768,384]{1,0:T(8,128)S(1)}, bf16[768,384]{1,0:T(8,128)(2,1)S(1)}, f32[768,384]{1,0:T(8,128)S(1)}) custom-call(bf16[520,768]{1,0:T(8,128)(2,1)S(1)} %get-tuple-element.142.two, bf16[520,768]{1,0:T(8,128)(2,1)S(1)} %get-tuple-element.143.hidden, bf16[520,768]{1,0:T(8,128)(2,1)S(1)} %get-tuple-element.110.low, ...), custom_call_target="tpu_custom_call" | custom-call | flops 1300000000 | bytes 7000000 | tf_op jit(solution)/shard_map/up_grads/pallas_call | solution.py:24
  83.0 2.2 %collective-permute-done.18.back2 = bf16[264,384]{1,0:T(8,128)(2,1)S(1)} collective-permute-done((bf16[264,384]{1,0:T(8,128)(2,1)S(1)}, bf16[264,384]{1,0:T(8,128)(2,1)S(1)}, u32[]{:S(2)}, u32[]{:S(2)}) %collective-permute-start.18) | collective-permute-done | bytes 202784 | tf_op jit(solution)/shard_map/ppermute | solution.py:577
  85.2 7.8 %attend_back.1 = (bf16[520,576]{1,0:T(8,128)(2,1)S(1)}, bf16[520,384]{1,0:T(8,128)(2,1)S(1)}, bf16[4,136,768]{2,1,0:T(8,128)(2,1)S(1)}, f32[4,136,768]{2,1,0:T(8...) custom-call(f32[264,384]{1,0:T(8,128)S(1)} %get-tuple-element.120.back0, ...), custom_call_target="tpu_custom_call" | custom-call | flops 4000000000 | bytes 16000000 | tf_op jit(solution)/shard_map/attend_back/pallas_call | solution.py:24
  98.3 9.0 %collective-permute-done.34.refs_0_ = bf16[192,768]{1,0:T(8,128)(2,1)S(1)} collective-permute-done((bf16[192,768]{1,0:T(8,128)(2,1)S(1)}, bf16[192,768]{1,0:T(8,128)(2,1)S(1)}, u32[]{:S(2)}, u32[]{:S(2)}) %collective-permute-start.34) | collective-permute-done | bytes 294944 | tf_op jit(solution)/shard_map/ppermute | solution.py:580
  107.3 2.0 %collective-permute-start.36 = (bf16[192,768]{1,0:T(8,128)(2,1)S(1)}, bf16[192,768]{1,0:T(8,128)(2,1)S(1)}, u32[]{:S(2)}, u32[]{:S(2)}) collective-permute-start(bf16[192,768]{1,0:T(8,128)(2,1)S(1)} %get-tuple-element.165), channel_id=1, source_target_pairs={{0,24},{8,0},{16,8},{24,16},{1,25},{9,1},{17,9},{25,17},{2,26},{10... | collective-permute-start | bytes 884744 | tf_op jit(solution)/shard_map/ppermute | solution.py:580
  111.6 9.3 %collective-permute-done.35.refs_1_ = bf16[192,768]{1,0:T(8,128)(2,1)S(1)} collective-permute-done((bf16[192,768]{1,0:T(8,128)(2,1)S(1)}, bf16[192,768]{1,0:T(8,128)(2,1)S(1)}, u32[]{:S(2)}, u32[]{:S(2)}) %collective-permute-start.35) | collective-permute-done | bytes 294944 | tf_op jit(solution)/shard_map/ppermute | solution.py:580
  121.0 5.9 %collective-permute-start.39 = (bf16[192,384]{1,0:T(8,128)(2,1)S(1)}, bf16[192,384]{1,0:T(8,128)(2,1)S(1)}, u32[]{:S(2)}, u32[]{:S(2)}) collective-permute-start(bf16[192,384]{1,0:T(8,128)(2,1)S(1)} %get-tuple-element.171), channel_id=1, source_target_pairs={{0,8},{8,16},{16,24},{24,0},{1,9},{9,17},{17,25},{25,1},{2,10},{10... | collective-permute-start | bytes 442376 | tf_op jit(solution)/shard_map/ppermute | solution.py:580
  126.9 3.4 %collective-permute-start.40 = (bf16[192,384]{1,0:T(8,128)(2,1)S(1)}, bf16[192,384]{1,0:T(8,128)(2,1)S(1)}, u32[]{:S(2)}, u32[]{:S(2)}) collective-permute-start(bf16[192,384]{1,0:T(8,128)(2,1)S(1)} %get-tuple-element.172), channel_id=1, source_target_pairs={{0,16},{8,24},{16,0},{24,8},{1,17},{9,25},{17,1},{25,9},{2,18},{10... | collective-permute-start | bytes 442376 | tf_op jit(solution)/shard_map/ppermute | solution.py:580
  130.4 4.0 %collective-permute-done.39.refs_0_ = bf16[192,384]{1,0:T(8,128)(2,1)S(1)} collective-permute-done((bf16[192,384]{1,0:T(8,128)(2,1)S(1)}, bf16[192,384]{1,0:T(8,128)(2,1)S(1)}, u32[]{:S(2)}, u32[]{:S(2)}) %collective-permute-start.39) | collective-permute-done | bytes 147488 | tf_op jit(solution)/shard_map/ppermute | solution.py:580
  140.4 2.5 %collective-permute-start.42 = (bf16[192,384]{1,0:T(8,128)(2,1)S(1)}, bf16[192,384]{1,0:T(8,128)(2,1)S(1)}, u32[]{:S(2)}, u32[]{:S(2)}) collective-permute-start(bf16[192,384]{1,0:T(8,128)(2,1)S(1)} %get-tuple-element.175), channel_id=1, source_target_pairs={{0,4},{4,0},{1,5},{5,1},{2,6},{6,2},{3,7},{7,3},{8,12},{12,8},{9,1... | collective-permute-start | bytes 442376 | tf_op jit(solution)/shard_map/ppermute | solution.py:574
  150.9 5.9 %collective-permute-done.20.far = bf16[2,136,768]{2,1,0:T(8,128)(2,1)S(1)} collective-permute-done((bf16[2,136,768]{2,1,0:T(8,128)(2,1)S(1)}, bf16[2,136,768]{2,1,0:T(8,128)(2,1)S(1)}, u32[]{:S(2)}, u32[]{:S(2)}) %collective-permute-start.20) | collective-permute-done | bytes 417824 | tf_op jit(solution)/shard_map/ppermute | solution.py:577
  (112 shorter events, 44.3 us)
Async XLA Ops:
  3.2 20.7 %collective-permute-start.2 = (bf16[224,768]{1,0:T(8,128)(2,1)}, bf16[224,768]{1,0:T(8,128)(2,1)S(1)}, u32[]{:S(2)}, u32[]{:S(2)}) collective-permute-start(bf16[224,768]{1,0:T(8,128)(2,1)} %get-tuple-element.96.refs_0_), channel_id=1, source_target_pairs={{0,8},{4,28},{8,16},{12,4},{16,24},{20,12},{24,0},{28,20},{1,9},{5... | collective-permute-start | bytes 1032200 | tf_op jit(solution)/shard_map/ppermute | solution.py:588
  6.2 17.7 %collective-permute-start.3 = (bf16[112,768]{1,0:T(8,128)(2,1)}, bf16[112,768]{1,0:T(8,128)(2,1)S(1)}, u32[]{:S(2)}, u32[]{:S(2)}) collective-permute-start(bf16[112,768]{1,0:T(8,128)(2,1)} %get-tuple-element.97), channel_id=1, source_target_pairs={{0,16},{8,24},{16,0},{24,8},{1,17},{9,25},{17,1},{25,9},{2,18},{10... | collective-permute-start | bytes 516104 | tf_op jit(solution)/shard_map/ppermute | solution.py:580
  8.8 16.6 %collective-permute-start = (bf16[520,384]{1,0:T(8,128)(2,1)}, bf16[520,384]{1,0:T(8,128)(2,1)S(1)}, u32[]{:S(2)}, u32[]{:S(2)}) collective-permute-start(bf16[520,384]{1,0:T(8,128)(2,1)} %get-tuple-element.95), channel_id=1, source_target_pairs={{0,4},{4,0},{1,5},{5,1},{2,6},{6,2},{3,7},{7,3},{8,12},{12,8},{9,1... | collective-permute-start | bytes 1198088 | tf_op jit(solution)/shard_map/ppermute | solution.py:574
  24.7 14.2 %collective-permute-start.4 = (bf16[336,768]{1,0:T(8,128)(2,1)}, bf16[336,768]{1,0:T(8,128)(2,1)S(1)}, u32[]{:S(2)}, u32[]{:S(2)}) collective-permute-start(bf16[336,768]{1,0:T(8,128)(2,1)} %pad_maximum_fusion), channel_id=1, source_target_pairs={{0,4},{4,0},{1,5},{5,1},{2,6},{6,2},{3,7},{7,3},{8,12},{12,8},{9,1... | collective-permute-start | bytes 1548296 | tf_op jit(solution)/shard_map/ppermute | solution.py:574
  26.3 14.4 %collective-permute-start.1 = (bf16[520,384]{1,0:T(8,128)(2,1)S(1)}, bf16[520,384]{1,0:T(8,128)(2,1)}, u32[]{:S(2)}, u32[]{:S(2)}) collective-permute-start(bf16[520,384]{1,0:T(8,128)(2,1)S(1)} %collective-permute-done.half_far), channel_id=1, source_target_pairs={{0,1},{1,0},{2,3},{3,2},{4,5},{5,4},{6,7},{7,6},{8,9},{9,8},{10,11... | collective-permute-start | bytes 1198088 | tf_op jit(solution)/shard_map/ppermute | solution.py:577
  26.3 25.0 %collective-permute-start.12 = (bf16[96,768]{1,0:T(8,128)(2,1)S(1)}, bf16[96,768]{1,0:T(8,128)(2,1)S(1)}, u32[]{:S(2)}, u32[]{:S(2)}) collective-permute-start(bf16[96,768]{1,0:T(8,128)(2,1)S(1)} %constant_dynamic-slice_fusion.1), channel_id=1, source_target_pairs={{0,16},{8,24},{16,0},{24,8},{1,17},{9,25},{17,1},{25,9},{2,18},{10... | collective-permute-start | bytes 442376 | tf_op jit(solution)/shard_map/ppermute | solution.py:580
  37.2 17.4 %collective-permute-start.14 = (bf16[192,768]{1,0:T(8,128)(2,1)S(1)}, bf16[192,768]{1,0:T(8,128)(2,1)S(1)}, u32[]{:S(2)}, u32[]{:S(2)}) collective-permute-start(bf16[192,768]{1,0:T(8,128)(2,1)S(1)} %bitcast.10), channel_id=1, source_target_pairs={{0,8},{4,28},{8,16},{12,4},{16,24},{20,12},{24,0},{28,20},{1,9},{5... | collective-permute-start | bytes 884744 | tf_op jit(solution)/shard_map/ppermute | solution.py:588
  37.2 17.3 %collective-permute-start.15 = (bf16[96,768]{1,0:T(8,128)(2,1)S(1)}, bf16[96,768]{1,0:T(8,128)(2,1)S(1)}, u32[]{:S(2)}, u32[]{:S(2)}) collective-permute-start(bf16[96,768]{1,0:T(8,128)(2,1)S(1)} %constant_dynamic-slice_fusion), channel_id=1, source_target_pairs={{0,16},{8,24},{16,0},{24,8},{1,17},{9,25},{17,1},{25,9},{2,18},{10... | collective-permute-start | bytes 442376 | tf_op jit(solution)/shard_map/ppermute | solution.py:580
  39.2 16.0 %collective-permute-start.9 = (bf16[384,384]{1,0:T(8,128)(2,1)S(1)}, bf16[384,384]{1,0:T(8,128)(2,1)S(1)}, u32[]{:S(2)}, u32[]{:S(2)}) collective-permute-start(bf16[384,384]{1,0:T(8,128)(2,1)S(1)} %get-tuple-element.101.refs_6_), channel_id=1, source_target_pairs={{0,2},{1,3},{2,0},{3,1},{4,6},{5,7},{6,4},{7,5},{8,10},{9,11},{10,... | collective-permute-start | bytes 884744 | tf_op jit(solution)/shard_map/ppermute | solution.py:577
  51.4 13.1 %collective-permute-start.13 = (bf16[288,768]{1,0:T(8,128)(2,1)S(1)}, bf16[288,768]{1,0:T(8,128)(2,1)S(1)}, u32[]{:S(2)}, u32[]{:S(2)}) collective-permute-start(bf16[288,768]{1,0:T(8,128)(2,1)S(1)} %pad_maximum_fusion.1), channel_id=1, source_target_pairs={{0,4},{4,0},{1,5},{5,1},{2,6},{6,2},{3,7},{7,3},{8,12},{12,8},{9,1... | collective-permute-start | bytes 1327112 | tf_op jit(solution)/shard_map/ppermute | solution.py:574
  54.6 18.5 %collective-permute-start.16 = (bf16[288,768]{1,0:T(8,128)(2,1)S(1)}, bf16[288,768]{1,0:T(8,128)(2,1)S(1)}, u32[]{:S(2)}, u32[]{:S(2)}) collective-permute-start(bf16[288,768]{1,0:T(8,128)(2,1)S(1)} %pad_maximum_fusion.2), channel_id=1, source_target_pairs={{0,4},{4,0},{1,5},{5,1},{2,6},{6,2},{3,7},{7,3},{8,12},{12,8},{9,1... | collective-permute-start | bytes 1327112 | tf_op jit(solution)/shard_map/ppermute | solution.py:574
  82.6 14.0 %collective-permute-start.25 = (bf16[768,384]{1,0:T(8,128)(2,1)S(1)}, bf16[768,384]{1,0:T(8,128)(2,1)S(1)}, u32[]{:S(2)}, u32[]{:S(2)}) collective-permute-start(bf16[768,384]{1,0:T(8,128)(2,1)S(1)} %get-tuple-element.145), channel_id=1, source_target_pairs={{0,1},{1,0},{2,3},{3,2},{4,5},{5,4},{6,7},{7,6},{8,9},{9,8},{10,11... | collective-permute-start | bytes 1769480 | tf_op jit(solution)/shard_map/ppermute | solution.py:577
  82.7 28.5 %collective-permute-start.38 = (bf16[768,384]{1,0:T(8,128)(2,1)S(1)}, bf16[768,384]{1,0:T(8,128)(2,1)S(1)}, u32[]{:S(2)}, u32[]{:S(2)}) collective-permute-start(bf16[768,384]{1,0:T(8,128)(2,1)S(1)} %get-tuple-element.169), channel_id=1, source_target_pairs={{0,4},{4,0},{1,5},{5,1},{2,6},{6,2},{3,7},{7,3},{8,12},{12,8},{9,1... | collective-permute-start | bytes 1769480 | tf_op jit(solution)/shard_map/ppermute | solution.py:574
  93.0 42.6 %collective-permute-start.22 = (bf16[4,136,768]{2,1,0:T(8,128)(2,1)S(1)}, bf16[4,136,768]{2,1,0:T(8,128)(2,1)S(1)}, u32[]{:S(2)}, u32[]{:S(2)}) collective-permute-start(bf16[4,136,768]{2,1,0:T(8,128)(2,1)S(1)} %get-tuple-element.131), channel_id=1, source_target_pairs={{0,1},{1,0},{2,3},{3,2},{4,5},{5,4},{6,7},{7,6},{8,9},{9,8},{10,11... | collective-permute-start | bytes 2506760 | tf_op jit(solution)/shard_map/ppermute | solution.py:577
  94.7 42.9 %collective-permute-start.19 = (bf16[4,136,768]{2,1,0:T(8,128)(2,1)S(1)}, bf16[4,136,768]{2,1,0:T(8,128)(2,1)S(1)}, u32[]{:S(2)}, u32[]{:S(2)}) collective-permute-start(bf16[4,136,768]{2,1,0:T(8,128)(2,1)S(1)} %get-tuple-element.116), channel_id=1, source_target_pairs={{0,1},{1,0},{2,3},{3,2},{4,5},{5,4},{6,7},{7,6},{8,9},{9,8},{10,11... | collective-permute-start | bytes 2506760 | tf_op jit(solution)/shard_map/ppermute | solution.py:577
  107.3 13.7 %collective-permute-start.35 = (bf16[192,768]{1,0:T(8,128)(2,1)S(1)}, bf16[192,768]{1,0:T(8,128)(2,1)S(1)}, u32[]{:S(2)}, u32[]{:S(2)}) collective-permute-start(bf16[192,768]{1,0:T(8,128)(2,1)S(1)} %get-tuple-element.164), channel_id=1, source_target_pairs={{0,16},{8,24},{16,0},{24,8},{1,17},{9,25},{17,1},{25,9},{2,18},{10... | collective-permute-start | bytes 884744 | tf_op jit(solution)/shard_map/ppermute | solution.py:580
  107.3 19.6 %collective-permute-start.36 = (bf16[192,768]{1,0:T(8,128)(2,1)S(1)}, bf16[192,768]{1,0:T(8,128)(2,1)S(1)}, u32[]{:S(2)}, u32[]{:S(2)}) collective-permute-start(bf16[192,768]{1,0:T(8,128)(2,1)S(1)} %get-tuple-element.165), channel_id=1, source_target_pairs={{0,24},{8,0},{16,8},{24,16},{1,25},{9,1},{17,9},{25,17},{2,26},{10... | collective-permute-start | bytes 884744 | tf_op jit(solution)/shard_map/ppermute | solution.py:580
  111.1 31.8 %collective-permute-start.27 = (bf16[800,384]{1,0:T(8,128)(2,1)S(1)}, bf16[800,384]{1,0:T(8,128)(2,1)S(1)}, u32[]{:S(2)}, u32[]{:S(2)}) collective-permute-start(bf16[800,384]{1,0:T(8,128)(2,1)S(1)} %get-tuple-element.151), channel_id=1, source_target_pairs={{0,4},{4,0},{1,5},{5,1},{2,6},{6,2},{3,7},{7,3},{8,12},{12,8},{9,1... | collective-permute-start | bytes 1843208 | tf_op jit(solution)/shard_map/ppermute | solution.py:574
  121.0 13.5 %collective-permute-start.39 = (bf16[192,384]{1,0:T(8,128)(2,1)S(1)}, bf16[192,384]{1,0:T(8,128)(2,1)S(1)}, u32[]{:S(2)}, u32[]{:S(2)}) collective-permute-start(bf16[192,384]{1,0:T(8,128)(2,1)S(1)} %get-tuple-element.171), channel_id=1, source_target_pairs={{0,8},{8,16},{16,24},{24,0},{1,9},{9,17},{17,25},{25,1},{2,10},{10... | collective-permute-start | bytes 442376 | tf_op jit(solution)/shard_map/ppermute | solution.py:580
  137.6 12.6 %collective-permute-start.23 = (bf16[2,136,768]{2,1,0:T(8,128)(2,1)S(1)}, bf16[2,136,768]{2,1,0:T(8,128)(2,1)S(1)}, u32[]{:S(2)}, u32[]{:S(2)}) collective-permute-start(bf16[2,136,768]{2,1,0:T(8,128)(2,1)S(1)} %get-tuple-element.133), channel_id=1, source_target_pairs={{0,2},{1,3},{2,0},{3,1},{4,6},{5,7},{6,4},{7,5},{8,10},{9,11},{10,... | collective-permute-start | bytes 1253384 | tf_op jit(solution)/shard_map/ppermute | solution.py:577
  139.3 17.5 %collective-permute-start.20 = (bf16[2,136,768]{2,1,0:T(8,128)(2,1)S(1)}, bf16[2,136,768]{2,1,0:T(8,128)(2,1)S(1)}, u32[]{:S(2)}, u32[]{:S(2)}) collective-permute-start(bf16[2,136,768]{2,1,0:T(8,128)(2,1)S(1)} %rows_half.1), channel_id=1, source_target_pairs={{0,2},{1,3},{2,0},{3,1},{4,6},{5,7},{6,4},{7,5},{8,10},{9,11},{10,... | collective-permute-start | bytes 1253384 | tf_op jit(solution)/shard_map/ppermute | solution.py:577
  143.1 15.1 %collective-permute-start.28 = (bf16[224,384]{1,0:T(8,128)(2,1)S(1)}, bf16[224,384]{1,0:T(8,128)(2,1)S(1)}, u32[]{:S(2)}, u32[]{:S(2)}) collective-permute-start(bf16[224,384]{1,0:T(8,128)(2,1)S(1)} %get-tuple-element.154), channel_id=1, source_target_pairs={{0,8},{8,16},{16,24},{24,0},{1,9},{9,17},{17,25},{25,1},{2,10},{10... | collective-permute-start | bytes 516104 | tf_op jit(solution)/shard_map/ppermute | solution.py:580
  144.9 13.3 %collective-permute-start.29 = (bf16[224,384]{1,0:T(8,128)(2,1)S(1)}, bf16[224,384]{1,0:T(8,128)(2,1)S(1)}, u32[]{:S(2)}, u32[]{:S(2)}) collective-permute-start(bf16[224,384]{1,0:T(8,128)(2,1)S(1)} %get-tuple-element.155), channel_id=1, source_target_pairs={{0,16},{8,24},{16,0},{24,8},{1,17},{9,25},{17,1},{25,9},{2,18},{10... | collective-permute-start | bytes 516104 | tf_op jit(solution)/shard_map/ppermute | solution.py:580
  150.3 15.3 %collective-permute-start.24 = (bf16[136,768]{1,0:T(8,128)(2,1)S(1)}, bf16[136,768]{1,0:T(8,128)(2,1)S(1)}, u32[]{:S(2)}, u32[]{:S(2)}) collective-permute-start(bf16[136,768]{1,0:T(8,128)(2,1)S(1)} %get-tuple-element.135), channel_id=1, source_target_pairs={{0,4},{4,0},{1,5},{5,1},{2,6},{6,2},{3,7},{7,3},{8,12},{12,8},{9,1... | collective-permute-start | bytes 626696 | tf_op jit(solution)/shard_map/ppermute | solution.py:574
  (27 other events, 374.2 us)

commit v5 on v4

v5 whole, which is shorter than its diff:
```python
import functools
import math

import jax
import jax.numpy as jnp
from jax import lax
from jax.experimental import pallas as pl
from jax.experimental.pallas import tpu as pltpu
from jax.sharding import PartitionSpec as P

HD = 64
EPS = 1e-06
NEG = -1e30
F32 = jnp.float32
LOW = jnp.bfloat16
VMEM = pl.BlockSpec(memory_space=pltpu.VMEM)
SMEM = pl.BlockSpec(memory_space=pltpu.SMEM)


def shape(dims, dtype=LOW):
    return jax.ShapeDtypeStruct(dims, dtype)


def call(body, name, out, args, scalars, scratch, room, token, weight):
    count = len(args)

    def kernel(*refs):
        body(*refs[:count], *refs[count + (token is not None) :])

    specs = [SMEM] * scalars + [VMEM] * (count - scalars)
    if token is not None:
        specs.append(pl.BlockSpec(memory_space=pl.ANY))
        args = [*args, token]
    return pl.pallas_call(
        kernel,
        name=name,
        out_shape=out,
        in_specs=specs,
        out_specs=[VMEM] * len(out),
        scratch_shapes=list(scratch),
        compiler_params=pltpu.CompilerParams(vmem_limit_bytes=room * 2**20),
        cost_estimate=pl.CostEstimate(
            flops=weight * 10**9 + 1, bytes_accessed=weight * 10**6 + 1, transcendentals=0
        ),
    )(*args)


def dot(left, right, left_dim=1, right_dim=0):
    return lax.dot_general(
        left, right, (((left_dim,), (right_dim,)), ((), ())), preferred_element_type=F32
    )


def norm_stats(values):
    centred = values - jnp.mean(values, axis=-1, keepdims=True)
    rate = lax.rsqrt(jnp.mean(centred * centred, axis=-1, keepdims=True) + EPS)
    return centred * rate, rate


def norm_back(grad, scaled, rate, gain):
    e = grad * gain
    inner = jnp.mean(e * scaled, axis=-1, keepdims=True)
    return rate * (e - jnp.mean(e, axis=-1, keepdims=True) - scaled * inner)


def own_other(counts):
    ctx = lax.axis_index("ctx")
    first, second = counts[0, 0], counts[0, 1]
    return jnp.where(ctx == 0, first, second), jnp.where(ctx == 0, second, first)


def wide(blocks):
    return jnp.concatenate(blocks, axis=1)


def to_chunks(value, ref):
    tp = lax.axis_index("tp")
    count = ref.shape[0]
    rows = value.shape[0] // count
    for g in range(count):
        ref[tp ^ g, :rows, :] = value[g * rows : (g + 1) * rows].astype(ref.dtype)


def folded_rows(rows):
    return (rows // 2 + 7) // 8 * 8


def fold_rows(value):
    top = folded_rows(value.shape[0])
    rest = value[top:]
    pad = jnp.zeros((top - rest.shape[0], value.shape[1]), value.dtype)
    if pad.shape[0]:
        rest = jnp.concatenate([rest, pad], axis=0)
    return wide([value[:top], rest])


def unfold_rows(value, rows):
    cols = value.shape[1] // 2
    return jnp.concatenate([value[:, :cols], value[: rows - value.shape[0], cols:]], axis=0)


def pack_body(qkv, gains, biases, proj, act, pack, pack_half, act_half):
    part, hw = qkv.shape[1], qkv.shape[2]
    width = pack.shape[1]
    pack[:part, :] = wide([qkv[0], qkv[1], qkv[2], proj[...].T])
    spare = pack.shape[0] - part
    vectors = jnp.concatenate(
        [gains[...].astype(F32), biases[...].astype(F32), jnp.zeros((spare - 6, part), F32)],
        axis=0,
    )
    pack[part:, :] = wide([vectors, jnp.zeros((spare, width - part), F32)]).astype(LOW)
    size = pack_half.shape[0]
    at = pl.multiple_of(lax.axis_index("ctx") * size, 16)
    pack_half[...] = pack[pl.ds(at, size), :]
    size = act_half.shape[1]
    core = lax.axis_index("tp") % 2
    act_half[...] = act[:, pl.ds(pl.multiple_of(core * size, 128), size)]


def assemble(parts, held):
    n, rows, _ = held.shape
    shard, ctx = lax.axis_index("shard"), lax.axis_index("ctx")
    pairs = (n - 1) // 2
    held[shard] = parts[0][...]
    for k in range(1, pairs + 1):
        step = jnp.where(ctx == 0, n - k, k)
        held[(shard + step) % n] = parts[2 * k - 1][...]
        held[(shard + n - step) % n] = parts[2 * k][...]
    far = (shard + n // 2) % n
    size = rows // 2
    held[far, pl.ds(pl.multiple_of(ctx * size, 8), size), :] = parts[-2][...]
    held[far, pl.ds(pl.multiple_of((1 - ctx) * size, 8), size), :] = parts[-1][...]


def mark_body(value, out):
    out[...] = value[:8, :128].astype(F32)


def half_body(block, out):
    size = out.shape[0]
    at = pl.multiple_of(lax.axis_index("ctx") * size, 8)
    out[...] = block[pl.ds(at, size), :]


def add_body(kept, proj_kept, near, total, proj_total, out, proj_out):
    rows = out.shape[0]
    total[...] = kept[0] + near[:rows, :].astype(F32)
    out[...] = (kept[1] + near[rows : 2 * rows, :].astype(F32)).astype(LOW)
    both = proj_kept[...] + near[2 * rows :, :].astype(F32)
    cols = both.shape[1] // 2
    half = proj_out.shape[0]
    proj_total[...] = both[:, :cols]
    proj_out[...] = wide([both[:half, cols:], both[half:, cols:]]).astype(LOW)


def pair_body(*refs):
    row = 0
    for ref in refs[:-1]:
        refs[-1][row : row + ref.shape[0], :] = ref[...]
        row += ref.shape[0]


def split_sums(value):
    high = value.astype(LOW).astype(F32)
    return jnp.concatenate([high, value - high], axis=0).astype(LOW)


def joined_sums(value):
    wide_value = value.astype(F32)
    return wide_value[:8] + wide_value[8:]


def join_body(n, *refs):
    half_far, half_near, *parts = refs[:-5]
    weights, proj, vectors, other, held = refs[-5:]
    core = lax.axis_index("tp") % 2
    size = half_far.shape[1]
    other[:, pl.ds(pl.multiple_of(core * size, 128), size)] = half_far[...]
    other[:, pl.ds(pl.multiple_of((1 - core) * size, 128), size)] = half_near[...]
    assemble(parts, held)
    part = weights.shape[0] // n
    for g in range(n):
        weights[g * part : (g + 1) * part, :] = held[g, :part, :]
    vectors[...] = wide([held[g, part : part + 16, :part].astype(F32) for g in range(n)])[:8]
    cols = weights.shape[1] // 4
    half = weights.shape[0] // 2
    proj[...] = wide([weights[:half, 3 * cols :], weights[half:, 3 * cols :]])


def attend_body(
    counts, act, other, weights, vectors, biases, mixed_out, turned_out, scale_out,
    normed_own, normed_other, q_out, k_out, v_out, e_out,
):
    slots = act.shape[0]
    hw = biases.shape[1]
    bias = biases[...].astype(F32)
    for src, dst in ((act, normed_own), (other, normed_other)):
        scaled, _ = norm_stats(src[...].astype(F32))
        dst[...] = (scaled * vectors[0:1] + vectors[2:3]).astype(LOW)
    queries = (dot(normed_own[...], weights[:, :hw]) + bias[0:1]).astype(LOW)
    q_out[...] = (queries.astype(F32) * (1.0 / math.sqrt(HD))).astype(LOW)
    for i, src in enumerate((normed_own, normed_other)):
        both = dot(src[...], weights[:, hw : 3 * hw])
        k_out[i] = both[:, :hw].astype(LOW)
        v_out[i] = (both[:, hw:] + bias[1:2]).astype(LOW)
    ids = lax.broadcasted_iota(jnp.int32, (slots, 1), 0)
    outs, scales = [], []
    for h in range(hw // HD):
        cols = slice(h * HD, (h + 1) * HD)
        query = q_out[:, cols]
        scores = [
            jnp.where(ids < count, dot(k_out[i][:, cols], query, 1, 1), NEG)
            for i, count in enumerate(own_other(counts))
        ]
        peak = jnp.maximum(*[jnp.max(s, axis=0, keepdims=True) for s in scores])
        mixed, total = 0.0, 0.0
        for i in range(2):
            e = jnp.exp(scores[i] - peak)
            total = total + jnp.sum(e, axis=0, keepdims=True)
            e_out[h, i] = e.astype(LOW)
            mixed = mixed + dot(v_out[i][:, cols], e_out[h, i], 0, 0)
        scales.append(1.0 / total)
        outs.append(mixed * scales[-1])
    turned = jnp.concatenate(outs, axis=0)
    turned_out[...] = turned
    mixed_out[...] = fold_rows(turned.T).astype(LOW)
    scales.append(jnp.zeros((8 - len(scales), slots), F32))
    scale_out[...] = jnp.concatenate(scales, axis=0).T


def unpair(mixed, mixed_far, proj, proj_far, paired):
    rows, more = mixed.shape[0], proj.shape[0]
    cuts = [0, rows, 2 * rows, 2 * rows + more, 2 * (rows + more)]
    near, cross, proj_near, proj_cross = [paired[a:b, :] for a, b in zip(cuts, cuts[1:])]
    return (
        (mixed[...], near, mixed_far[...], cross),
        (proj[...], proj_near, proj_far[...], proj_cross),
    )


def hidden_body(n, *refs):
    (counts, act, *rest) = refs
    mixed, mixed_far, packed, packed_far, paired, vectors, hidden_bias, cot, *rest = rest
    mixes, projs = unpair(mixed, mixed_far, packed, packed_far, paired)
    ups, rest = rest[: n + 1], rest[n + 1 :]
    two_out, gelu_out, slope_out, branch_out, middle_out, up_out, proj, held = rest
    slots = act.shape[0]
    width = act.shape[1]
    own, _ = own_other(counts)
    valid = lax.broadcasted_iota(jnp.int32, (slots, 1), 0) < own
    branch_out[...] = jnp.where(valid, cot[...].astype(F32), 0.0).astype(LOW)
    top, bottom = 0.0, 0.0
    for j, (mixed, packed) in enumerate(zip(mixes, projs)):
        cols = packed.shape[1] // 2
        half = packed.shape[0]
        proj[j, :half, :] = packed[:, :cols]
        proj[j, half:, :] = packed[:, cols:]
        top = top + dot(mixed[:, :cols], proj[j], 1, 1)
        bottom = bottom + dot(mixed[:, cols:], proj[j], 1, 1)
    rows = slots - top.shape[0]
    middle = jnp.concatenate([top, bottom[:rows]], axis=0) + act[...].astype(F32) + vectors[4:5]
    middle_out[...] = middle
    scaled, _ = norm_stats(middle)
    two = (scaled * vectors[1:2] + vectors[3:4]).astype(LOW)
    two_out[...] = two
    assemble(ups, held)
    up = held[...].reshape(width, -1)
    up_out[...] = up
    hidden = dot(two, up) + hidden_bias[...].astype(F32)
    share = 0.5 * (1.0 + lax.erf(hidden * math.sqrt(0.5)))
    gelu_out[...] = (hidden * share).astype(LOW)
    bell = jnp.exp(hidden * hidden * -0.5) * (1.0 / math.sqrt(2.0 * math.pi))
    slope_out[...] = share + hidden * bell


def block(ref, owner, rows):
    return ref[pl.ds(pl.multiple_of(owner * rows, 8), rows), :]


def down_grads_body(n, branch, gelu, total, up_half, down_half):
    rows = total.shape[0] // n
    half = up_half.shape[0]
    total[...] = dot(branch[...], gelu[...], 0, 0)
    far = (lax.axis_index("shard") + n // 2) % n
    up_half[...] = block(total, 2 * far, half).astype(LOW)
    down_half[...] = block(total, 2 * far + 1, half).astype(LOW)


def both_ways_body(n, left, total, got_up, got_down, up_out, down_out):
    shard = lax.axis_index("shard")
    rows = total.shape[0] // n
    for owner, got, out, last in (
        ((shard + left) % n, got_up, up_out, 0),
        ((shard + n - left) % n, got_down, down_out, 1),
    ):
        value = block(total, owner, rows)
        half = got.shape[0]
        if half == rows:
            out[...] = (value + got[...].astype(F32)).astype(LOW)
        else:
            both = [value[:half], value[half:]]
            both[last] = both[last] + got[...].astype(F32)
            out[...] = jnp.concatenate(both, axis=0).astype(LOW)


def both_ways_end_body(n, total, got_up, got_down, own, low):
    rows = own.shape[0]
    value = block(total, lax.axis_index("shard"), rows)
    value = value + got_up[...].astype(F32) + got_down[...].astype(F32)
    own[...] = value
    low[...] = value.astype(LOW)


def give(n, value, sent):
    shard, ctx = lax.axis_index("shard"), lax.axis_index("ctx")
    rows = value.shape[0] // n
    half = rows // 2
    theirs = jnp.where(ctx == 0, n - 1, 1)
    far = n // 2
    for k in range(1, far):
        owner = (shard + theirs * k) % n
        sent[(k - 1) * rows : k * rows, :] = block(value, owner, rows).astype(LOW)
    at = (far - 1) * rows
    for i, owner in enumerate(((shard + far) % n, shard)):
        piece = block(value, 2 * owner + (1 - ctx), half)
        sent[at + i * half : at + (i + 1) * half, :] = piece.astype(LOW)


def ring_first_body(n, value, got, out):
    shard, ctx = lax.axis_index("shard"), lax.axis_index("ctx")
    rows = value.shape[0] // n
    half = rows // 2
    at = (n // 2 - 1) * rows
    far = (shard + n // 2) % n
    piece = block(value, 2 * far + ctx, half) + got[at : at + half, :].astype(F32)
    out[...] = piece.astype(LOW)


def add_half(value, piece):
    ctx = lax.axis_index("ctx")
    zeros = jnp.zeros_like(piece)
    low = jnp.where(ctx == 0, piece, zeros)
    high = jnp.where(ctx == 0, zeros, piece)
    return value + jnp.concatenate([low, high], axis=0)


def ring_step_body(n, left, sums_too, value, got, came, *refs):
    shard, ctx = lax.axis_index("shard"), lax.axis_index("ctx")
    rows = value.shape[0] // n
    out = refs[-1]
    owner = (shard + jnp.where(ctx == 0, left, n - left)) % n
    first = left == n // 2 - 1
    piece = came[: rows // 2 if first else rows, :].astype(F32)
    total = block(value, owner, rows) + got[(left - 1) * rows : left * rows, :].astype(F32)
    total = add_half(total, piece) if first else total + piece
    out[:rows, :] = total.astype(LOW)
    if sums_too:
        more = joined_sums(came[piece.shape[0] :, :])
        if first:
            more = jnp.where(ctx == 0, more, 0.0)
        out[rows:, :] = split_sums(refs[0][...] + more)


def ring_end_body(n, sums_too, value, got, came, *refs):
    shard, ctx = lax.axis_index("shard"), lax.axis_index("ctx")
    rows = value.shape[0] // n
    half = rows // 2
    at = (n // 2 - 1) * rows + half
    piece = block(value, 2 * shard + ctx, half) + got[at : at + half, :].astype(F32)
    total = add_half(came[:rows, :].astype(F32), piece)
    if sums_too:
        both, own, low, sums = refs
        value_sums = jnp.where(ctx == 0, both[...], 0.0) + joined_sums(came[rows:, :])
        sums[...] = value_sums
        low[rows:, :] = split_sums(value_sums)
    else:
        own, low = refs
    own[...] = total
    low[:rows, :] = total.astype(LOW)


def middle_back_body(n, *refs):
    branch, slope, up, middle, vectors, proj, mixed, mixed_far, paired, *rest = refs
    downs, rest = rest[: n + 1], rest[n + 1 :]
    near, keep, proj_keep, hidden_out, low_out, down_out, sums, held = rest
    width = up.shape[0]
    assemble(downs, held)
    down = held[...].reshape(width, -1)
    down_out[...] = down
    branch_low = branch[...]
    grad_hidden = (dot(branch_low, down) * slope[...]).astype(LOW)
    hidden_out[...] = grad_hidden
    grad_two = dot(grad_hidden, up[...], 1, 1)
    scaled, rate = norm_stats(middle[...])
    back = norm_back(grad_two, scaled, rate, vectors[1:2])
    low = back.astype(LOW)
    low_out[...] = low
    rows = keep.shape[1]
    keep[0] = fold_rows(dot(low, proj[0]) + dot(branch_low, proj[0]))
    keep[1] = fold_rows(dot(low, proj[2]))
    near[:rows, :] = fold_rows(dot(low, proj[1])).astype(LOW)
    near[rows : 2 * rows, :] = fold_rows(dot(low, proj[3])).astype(LOW)
    first_tp = jnp.where(lax.axis_index("tp") == 0, 1.0, 0.0)
    attn = (back + first_tp * branch_low.astype(F32)).astype(LOW)
    blocks = (mixed[...], paired[:rows, :], mixed_far[...], paired[rows : 2 * rows, :])
    grads = [
        dot(attn, unfold_rows(block.astype(F32), attn.shape[0]).astype(LOW), 0, 0)
        for block in blocks
    ]
    near[2 * rows :, :] = wide([grads[1], grads[3]]).astype(LOW)
    proj_keep[...] = wide([grads[0], grads[2]])
    branch_sum = jnp.sum(branch_low.astype(F32), axis=0, keepdims=True) * first_tp
    sums[...] = jnp.concatenate(
        [
            jnp.sum(grad_two * scaled, axis=0, keepdims=True),
            jnp.sum(grad_two, axis=0, keepdims=True),
            branch_sum + jnp.sum(back, axis=0, keepdims=True),
            branch_sum,
            jnp.sum(grad_hidden.astype(F32), axis=0, keepdims=True),
            jnp.zeros((3, sums.shape[1]), F32),
        ],
        axis=0,
    )


def up_grads_body(n, two, hidden, sent, kept):
    kept[...] = dot(two[...], hidden[...], 0, 0)
    give(n, kept, sent)


def ffn_rows_body(gelu, branch, low, middle, down, near, keep, own_middle, own_branch, chunks):
    rows = own_middle.shape[0]
    chunks[:, rows - 2 :, :] = jnp.zeros_like(chunks[:, rows - 2 :, :])
    to_chunks(dot(gelu[...], down[...], 1, 1), chunks)
    near[0] = chunks[1].astype(LOW)
    near[1] = chunks[3].astype(LOW)
    keep[0] = chunks[0]
    keep[2] = chunks[2]
    to_chunks(low[...].astype(F32), chunks)
    near[2] = chunks[1].astype(LOW)
    near[3] = chunks[3].astype(LOW)
    keep[1] = chunks[0]
    keep[3] = chunks[2]
    to_chunks(middle[...], chunks)
    own_middle[...] = chunks[0, :rows, :]
    to_chunks(branch[...].astype(F32), chunks)
    own_branch[...] = chunks[0, :rows, :]


def rows_body(counts, rows_own, far, own_middle, own_branch, vectors, layer_out, middle_grad):
    own, _ = own_other(counts)
    rows = layer_out.shape[0]
    ids = lax.broadcasted_iota(jnp.int32, (rows, 1), 0) + lax.axis_index("tp") * rows
    mlp = rows_own[0] + far[0].astype(F32)
    value = own_middle[...] + mlp[:rows] + vectors[5:6]
    layer_out[...] = jnp.where(ids < own, value, 0.0).astype(LOW)
    back = rows_own[1] + far[1].astype(F32)
    middle_grad[...] = own_branch[...] + back[:rows]


def attend_back_body(
    back, far, q, k, v, e, scales, turned, weights, act, other, sums_in,
    row_near, own_out, other_out, near, keep, own_act, sums, chunks,
):
    slots, hw = q.shape
    grad_mixed = back[...] + far[...].astype(F32)
    grad_mixed = unfold_rows(grad_mixed, slots).astype(LOW).astype(F32)
    scaled_grads = [
        grad_mixed[:, h * HD : (h + 1) * HD] * scales[:, h : h + 1] for h in range(hw // HD)
    ]
    scaled_grad = wide(scaled_grads)
    inner = scaled_grad.T * turned[...]
    scaled_low = scaled_grad.astype(LOW)
    scale = 1.0 / math.sqrt(HD)
    gq, gk, gv = [], ([], []), ([], [])
    for h in range(hw // HD):
        cols = slice(h * HD, (h + 1) * HD)
        grad = scaled_low[:, cols]
        row = jnp.sum(inner[cols], axis=0, keepdims=True)
        gq_head = 0.0
        for i in range(2):
            gv[i].append(dot(e[h, i], grad))
            probs_grad = dot(v[i][:, cols], grad, 1, 1)
            scores_grad = (e[h, i].astype(F32) * (probs_grad - row)).astype(LOW)
            gk[i].append(dot(scores_grad, q[:, cols]))
            gq_head = gq_head + dot(k[i][:, cols], scores_grad, 0, 0)
        gq.append(gq_head * scale)
    gq = jnp.concatenate(gq, axis=0).T
    own_out[...] = wide([gq, *gk[0], *gv[0]]).astype(LOW)
    other_out[...] = wide([*gk[1], *gv[1]]).astype(LOW)
    rows = own_act.shape[0]
    chunks[:, rows - 2 :, :] = jnp.zeros_like(chunks[:, rows - 2 :, :])
    near[4:] = row_near[...]
    gain_sum, shift_sum = 0.0, 0.0
    for i, src in enumerate((act, other)):
        if i == 0:
            grad = dot(own_out[...], weights[:, : 3 * hw], 1, 1)
        else:
            grad = dot(other_out[...], weights[:, hw : 3 * hw], 1, 1)
        scaled, _ = norm_stats(src[...].astype(F32))
        gain_sum = gain_sum + jnp.sum(grad * scaled, axis=0, keepdims=True)
        shift_sum = shift_sum + jnp.sum(grad, axis=0, keepdims=True)
        to_chunks(grad, chunks)
        near[2 * i] = chunks[1].astype(LOW)
        near[2 * i + 1] = chunks[3].astype(LOW)
        keep[2 * i] = chunks[0]
        keep[2 * i + 1] = chunks[2]
    to_chunks(act[...].astype(F32), chunks)
    own_act[...] = chunks[0, :rows, :]
    ones = jnp.ones((8, slots), LOW)
    own_sums = dot(ones, own_out[...])[0:1]
    other_sums = dot(ones, other_out[...])[0:1]
    head_v = own_sums[:, 2 * hw :] + other_sums[:, hw:]
    pad = jnp.zeros((1, sums.shape[1] - 2 * hw), F32)
    sums[...] = jnp.concatenate(
        [
            gain_sum,
            sums_in[0:1],
            shift_sum,
            sums_in[1:2],
            sums_in[2:3],
            sums_in[3:4],
            sums_in[4:5],
            wide([own_sums[:, :hw], head_v, pad]),
        ],
        axis=0,
    )


def head_grads_body(
    n, own, other, normed_own, normed_other, proj_own, proj_far, sent, early, kept
):
    hw = own.shape[1] // 3
    far = jnp.concatenate([proj_far[:, :hw], proj_far[:, hw:]], axis=0)
    from_own = dot(normed_own[...], own[...], 0, 0)
    from_other = dot(normed_other[...], other[...], 0, 0)
    k_grad = from_own[:, hw : 2 * hw] + from_other[:, :hw]
    v_grad = from_own[:, 2 * hw :] + from_other[:, hw:]
    kept[...] = wide([from_own[:, :hw], k_grad, v_grad, proj_own[...] + far.astype(F32)])
    give(n, kept, sent)
    early[...] = sent[:, : early.shape[1]]


def head_late_body(sent, sums, late):
    rows, half = sent.shape[0], late.shape[1]
    late[:rows, :] = sent[:, half:]
    packed = split_sums(sums[...])
    late[rows : rows + 16, :] = packed[:, :half]
    late[rows + 16 :, :] = packed[:, half:]


def head_first_body(n, value, early, late, sums, got, both, out):
    rows = early.shape[0]
    got[...] = wide([early[...], late[:rows, :]])
    both[...] = sums[...] + joined_sums(wide([late[rows : rows + 16, :], late[rows + 16 :, :]]))
    half = value.shape[0] // n // 2
    ring_first_body(n, value, got, out.at[:half, :])
    out[half:, :] = split_sums(both[...])


def swap_end_body(mine, other, grad):
    grad[...] = mine[...] + other[...].astype(F32)


def tp_sums_body(own, near, out):
    shared = lax.broadcasted_iota(jnp.int32, own.shape, 0) < 6
    out[...] = own[...] + jnp.where(shared, near[...], 0.0)


def finish_body(n, mine, other, sums, qkv_grad, proj_grad, gains, biases, heads, hidden):
    shard = lax.axis_index("shard")
    rows = mine.shape[0]
    total = mine[...] + other[:rows, :].astype(F32)
    hw = proj_grad.shape[0]
    for i in range(3):
        qkv_grad[i] = total[:, i * hw : (i + 1) * hw]
    proj_grad[...] = total[:, 3 * hw :].T
    shared = sums[...] + joined_sums(other[rows:, :])
    part = gains.shape[1]
    own = 0.0
    for g in range(n):
        own = own + jnp.where(shard == g, shared[:, g * part : (g + 1) * part], 0.0)
    gains[...] = own[0:2]
    biases[...] = own[2:6]
    hidden[...] = shared[6]
    heads[...] = jnp.concatenate([shared[7:8, :hw], shared[7:8, hw : 2 * hw]], axis=0)


def halfway_body(keep, row_keep, near, own, far, rows_own, rows_far):
    own[0] = keep[0] + near[0].astype(F32)
    own[1] = keep[2] + near[2].astype(F32)
    far[0] = (keep[1] + near[1].astype(F32)).astype(LOW)
    far[1] = (keep[3] + near[3].astype(F32)).astype(LOW)
    rows_own[0] = row_keep[0] + near[4].astype(F32)
    rows_own[1] = row_keep[1] + near[6].astype(F32)
    rows_far[0] = (row_keep[2] + near[5].astype(F32)).astype(LOW)
    rows_far[1] = (row_keep[3] + near[7].astype(F32)).astype(LOW)


def input_cross_body(own, far, kept, out):
    kept[...] = own[0] + far[0].astype(F32)
    out[...] = (own[1] + far[1].astype(F32)).astype(LOW)


def input_body(kept, cross, own_act, middle_grad, vectors, out):
    rows = out.shape[0]
    grad = kept[...] + cross[...].astype(F32)
    scaled, rate = norm_stats(own_act[...])
    back = norm_back(grad[:rows], scaled, rate, vectors[0:1])
    out[...] = (middle_grad[...] + back).astype(LOW)


def per_device(
    activations,
    slot_counts,
    qkv_weight,
    proj_weight,
    up_weight,
    down_weight,
    norm_gains,
    row_biases,
    head_biases,
    hidden_bias,
    cotangent,
):
    images, slots, width = activations.shape
    n = lax.axis_size("shard")
    n_ctx = lax.axis_size("ctx")
    n_tp = lax.axis_size("tp")
    assert images == 1 and n_ctx == 2 and n_tp == 4 and n % 2 == 0
    part = width // n
    hw = qkv_weight.shape[2]
    ff = up_weight.shape[1]
    quarter = slots // n_tp
    padded = (quarter + 7) // 8 * 8
    fold = folded_rows(slots)
    heads = hw // HD

    now = None

    def place(x):
        nonlocal now
        if now is not None:
            x, now = lax.optimization_barrier((x, now))
        return x

    def wait(*arrays):
        nonlocal now
        now, *arrays = lax.optimization_barrier((now, *arrays))
        return arrays[0] if len(arrays) == 1 else arrays

    def run(body, name, out, args, scalars=0, scratch=(), room=24, weight=0):
        nonlocal now
        outs = call(body, name, out, args, scalars, scratch, room, now, weight)
        now = outs[-1]
        return outs if len(outs) > 1 else outs[0]

    def move(x, axes, moves):
        return lax.ppermute(place(x), axes, moves)

    def over_ctx(x):
        return move(x, "ctx", [(i, i ^ 1) for i in range(n_ctx)])

    def over_tp(x, bit):
        return move(x, "tp", [(i, i ^ bit) for i in range(n_tp)])

    def ring(x):
        moves = [
            (i * n_ctx + r, ((i + (1 if r == 0 else n - 1)) % n) * n_ctx + r)
            for i in range(n)
            for r in range(n_ctx)
        ]
        return move(x, ("shard", "ctx"), moves)

    def step(x, k):
        return move(x, "shard", [(i, (i + k) % n) for i in range(n)])

    def with_n(body, *more):
        return functools.partial(body, n, *more)

    far = n // 2

    def first_hops(block):
        parts, x = [block], ring(block)
        for _ in range(far - 2):
            x = wait(x)
            parts += [x, over_ctx(x)]
            x = ring(x)
        return parts, x

    def half_of(x, weight=0):
        size = (x.shape[0] // 2, x.shape[1])
        return run(half_body, "half", [shape(size)], [x], weight=weight)

    def mark(x, weight):
        run(mark_body, "mark", [shape((8, 128), F32)], [x], weight=weight)

    def ring_step(weight, left, kept, got, came, *sums):
        cols = kept.shape[1]
        extra = 16 * len(sums)
        return run(
            with_n(ring_step_body, left, extra),
            "ring_step",
            [shape((part + extra, cols))],
            [kept, got, came, *sums],
            weight=weight,
        )

    act = activations[0]
    down_turned = down_weight.T
    rows = -(-(part + 6) // 32) * 32
    pack, pack_half, act_half = run(
        pack_body,
        "pack",
        [shape((rows, width)), shape((rows // 2, width)), shape((slots, width // 2))],
        [qkv_weight, norm_gains, row_biases, proj_weight, act],
        room=58,
    )
    pack_parts, last = first_hops(pack)
    piece = step(pack_half, far)
    act_far = over_ctx(act_half)
    last = wait(last)
    mark(last, 0)
    pack_parts += [last, over_ctx(last)]
    up_parts, up_last = first_hops(up_weight)
    act_far = wait(act_far)
    act_near = over_tp(act_far, 1)
    piece = wait(piece)
    mark(piece, 20)
    pack_parts += [piece, over_ctx(piece)]
    pack_parts[-3] = wait(pack_parts[-3])
    up_last = wait(up_last)
    up_piece = half_of(up_last)
    up_piece = ring(up_piece)
    up_parts += [up_last, over_ctx(up_last)]
    weights, proj, vectors, other = run(
        with_n(join_body),
        "join",
        [
            shape((width, width)),
            shape((width // 2, 2 * hw)),
            shape((8, width), F32),
            shape((slots, width)),
        ],
        [act_far, act_near, *pack_parts],
        scratch=[pltpu.VMEM((n, rows, width), LOW)],
        weight=20,
    )
    proj_far = over_tp(proj, 2)
    down_parts, down_last = first_hops(down_turned)
    (mixed, turned, scales, normed_own, normed_other, q, k, v, e) = run(
        attend_body,
        "attend",
        [
            shape((fold, 2 * hw)),
            shape((hw, slots), F32),
            shape((slots, 8), F32),
            shape((slots, width)),
            shape((slots, width)),
            shape((slots, hw)),
            shape((2, slots, hw)),
            shape((2, slots, hw)),
            shape((heads, 2, slots, slots)),
        ],
        [slot_counts, act, other, weights, vectors, head_biases],
        scalars=1,
    )
    mixed_far = over_tp(mixed, 2)
    up_piece = wait(up_piece)
    up_parts += [up_piece, over_ctx(up_piece)]
    up_parts[-3] = wait(up_parts[-3])
    mark(up_parts[-3], 3)
    proj_far = wait(proj_far)
    down_last = wait(down_last)
    mixed_far = wait(mixed_far)
    paired = run(
        pair_body,
        "pair",
        [shape((2 * fold + width, 2 * hw))],
        [mixed, mixed_far, proj, proj_far],
    )
    paired = over_tp(paired, 1)
    up_parts[-1] = wait(up_parts[-1])
    down_piece = half_of(down_last, 10)
    down_piece = ring(down_piece)
    down_parts += [down_last, over_ctx(down_last)]
    two, gelu, slope, branch, middle, up, proj_full = run(
        with_n(hidden_body),
        "hidden",
        [
            shape((slots, width)),
            shape((slots, ff)),
            shape((slots, ff), F32),
            shape((slots, width)),
            shape((slots, width), F32),
            shape((width, ff)),
            shape((n_tp, width, hw)),
        ],
        [slot_counts, act, mixed, mixed_far, proj, proj_far, paired, vectors]
        + [hidden_bias.reshape(1, ff), cotangent[0]]
        + up_parts,
        scalars=1,
        scratch=[pltpu.VMEM((n, part, ff), LOW)],
    )
    down_piece = wait(down_piece)
    down_parts += [down_piece, over_ctx(down_piece)]
    down_total, to_up, to_down = run(
        with_n(down_grads_body),
        "down_grads",
        [shape((width, ff), F32)] + [shape((part // 2, ff))] * 2,
        [branch, gelu],
    )
    to_up, to_down = step(to_up, 1), step(to_down, n - 1)
    near, keep, proj_keep, hidden, back_low, down, sums = run(
        with_n(middle_back_body),
        "middle_back",
        [
            shape((2 * fold + width, 2 * hw)),
            shape((2, fold, 2 * hw), F32),
            shape((width, 2 * hw), F32),
            shape((slots, ff)),
            shape((slots, width)),
            shape((width, ff)),
            shape((8, width), F32),
        ],
        [branch, slope, up, middle, vectors, proj_full, mixed, mixed_far, paired] + down_parts,
        scratch=[pltpu.VMEM((n, part, ff), LOW)],
    )
    near = over_tp(near, 1)
    up_sent, up_kept = run(
        with_n(up_grads_body),
        "up_grads",
        [shape((far * part, ff)), shape((width, ff), F32)],
        [two, hidden],
    )
    for left in range(far - 1, 0, -1):
        to_up, to_down = wait(to_up, to_down)
        to_up, to_down = run(
            with_n(both_ways_body, left),
            "both_ways",
            [shape((part, ff))] * 2,
            [down_total, to_up, to_down],
            weight=20,
        )
        if left > 1:
            to_up, to_down = step(to_up, 1), step(to_down, n - 1)
    near = wait(near)
    back, proj_own, back_far, proj_far = run(
        add_body,
        "back_add",
        [
            shape((fold, 2 * hw), F32),
            shape((width, hw), F32),
            shape((fold, 2 * hw)),
            shape((width // 2, 2 * hw)),
        ],
        [keep, proj_keep, near],
    )
    back_far = over_tp(back_far, 2)
    proj_far = over_tp(proj_far, 2)
    to_up, to_down = step(to_up, 1), step(to_down, n - 1)
    up_got = over_ctx(up_sent)
    row_near, row_keep, own_middle, own_branch = run(
        ffn_rows_body,
        "ffn_rows",
        [
            shape((4, padded, width)),
            shape((4, padded, width), F32),
            shape((quarter, width), F32),
            shape((quarter, width), F32),
        ],
        [gelu, branch, back_low, middle, down],
        scratch=[pltpu.VMEM((n_tp, padded, width), F32)],
    )
    back_far = wait(back_far)
    mark(back_far, 60)
    own_grads, other_grads, near, keep, own_act, sums = run(
        attend_back_body,
        "attend_back",
        [
            shape((slots, 3 * hw)),
            shape((slots, 2 * hw)),
            shape((8, padded, width)),
            shape((4, padded, width), F32),
            shape((quarter, width), F32),
            shape((8, width), F32),
        ],
        [back, back_far, q, k, v, e, scales, turned, weights, act, other, sums, row_near],
        scratch=[pltpu.VMEM((n_tp, padded, width), F32)],
    )
    to_up, to_down = wait(to_up, to_down)
    down_mine, down_low = run(
        with_n(both_ways_end_body),
        "both_ways_end",
        [shape((part, ff), F32), shape((part, ff))],
        [down_total, to_up, to_down],
    )
    proj_far = wait(proj_far)
    head_sent, head_early, head_kept = run(
        with_n(head_grads_body),
        "head_grads",
        [shape((far * part, width)), shape((far * part, width // 2)), shape((width, width), F32)],
        [own_grads, other_grads, normed_own, normed_other, proj_own, proj_far],
    )
    head_early = over_ctx(head_early)
    sums_near = over_tp(sums, 1)
    near = over_tp(near, 1)
    sums_near = wait(sums_near)
    sums = run(tp_sums_body, "tp_sums", [shape((8, width), F32)], [sums, sums_near])
    sums_far = over_tp(sums, 2)
    up_got = wait(up_got)
    up_came = run(
        with_n(ring_first_body),
        "ring_first",
        [shape((part // 2, ff))],
        [up_kept, up_got],
        weight=30,
    )
    up_came = ring(up_came)
    sums_far = wait(sums_far)
    sums = run(tp_sums_body, "tp_sums", [shape((8, width), F32)], [sums, sums_far])
    head_late = run(
        head_late_body,
        "head_late",
        [shape((far * part + 32, width // 2))],
        [head_sent, sums],
    )
    head_late = over_ctx(head_late)
    down_other = over_ctx(down_low)
    near = wait(near)
    input_own, input_far, rows_own, rows_far = run(
        halfway_body,
        "halfway",
        [shape((2, padded, width), F32), shape((2, padded, width))] * 2,
        [keep, row_keep, near],
    )
    input_far = over_tp(input_far, 2)
    head_early = wait(head_early)
    for left in range(far - 1, 0, -1):
        up_came = wait(up_came)
        up_came = ring(ring_step(20, left, up_kept, up_got, up_came))
    head_late = wait(head_late)
    head_got, sums, head_came = run(
        with_n(head_first_body),
        "head_first",
        [shape((far * part, width)), shape((8, width), F32), shape((part // 2 + 16, width))],
        [head_kept, head_early, head_late, sums],
    )
    head_came = ring(head_came)
    rows_far = over_tp(rows_far, 2)
    input_far = wait(input_far)
    input_kept, input_cross = run(
        input_cross_body,
        "input_cross",
        [shape((padded, width), F32), shape((padded, width))],
        [input_own, input_far],
    )
    input_cross = over_ctx(input_cross)
    up_came = wait(up_came)
    up_mine, up_low = run(
        with_n(ring_end_body, 0),
        "up_end",
        [shape((part, ff), F32), shape((part, ff))],
        [up_kept, up_got, up_came],
    )
    up_other = over_ctx(up_low)
    down_other = wait(down_other)
    down_grad = run(
        swap_end_body, "swap_end", [shape((part, ff), F32)], [down_mine, down_other], weight=40
    )
    for left in range(far - 1, 0, -1):
        head_came = wait(head_came)
        head_came = ring(ring_step(0, left, head_kept, head_got, head_came, sums))
    head_came = wait(head_came)
    head_mine, head_low, sums = run(
        with_n(ring_end_body, 1),
        "ring_end",
        [shape((part, width), F32), shape((part + 16, width)), shape((8, width), F32)],
        [head_kept, head_got, head_came, sums],
    )
    head_other = over_ctx(head_low)
    input_cross = wait(input_cross)
    mark(input_cross, 40)
    rows_far = wait(rows_far)
    layer_out, middle_grad = run(
        rows_body,
        "rows",
        [shape((quarter, width)), shape((quarter, width), F32)],
        [slot_counts, rows_own, rows_far, own_middle, own_branch, vectors],
        scalars=1,
    )
    input_grad = run(
        input_body,
        "input",
        [shape((quarter, width))],
        [input_kept, input_cross, own_act, middle_grad, vectors],
    )
    up_other = wait(up_other)
    up_grad = run(swap_end_body, "swap_end", [shape((part, ff), F32)], [up_mine, up_other])
    qkv_grad, proj_grad, gains_grad, biases_grad, heads_grad, hidden_grad = run(
        with_n(finish_body),
        "finish",
        [
            shape((3, part, hw), F32),
            shape((hw, part), F32),
            shape((2, part), F32),
            shape((4, part), F32),
            shape((2, hw), F32),
            shape((ff,), F32),
        ],
        [head_mine, head_other, sums],
    )
    return (
        layer_out[None],
        input_grad[None],
        qkv_grad,
        proj_grad,
        up_grad,
        down_grad.T,
        gains_grad,
        biases_grad,
        heads_grad,
        hidden_grad,
    )


def solution(mesh):
    placed = (
        P("shard", "ctx", None),
        P("shard", None),
        P(None, "shard", "tp"),
        P("tp", "shard"),
        P("shard", "tp"),
        P("tp", "shard"),
        P(None, "shard"),
        P(None, "shard"),
        P(None, "tp"),
        P("tp"),
        P("shard", "ctx", None),
    )
    return jax.shard_map(
        per_device,
        mesh=mesh,
        in_specs=placed,
        out_specs=(
            P("shard", ("ctx", "tp"), None),
            P("shard", ("ctx", "tp"), None),
            P(None, "shard", "tp"),
            P("tp", "shard"),
            P("shard", "tp"),
            P("tp", "shard"),
            P(None, "shard"),
            P(None, "shard"),
            P(None, "tp"),
            P("tp"),
        ),
        check_vma=False,
    )
```

time: 167 us -> 144 us (0.86)
  waiting for transfers between devices: 78.1 us -> 55.4 us
  local copies, waits for them, and re-layouts: 1.35 us -> 4.13 us
  starting transfers between devices: 47.1 us -> 44.6 us
    ppermute x43 -> x40, waiting for transfers between devices: 78.1 us -> 55.4 us  [move(): return lax.ppermute(place(x), axes, moves)]
    unnamed x16 -> x30, local copies, waits for them, and re-layouts: 0.04 us -> 4.12 us
    ppermute x43 -> x40, starting transfers between devices: 47.1 us -> 44.6 us  [move(): return lax.ppermute(place(x), axes, moves)]
    pallas_call x23 -> x37, Pallas kernels: 38.2 us -> 38.6 us  [call(): pl.pallas_call(kernel, name=name, out_shape=out, in_specs=specs, out_spec...]
  transfers between devices with their start and end apart: 43 -> 40, of which waited for: 17 -> 22; matrix products, arithmetic and copies ran while one was open for 1% -> 0% of each run, Pallas kernels for 19% -> 24%
where the time goes in v5:
time: 144 us
  waiting for transfers between devices  55.4 us (38%)
  starting transfers between devices  44.6 us (31%)
  Pallas kernels  38.6 us (27%)
  local copies, waits for them, and re-layouts  4.13 us (3%)
    ppermute x40, waiting for transfers between devices, move(): return lax.ppermute(place(x), axes, moves)  55.4 us
    ppermute x40, starting transfers between devices, move(): return lax.ppermute(place(x), axes, moves)  44.6 us
    pallas_call x37, Pallas kernels, call(): pl.pallas_call(kernel, name=name, out_shape=out, in_specs=specs, out_spec...  38.6 us
    unnamed x30, local copies, waits for them, and re-layouts  4.12 us
  transfers between devices with their start and end apart: 40, of which 22 were waited for; matrix products, arithmetic and copies ran while one was open for 0% of the time, Pallas kernels for 24%

profile of v5, /device:TPU:0, one launch (start us, length us, event | category | flops | bytes accessed | tf_op | source)
XLA Modules:
  0.0 143.7 jit_solution(17527221429579292826)
XLA Ops:
  0.7 2.5 %pack.1 = (bf16[224,768]{1,0:T(8,128)(2,1)}, bf16[112,768]{1,0:T(8,128)(2,1)}, bf16[520,384]{1,0:T(8,128)(2,1)}) custom-call(bf16[3,192,192]{2,1,0:T(8,128)(2,1)} %refs_0_.4, bf16[2,192]{1,0:T(2,128)(2,1)} %refs_1_.1, bf16[4,192]{1,0:T(4,128)(2,1)} %refs_2_.1, bf16[192,192]{1,0:T(8,128)(2,1)} %refs_3_.1, bf16[520,768]{1,0:T(8,128)(2,1)} %bitcast.6), custom_call_target="tpu_custom_call" | custom-call | flops 1 | bytes 1 | tf_op jit(solution)/shard_map/pack/pallas_call | solution.py:34
  3.1 2.9 %collective-permute-start.1 = (bf16[520,384]{1,0:T(8,128)(2,1)}, bf16[520,384]{1,0:T(8,128)(2,1)S(1)}, u32[]{:S(2)}, u32[]{:S(2)}) collective-permute-start(bf16[520,384]{1,0:T(8,128)(2,1)} %get-tuple-element.245.refs_1_), channel_id=1, source_target_pairs={{0,4},{4,0},{1,5},{5,1},{2,6},{6,2},{3,7},{7,3},{8,12},{12,8},{9,1... | collective-permute-start | bytes 1198088 | tf_op jit(solution)/shard_map/ppermute | solution.py:659
  7.6 2.6 %collective-permute-start.3 = (bf16[112,768]{1,0:T(8,128)(2,1)}, bf16[112,768]{1,0:T(8,128)(2,1)S(1)}, u32[]{:S(2)}, u32[]{:S(2)}) collective-permute-start(bf16[112,768]{1,0:T(8,128)(2,1)} %get-tuple-element.250), channel_id=1, source_target_pairs={{0,16},{8,24},{16,0},{24,8},{1,17},{9,25},{17,1},{25,9},{2,18},{10... | collective-permute-start | bytes 516104 | tf_op jit(solution)/shard_map/ppermute | solution.py:659
  10.2 8.9 %collective-permute-done.refs_0_.refs_3_ = bf16[224,768]{1,0:T(8,128)(2,1)S(1)} collective-permute-done((bf16[224,768]{1,0:T(8,128)(2,1)}, bf16[224,768]{1,0:T(8,128)(2,1)S(1)}, u32[]{:S(2)}, u32[]{:S(2)}) %collective-permute-start) | collective-permute-done | bytes 344096 | tf_op jit(solution)/shard_map/ppermute | solution.py:659
  20.2 2.4 %collective-permute-start.6 = (bf16[192,768]{1,0:T(8,128)(2,1)S(1)}, bf16[192,768]{1,0:T(8,128)(2,1)S(1)}, u32[]{:S(2)}, u32[]{:S(2)}) collective-permute-start(bf16[192,768]{1,0:T(8,128)(2,1)S(1)} %copy-done.9), channel_id=1, source_target_pairs={{0,8},{4,28},{8,16},{12,4},{16,24},{20,12},{24,0},{28,20},{1,9},{5... | collective-permute-start | bytes 884744 | tf_op jit(solution)/shard_map/ppermute | solution.py:659
  24.3 7.1 %collective-permute-done.3.refs_0_.refs_5_ = bf16[112,768]{1,0:T(8,128)(2,1)S(1)} collective-permute-done((bf16[112,768]{1,0:T(8,128)(2,1)}, bf16[112,768]{1,0:T(8,128)(2,1)S(1)}, u32[]{:S(2)}, u32[]{:S(2)}) %collective-permute-start.3) | collective-permute-done | bytes 172064 | tf_op jit(solution)/shard_map/ppermute | solution.py:659
  32.5 2.4 %collective-permute-start.8 = (bf16[192,768]{1,0:T(8,128)(2,1)S(1)}, bf16[192,768]{1,0:T(8,128)(2,1)S(1)}, u32[]{:S(2)}, u32[]{:S(2)}) collective-permute-start(bf16[192,768]{1,0:T(8,128)(2,1)S(1)} %collective-permute-done.6.refs_0_.refs_11_), channel_id=1, source_target_pairs={{0,4},{4,0},{1,5},{5,1},{2,6},{6,2},{3,7},{7,3},{8,12},{12,8},{9,1... | collective-permute-start | bytes 884744 | tf_op jit(solution)/shard_map/ppermute | solution.py:659
  34.9 3.7 %collective-permute-done.5.refs_6_ = bf16[112,768]{1,0:T(8,128)(2,1)S(1)} collective-permute-done((bf16[112,768]{1,0:T(8,128)(2,1)S(1)}, bf16[112,768]{1,0:T(8,128)(2,1)S(1)}, u32[]{:S(2)}, u32[]{:S(2)}) %collective-permute-start.5) | collective-permute-done | bytes 172064 | tf_op jit(solution)/shard_map/ppermute | solution.py:659
  40.5 6.9 %attend.1 = (bf16[264,384]{1,0:T(8,128)(2,1)S(1)}, f32[192,520]{1,0:T(8,128)S(1)}, f32[520,8]{1,0:T(8,128)S(1)}, bf16[520,768]{1,0:T(8,128)(2,1)S(1)}, bf16[520,...) custom-call(s32[1,2]{1,0:T(1,128)S(1)} %copy-done.10, ...), custom_call_target="tpu_custom_call" | custom-call | flops 1 | bytes 1 | tf_op jit(solution)/shard_map/attend/pallas_call | solution.py:34
  47.9 3.3 %collective-permute-start.13 = (bf16[96,768]{1,0:T(8,128)(2,1)S(1)}, bf16[96,768]{1,0:T(8,128)(2,1)S(1)}, u32[]{:S(2)}, u32[]{:S(2)}) collective-permute-start(bf16[96,768]{1,0:T(8,128)(2,1)S(1)} %collective-permute-done.7.refs_13_), channel_id=1, source_target_pairs={{0,4},{4,0},{1,5},{5,1},{2,6},{6,2},{3,7},{7,3},{8,12},{12,8},{9,1... | collective-permute-start | bytes 442376 | tf_op jit(solution)/shard_map/ppermute | solution.py:659
  51.3 2.1 %collective-permute-done.11.refs_1_.refs_3_.refs_7_ = bf16[264,384]{1,0:T(8,128)(2,1)S(1)} collective-permute-done((bf16[264,384]{1,0:T(8,128)(2,1)S(1)}, bf16[264,384]{1,0:T(8,128)(2,1)S(1)}, u32[]{:S(2)}, u32[]{:S(2)}) %collective-permute-start.11) | collective-permute-done | bytes 202784 | tf_op jit(solution)/shard_map/ppermute | solution.py:659
  54.6 2.6 %collective-permute-start.14 = (bf16[192,768]{1,0:T(8,128)(2,1)S(1)}, bf16[192,768]{1,0:T(8,128)(2,1)S(1)}, u32[]{:S(2)}, u32[]{:S(2)}) collective-permute-start(bf16[192,768]{1,0:T(8,128)(2,1)S(1)} %collective-permute-done.10.refs_0_.refs_10_), channel_id=1, source_target_pairs={{0,4},{4,0},{1,5},{5,1},{2,6},{6,2},{3,7},{7,3},{8,12},{12,8},{9,1... | collective-permute-start | bytes 884744 | tf_op jit(solution)/shard_map/ppermute | solution.py:659
  57.3 3.6 %hidden.1 = (bf16[520,768]{1,0:T(8,128)(2,1)S(1)}, bf16[520,768]{1,0:T(8,128)(2,1)S(1)}, f32[520,768]{1,0:T(8,128)S(1)}, bf16[520,768]{1,0:T(8,128)(2,1)S(1)}, f...) custom-call(s32[1,2]{1,0:T(1,128)S(1)} %copy-done.10, ...), custom_call_target="tpu_custom_call" | custom-call | flops 1 | bytes 1 | tf_op jit(solution)/shard_map/hidden/pallas_call | solution.py:34
  64.3 2.1 %collective-permute-start.18 = (bf16[96,768]{1,0:T(8,128)(2,1)S(1)}, bf16[96,768]{1,0:T(8,128)(2,1)S(1)}, u32[]{:S(2)}, u32[]{:S(2)}) collective-permute-start(bf16[96,768]{1,0:T(8,128)(2,1)S(1)} %get-tuple-element.321.refs_14_), channel_id=1, source_target_pairs={{0,24},{8,0},{16,8},{24,16},{1,25},{9,1},{17,9},{25,17},{2,26},{10... | collective-permute-start | bytes 442376 | tf_op jit(solution)/shard_map/ppermute | solution.py:659
  68.2 4.9 %middle_back.1 = (bf16[1296,384]{1,0:T(8,128)(2,1)S(1)}, f32[2,264,384]{2,1,0:T(8,128)S(1)}, f32[768,384]{1,0:T(8,128)S(1)}, bf16[520,768]{1,0:T(8,128)(2,1)S(1)...) custom-call(bf16[520,768]{1,0:T(8,128)(2,1)S(1)} %get-tuple-element.295.refs_0_.refs_1_, ...), custom_call_target="tpu_custom_call" | custom-call | flops 1 | bytes 1 | tf_op jit(solution)/shard_map/middle_back/pallas_call | solution.py:34
  77.6 2.6 %collective-permute-start.22 = (bf16[192,768]{1,0:T(8,128)(2,1)S(1)}, bf16[192,768]{1,0:T(8,128)(2,1)S(1)}, u32[]{:S(2)}, u32[]{:S(2)}) collective-permute-start(bf16[192,768]{1,0:T(8,128)(2,1)S(1)} %get-tuple-element.355.refs_3_), channel_id=1, source_target_pairs={{0,24},{8,0},{16,8},{24,16},{1,25},{9,1},{17,9},{25,17},{2,26},{10... | collective-permute-start | bytes 884744 | tf_op jit(solution)/shard_map/ppermute | solution.py:659
  83.8 7.9 %attend_back.1 = (bf16[520,576]{1,0:T(8,128)(2,1)S(1)}, bf16[520,384]{1,0:T(8,128)(2,1)S(1)}, bf16[8,136,768]{2,1,0:T(8,128)(2,1)S(1)}, f32[4,136,768]{2,1,0:T(8...) custom-call(f32[264,384]{1,0:T(8,128)S(1)} %get-tuple-element.329.refs_0_, ...), custom_call_target="tpu_custom_call" | custom-call | flops 1 | bytes 1 | tf_op jit(solution)/shard_map/attend_back/pallas_call | solution.py:34
  91.8 2.1 %collective-permute-done.21.refs_1_ = bf16[192,768]{1,0:T(8,128)(2,1)S(1)} collective-permute-done((bf16[192,768]{1,0:T(8,128)(2,1)S(1)}, bf16[192,768]{1,0:T(8,128)(2,1)S(1)}, u32[]{:S(2)}, u32[]{:S(2)}) %collective-permute-start.21) | collective-permute-done | bytes 294944 | tf_op jit(solution)/shard_map/ppermute | solution.py:659
  99.1 3.3 %collective-permute-done.26.refs_1_ = f32[8,768]{1,0:T(8,128)S(1)} collective-permute-done((f32[8,768]{1,0:T(8,128)S(1)}, f32[8,768]{1,0:T(8,128)S(1)}, u32[]{:S(2)}, u32[]{:S(2)}) %collective-permute-start.26) | collective-permute-done | bytes 24608 | tf_op jit(solution)/shard_map/ppermute | solution.py:659
  109.7 3.4 %collective-permute-done.30.refs_2_ = bf16[416,384]{1,0:T(8,128)(2,1)S(1)} collective-permute-done((bf16[416,384]{1,0:T(8,128)(2,1)S(1)}, bf16[416,384]{1,0:T(8,128)(2,1)S(1)}, u32[]{:S(2)}, u32[]{:S(2)}) %collective-permute-start.30) | collective-permute-done | bytes 319520 | tf_op jit(solution)/shard_map/ppermute | solution.py:659
  114.2 2.4 %collective-permute-done.31.refs_1_ = bf16[2,136,768]{2,1,0:T(8,128)(2,1)S(1)} collective-permute-done((bf16[2,136,768]{2,1,0:T(8,128)(2,1)S(1)}, bf16[2,136,768]{2,1,0:T(8,128)(2,1)S(1)}, u32[]{:S(2)}, u32[]{:S(2)}) %collective-permute-start.31) | collective-permute-done | bytes 417824 | tf_op jit(solution)/shard_map/ppermute | solution.py:659
  122.0 2.2 %collective-permute-start.36 = (bf16[136,768]{1,0:T(8,128)(2,1)S(1)}, bf16[136,768]{1,0:T(8,128)(2,1)S(1)}, u32[]{:S(2)}, u32[]{:S(2)}) collective-permute-start(bf16[136,768]{1,0:T(8,128)(2,1)S(1)} %get-tuple-element.435.refs_3_), channel_id=1, source_target_pairs={{0,4},{4,0},{1,5},{5,1},{2,6},{6,2},{3,7},{7,3},{8,12},{12,8},{9,1... | collective-permute-start | bytes 626696 | tf_op jit(solution)/shard_map/ppermute | solution.py:659
  125.1 6.1 %collective-permute-done.35.refs_2_ = bf16[208,768]{1,0:T(8,128)(2,1)S(1)} collective-permute-done((bf16[208,768]{1,0:T(8,128)(2,1)S(1)}, bf16[208,768]{1,0:T(8,128)(2,1)S(1)}, u32[]{:S(2)}, u32[]{:S(2)}) %collective-permute-start.35) | collective-permute-done | bytes 319520 | tf_op jit(solution)/shard_map/ppermute | solution.py:659
  138.5 3.2 %collective-permute-done.38.refs_1_ = bf16[208,768]{1,0:T(8,128)(2,1)S(1)} collective-permute-done((bf16[208,768]{1,0:T(8,128)(2,1)S(1)}, bf16[208,768]{1,0:T(8,128)(2,1)S(1)}, u32[]{:S(2)}, u32[]{:S(2)}) %collective-permute-start.38) | collective-permute-done | bytes 319520 | tf_op jit(solution)/shard_map/ppermute | solution.py:659
  (124 shorter events, 51.4 us)
Async XLA Ops:
  3.1 21.1 %collective-permute-start.1 = (bf16[520,384]{1,0:T(8,128)(2,1)}, bf16[520,384]{1,0:T(8,128)(2,1)S(1)}, u32[]{:S(2)}, u32[]{:S(2)}) collective-permute-start(bf16[520,384]{1,0:T(8,128)(2,1)} %get-tuple-element.245.refs_1_), channel_id=1, source_target_pairs={{0,4},{4,0},{1,5},{5,1},{2,6},{6,2},{3,7},{7,3},{8,12},{12,8},{9,1... | collective-permute-start | bytes 1198088 | tf_op jit(solution)/shard_map/ppermute | solution.py:659
  6.1 13.1 %collective-permute-start = (bf16[224,768]{1,0:T(8,128)(2,1)}, bf16[224,768]{1,0:T(8,128)(2,1)S(1)}, u32[]{:S(2)}, u32[]{:S(2)}) collective-permute-start(bf16[224,768]{1,0:T(8,128)(2,1)} %get-tuple-element.240.refs_2_), channel_id=1, source_target_pairs={{0,8},{4,28},{8,16},{12,4},{16,24},{20,12},{24,0},{28,20},{1,9},{5... | collective-permute-start | bytes 1032200 | tf_op jit(solution)/shard_map/ppermute | solution.py:659
  7.6 23.7 %collective-permute-start.3 = (bf16[112,768]{1,0:T(8,128)(2,1)}, bf16[112,768]{1,0:T(8,128)(2,1)S(1)}, u32[]{:S(2)}, u32[]{:S(2)}) collective-permute-start(bf16[112,768]{1,0:T(8,128)(2,1)} %get-tuple-element.250), channel_id=1, source_target_pairs={{0,16},{8,24},{16,0},{24,8},{1,17},{9,25},{17,1},{25,9},{2,18},{10... | collective-permute-start | bytes 516104 | tf_op jit(solution)/shard_map/ppermute | solution.py:659
  20.2 11.2 %collective-permute-start.6 = (bf16[192,768]{1,0:T(8,128)(2,1)S(1)}, bf16[192,768]{1,0:T(8,128)(2,1)S(1)}, u32[]{:S(2)}, u32[]{:S(2)}) collective-permute-start(bf16[192,768]{1,0:T(8,128)(2,1)S(1)} %copy-done.9), channel_id=1, source_target_pairs={{0,8},{4,28},{8,16},{12,4},{16,24},{20,12},{24,0},{28,20},{1,9},{5... | collective-permute-start | bytes 884744 | tf_op jit(solution)/shard_map/ppermute | solution.py:659
  31.5 16.5 %collective-permute-start.7 = (bf16[96,768]{1,0:T(8,128)(2,1)S(1)}, bf16[96,768]{1,0:T(8,128)(2,1)S(1)}, u32[]{:S(2)}, u32[]{:S(2)}) collective-permute-start(bf16[96,768]{1,0:T(8,128)(2,1)S(1)} %half.2.refs_7_), channel_id=1, source_target_pairs={{0,8},{4,28},{8,16},{12,4},{16,24},{20,12},{24,0},{28,20},{1,9},{5... | collective-permute-start | bytes 442376 | tf_op jit(solution)/shard_map/ppermute | solution.py:659
  32.5 18.8 %collective-permute-start.8 = (bf16[192,768]{1,0:T(8,128)(2,1)S(1)}, bf16[192,768]{1,0:T(8,128)(2,1)S(1)}, u32[]{:S(2)}, u32[]{:S(2)}) collective-permute-start(bf16[192,768]{1,0:T(8,128)(2,1)S(1)} %collective-permute-done.6.refs_0_.refs_11_), channel_id=1, source_target_pairs={{0,4},{4,0},{1,5},{5,1},{2,6},{6,2},{3,7},{7,3},{8,12},{12,8},{9,1... | collective-permute-start | bytes 884744 | tf_op jit(solution)/shard_map/ppermute | solution.py:659
  38.9 12.4 %collective-permute-start.9 = (bf16[384,384]{1,0:T(8,128)(2,1)S(1)}, bf16[384,384]{1,0:T(8,128)(2,1)S(1)}, u32[]{:S(2)}, u32[]{:S(2)}) collective-permute-start(bf16[384,384]{1,0:T(8,128)(2,1)S(1)} %get-tuple-element.279.refs_2_.refs_4_), channel_id=1, source_target_pairs={{0,2},{1,3},{2,0},{3,1},{4,6},{5,7},{6,4},{7,5},{8,10},{9,11},{10,... | collective-permute-start | bytes 884744 | tf_op jit(solution)/shard_map/ppermute | solution.py:659
  40.4 10.8 %collective-permute-start.10 = (bf16[192,768]{1,0:T(8,128)(2,1)S(1)}, bf16[192,768]{1,0:T(8,128)(2,1)S(1)}, u32[]{:S(2)}, u32[]{:S(2)}) collective-permute-start(bf16[192,768]{1,0:T(8,128)(2,1)S(1)} %bitcast.13), channel_id=1, source_target_pairs={{0,8},{4,28},{8,16},{12,4},{16,24},{20,12},{24,0},{28,20},{1,9},{5... | collective-permute-start | bytes 884744 | tf_op jit(solution)/shard_map/ppermute | solution.py:659
  54.6 11.9 %collective-permute-start.14 = (bf16[192,768]{1,0:T(8,128)(2,1)S(1)}, bf16[192,768]{1,0:T(8,128)(2,1)S(1)}, u32[]{:S(2)}, u32[]{:S(2)}) collective-permute-start(bf16[192,768]{1,0:T(8,128)(2,1)S(1)} %collective-permute-done.10.refs_0_.refs_10_), channel_id=1, source_target_pairs={{0,4},{4,0},{1,5},{5,1},{2,6},{6,2},{3,7},{7,3},{8,12},{12,8},{9,1... | collective-permute-start | bytes 884744 | tf_op jit(solution)/shard_map/ppermute | solution.py:659
  64.3 10.0 %collective-permute-start.18 = (bf16[96,768]{1,0:T(8,128)(2,1)S(1)}, bf16[96,768]{1,0:T(8,128)(2,1)S(1)}, u32[]{:S(2)}, u32[]{:S(2)}) collective-permute-start(bf16[96,768]{1,0:T(8,128)(2,1)S(1)} %get-tuple-element.321.refs_14_), channel_id=1, source_target_pairs={{0,24},{8,0},{16,8},{24,16},{1,25},{9,1},{17,9},{25,17},{2,26},{10... | collective-permute-start | bytes 442376 | tf_op jit(solution)/shard_map/ppermute | solution.py:659
  77.6 14.2 %collective-permute-start.22 = (bf16[192,768]{1,0:T(8,128)(2,1)S(1)}, bf16[192,768]{1,0:T(8,128)(2,1)S(1)}, u32[]{:S(2)}, u32[]{:S(2)}) collective-permute-start(bf16[192,768]{1,0:T(8,128)(2,1)S(1)} %get-tuple-element.355.refs_3_), channel_id=1, source_target_pairs={{0,24},{8,0},{16,8},{24,16},{1,25},{9,1},{17,9},{25,17},{2,26},{10... | collective-permute-start | bytes 884744 | tf_op jit(solution)/shard_map/ppermute | solution.py:659
  80.1 13.8 %collective-permute-start.21 = (bf16[192,768]{1,0:T(8,128)(2,1)S(1)}, bf16[192,768]{1,0:T(8,128)(2,1)S(1)}, u32[]{:S(2)}, u32[]{:S(2)}) collective-permute-start(bf16[192,768]{1,0:T(8,128)(2,1)S(1)} %get-tuple-element.354), channel_id=1, source_target_pairs={{0,8},{8,16},{16,24},{24,0},{1,9},{9,17},{17,25},{25,1},{2,10},{10... | collective-permute-start | bytes 884744 | tf_op jit(solution)/shard_map/ppermute | solution.py:659
  80.1 13.9 %collective-permute-start.23 = (bf16[384,384]{1,0:T(8,128)(2,1)S(1)}, bf16[384,384]{1,0:T(8,128)(2,1)S(1)}, u32[]{:S(2)}, u32[]{:S(2)}) collective-permute-start(bf16[384,384]{1,0:T(8,128)(2,1)S(1)} %get-tuple-element.365.refs_5_), channel_id=1, source_target_pairs={{0,2},{1,3},{2,0},{3,1},{4,6},{5,7},{6,4},{7,5},{8,10},{9,11},{10,... | collective-permute-start | bytes 884744 | tf_op jit(solution)/shard_map/ppermute | solution.py:659
  80.7 16.5 %collective-permute-start.25 = (bf16[384,768]{1,0:T(8,128)(2,1)S(1)}, bf16[384,768]{1,0:T(8,128)(2,1)S(1)}, u32[]{:S(2)}, u32[]{:S(2)}) collective-permute-start(bf16[384,768]{1,0:T(8,128)(2,1)S(1)} %get-tuple-element.379), channel_id=1, source_target_pairs={{0,4},{4,0},{1,5},{5,1},{2,6},{6,2},{3,7},{7,3},{8,12},{12,8},{9,1... | collective-permute-start | bytes 1769480 | tf_op jit(solution)/shard_map/ppermute | solution.py:659
  96.0 9.9 %collective-permute-start.28 = (bf16[384,384]{1,0:T(8,128)(2,1)S(1)}, bf16[384,384]{1,0:T(8,128)(2,1)S(1)}, u32[]{:S(2)}, u32[]{:S(2)}) collective-permute-start(bf16[384,384]{1,0:T(8,128)(2,1)S(1)} %get-tuple-element.395), channel_id=1, source_target_pairs={{0,4},{4,0},{1,5},{5,1},{2,6},{6,2},{3,7},{7,3},{8,12},{12,8},{9,1... | collective-permute-start | bytes 884744 | tf_op jit(solution)/shard_map/ppermute | solution.py:659
  102.5 10.5 %collective-permute-start.30 = (bf16[416,384]{1,0:T(8,128)(2,1)S(1)}, bf16[416,384]{1,0:T(8,128)(2,1)S(1)}, u32[]{:S(2)}, u32[]{:S(2)}) collective-permute-start(bf16[416,384]{1,0:T(8,128)(2,1)S(1)} %head_late.1.refs_3_), channel_id=1, source_target_pairs={{0,4},{4,0},{1,5},{5,1},{2,6},{6,2},{3,7},{7,3},{8,12},{12,8},{9,1... | collective-permute-start | bytes 958472 | tf_op jit(solution)/shard_map/ppermute | solution.py:659
  105.8 10.8 %collective-permute-start.31 = (bf16[2,136,768]{2,1,0:T(8,128)(2,1)S(1)}, bf16[2,136,768]{2,1,0:T(8,128)(2,1)S(1)}, u32[]{:S(2)}, u32[]{:S(2)}) collective-permute-start(bf16[2,136,768]{2,1,0:T(8,128)(2,1)S(1)} %get-tuple-element.411), channel_id=1, source_target_pairs={{0,2},{1,3},{2,0},{3,1},{4,6},{5,7},{6,4},{7,5},{8,10},{9,11},{10,... | collective-permute-start | bytes 1253384 | tf_op jit(solution)/shard_map/ppermute | solution.py:659
  106.8 10.0 %collective-permute-start.32 = (bf16[192,768]{1,0:T(8,128)(2,1)S(1)}, bf16[192,768]{1,0:T(8,128)(2,1)S(1)}, u32[]{:S(2)}, u32[]{:S(2)}) collective-permute-start(bf16[192,768]{1,0:T(8,128)(2,1)S(1)} %ring_step.2.refs_4_), channel_id=1, source_target_pairs={{0,8},{4,28},{8,16},{12,4},{16,24},{20,12},{24,0},{28,20},{1,9},{5... | collective-permute-start | bytes 884744 | tf_op jit(solution)/shard_map/ppermute | solution.py:659
  107.9 10.7 %collective-permute-start.33 = (bf16[192,768]{1,0:T(8,128)(2,1)S(1)}, bf16[192,768]{1,0:T(8,128)(2,1)S(1)}, u32[]{:S(2)}, u32[]{:S(2)}) collective-permute-start(bf16[192,768]{1,0:T(8,128)(2,1)S(1)} %get-tuple-element.421.refs_6_), channel_id=1, source_target_pairs={{0,4},{4,0},{1,5},{5,1},{2,6},{6,2},{3,7},{7,3},{8,12},{12,8},{9,1... | collective-permute-start | bytes 884744 | tf_op jit(solution)/shard_map/ppermute | solution.py:659
  121.6 9.6 %collective-permute-start.35 = (bf16[208,768]{1,0:T(8,128)(2,1)S(1)}, bf16[208,768]{1,0:T(8,128)(2,1)S(1)}, u32[]{:S(2)}, u32[]{:S(2)}) collective-permute-start(bf16[208,768]{1,0:T(8,128)(2,1)S(1)} %ring_step.3.refs_4_), channel_id=1, source_target_pairs={{0,8},{4,28},{8,16},{12,4},{16,24},{20,12},{24,0},{28,20},{1,9},{5... | collective-permute-start | bytes 958472 | tf_op jit(solution)/shard_map/ppermute | solution.py:659
  122.0 9.3 %collective-permute-start.36 = (bf16[136,768]{1,0:T(8,128)(2,1)S(1)}, bf16[136,768]{1,0:T(8,128)(2,1)S(1)}, u32[]{:S(2)}, u32[]{:S(2)}) collective-permute-start(bf16[136,768]{1,0:T(8,128)(2,1)S(1)} %get-tuple-element.435.refs_3_), channel_id=1, source_target_pairs={{0,4},{4,0},{1,5},{5,1},{2,6},{6,2},{3,7},{7,3},{8,12},{12,8},{9,1... | collective-permute-start | bytes 626696 | tf_op jit(solution)/shard_map/ppermute | solution.py:659
  124.3 9.0 %collective-permute-start.37 = (bf16[2,136,768]{2,1,0:T(8,128)(2,1)S(1)}, bf16[2,136,768]{2,1,0:T(8,128)(2,1)S(1)}, u32[]{:S(2)}, u32[]{:S(2)}) collective-permute-start(bf16[2,136,768]{2,1,0:T(8,128)(2,1)S(1)} %get-tuple-element.438.refs_3_), channel_id=1, source_target_pairs={{0,2},{1,3},{2,0},{3,1},{4,6},{5,7},{6,4},{7,5},{8,10},{9,11},{10,... | collective-permute-start | bytes 1253384 | tf_op jit(solution)/shard_map/ppermute | solution.py:659
  125.1 11.5 %collective-permute-start.39 = (bf16[192,768]{1,0:T(8,128)(2,1)S(1)}, bf16[192,768]{1,0:T(8,128)(2,1)S(1)}, u32[]{:S(2)}, u32[]{:S(2)}) collective-permute-start(bf16[192,768]{1,0:T(8,128)(2,1)S(1)} %get-tuple-element.449.refs_2_), channel_id=1, source_target_pairs={{0,4},{4,0},{1,5},{5,1},{2,6},{6,2},{3,7},{7,3},{8,12},{12,8},{9,1... | collective-permute-start | bytes 884744 | tf_op jit(solution)/shard_map/ppermute | solution.py:659
  131.4 10.3 %collective-permute-start.38 = (bf16[208,768]{1,0:T(8,128)(2,1)S(1)}, bf16[208,768]{1,0:T(8,128)(2,1)S(1)}, u32[]{:S(2)}, u32[]{:S(2)}) collective-permute-start(bf16[208,768]{1,0:T(8,128)(2,1)S(1)} %get-tuple-element.447), channel_id=1, source_target_pairs={{0,4},{4,0},{1,5},{5,1},{2,6},{6,2},{3,7},{7,3},{8,12},{12,8},{9,1... | collective-permute-start | bytes 958472 | tf_op jit(solution)/shard_map/ppermute | solution.py:659
  (31 other events, 217.9 us)
